TPU v7x, 768 devices: a whole 4x8x12 slice. The times are simulated.
768 devices in a mesh: tile: 96 (over y_lo, z, core), scan: 8 (over x, y_hi).
Axes of the slice: x: 4, y: 8 (y_hi: 2, y_lo: 4; y = y_hi * 4 + y_lo), z: 12, core: 2. Of those that a mesh axis runs over, the one named last changes fastest.
Arguments:
- consensus: float32 [96, 2, 256, 256], P('tile'), may hold values from -4 to 4
- duals: float32 [8, 96, 2, 256, 256], P('scan', 'tile'), may hold values from -3 to 3
- probes: float32 [8, 2, 256, 256], P('scan'), may hold values from -4 to 4
- amplitudes: bfloat16 [8, 96, 4, 256, 256], P('scan', 'tile'), may hold values from 0.19921875 to 2
- offsets: int32 [8, 96, 4, 2], P('scan', 'tile'), may hold values from 0 to 128
- counts: int32 [8, 96], P('scan', 'tile'), may hold values from 1 to 4, as said below
Outputs:
- consensus_new: float32 [96, 2, 256, 256], P('tile')
- duals_new: float32 [8, 96, 2, 256, 256], P('scan', 'tile')
- probes_new: float32 [8, 2, 256, 256], P('scan')
Inputs may be any that keep to these rules, and one draw needn't show every extreme that they name: counts: some group has 4 scan positions in some tile; slots at or past the count are unused. offsets: first the row, then the column.
All inputs are finite; a program needn't handle non-finite values.
Results may differ from a plain program's by a relative error of at most 0.015.
Values may be sent and summed in bfloat16 or wider, within the bound.
A program may use at most 32 MiB of HBM per device.

v0:
```python
import math

import jax
import jax.numpy as jnp
from jax import lax
from jax.sharding import PartitionSpec as P

PS = 256
TS = 256
OVER = 128
TGW = 4
INNER = 2


penalty = 0.5
smoothing = 0.05
probe_step = 3.0


def passed_along(value, axis, by):
    length = lax.axis_size(axis)
    pairs = [(i, i + by) for i in range(length) if 0 <= i + by < length]
    return lax.ppermute(value, axis, pairs)


def dft_tables(length):
    indices = jnp.arange(length, dtype=jnp.int32)
    phase_index = indices[:, None] * indices[None, :] % length
    angles = phase_index.astype(jnp.float32) * (2.0 * math.pi / length)
    norm_scale = 1.0 / math.sqrt(length)
    real_part = (jnp.cos(angles) * norm_scale).astype(jnp.bfloat16)
    imag_part = (-jnp.sin(angles) * norm_scale).astype(jnp.bfloat16)
    return (real_part, imag_part)


def forward_wave(wave_real, wave_imag, stacked, spread, length):
    section_one = jnp.dot(
        stacked, jnp.concatenate([wave_real, wave_imag], 1), preferred_element_type=jnp.float32
    )
    inner_real = (section_one[:length, :length] - section_one[length:, length:]).astype(
        jnp.bfloat16
    )
    inner_imag = (section_one[:length, length:] + section_one[length:, :length]).astype(
        jnp.bfloat16
    )
    section_two = jnp.dot(
        jnp.concatenate([inner_real, inner_imag], 0), spread, preferred_element_type=jnp.float32
    )
    return (
        section_two[:length, :length] - section_two[length:, length:],
        section_two[:length, length:] + section_two[length:, :length],
    )


def inverse_wave(wave_real, wave_imag, stacked, spread, length):
    section_one = jnp.dot(
        stacked, jnp.concatenate([wave_real, wave_imag], 1), preferred_element_type=jnp.float32
    )
    inner_real = (section_one[:length, :length] + section_one[length:, length:]).astype(
        jnp.bfloat16
    )
    inner_imag = (section_one[:length, length:] - section_one[length:, :length]).astype(
        jnp.bfloat16
    )
    section_two = jnp.dot(
        jnp.concatenate([inner_real, inner_imag], 0), spread, preferred_element_type=jnp.float32
    )
    return (
        section_two[:length, :length] + section_two[length:, length:],
        section_two[length:, :length] - section_two[:length, length:],
    )


def patch_terms(window, probe_field, measured, stacked, spread):
    length = window.shape[1]
    object_real = window[0].astype(jnp.float32)
    object_imag = window[1].astype(jnp.float32)
    probe_real = probe_field[0]
    probe_imag = probe_field[1]
    exit_real = (probe_real * object_real - probe_imag * object_imag).astype(jnp.bfloat16)
    exit_imag = (probe_real * object_imag + probe_imag * object_real).astype(jnp.bfloat16)
    wave_real, wave_imag = forward_wave(exit_real, exit_imag, stacked, spread, length)
    modulus = jnp.sqrt(wave_real * wave_real + wave_imag * wave_imag + smoothing)
    factor = measured.astype(jnp.float32) / modulus - 1.0
    resid_real = (wave_real * factor).astype(jnp.bfloat16)
    resid_imag = (wave_imag * factor).astype(jnp.bfloat16)
    back_real, back_imag = inverse_wave(resid_real, resid_imag, stacked, spread, length)
    object_terms = jnp.stack(
        [
            probe_real * back_real + probe_imag * back_imag,
            probe_real * back_imag - probe_imag * back_real,
            probe_real * probe_real + probe_imag * probe_imag,
        ]
    )
    probe_terms = jnp.stack(
        [
            object_real * back_real + object_imag * back_imag,
            object_real * back_imag - object_imag * back_real,
            object_real * object_real + object_imag * object_imag,
        ]
    )
    return (object_terms, probe_terms)


def pull_rim(window, distance):
    return passed_along(window, "tile", distance)


def push_rim(window, distance):
    return passed_along(window.astype(jnp.bfloat16), "tile", distance).astype(window.dtype)


def project_modulus(average):
    magnitude = jnp.sqrt(average[0] * average[0] + average[1] * average[1])
    return average / jnp.maximum(magnitude, 1.0)[None]


def shards(consensus, duals, probes, amplitudes, offsets, counts):
    real_part, imag_part = dft_tables(PS)
    stacked = jnp.concatenate([real_part, imag_part], 0)
    spread = jnp.concatenate([real_part, imag_part], 1)
    column = lax.axis_index("tile") % TGW
    grid_consensus = consensus[0]
    dual_tile = duals[0, 0]
    probe_field = probes[0]
    measured = amplitudes[0, 0]
    corners = offsets[0, 0]
    slot_count = counts[0, 0]
    zero_index = jnp.zeros((), jnp.int32)
    span = TS + OVER
    estimate = grid_consensus
    probe_sum = jnp.zeros((3, PS, PS), jnp.float32)
    for sweep_index in range(INNER):
        rounded = estimate.astype(jnp.bfloat16)
        from_right = pull_rim(rounded[:, :, :OVER], -1)
        from_right = jnp.where(column == TGW - 1, jnp.zeros_like(from_right), from_right)
        widened = jnp.concatenate([rounded, from_right], 2)
        from_below = pull_rim(widened[:, :OVER, :], -TGW)
        extended = jnp.concatenate([widened, from_below], 1)

        def visit_slot(slot_index, inner_state):
            local_totals, local_probe = inner_state
            top_row = corners[slot_index, 0]
            left_col = corners[slot_index, 1]
            window = lax.dynamic_slice(extended, (zero_index, top_row, left_col), (2, PS, PS))
            object_terms, probe_terms = patch_terms(
                window, probe_field, measured[slot_index], stacked, spread
            )
            region = lax.dynamic_slice(local_totals, (zero_index, top_row, left_col), (3, PS, PS))
            local_totals = lax.dynamic_update_slice(
                local_totals, region + object_terms, (zero_index, top_row, left_col)
            )
            return (local_totals, local_probe + probe_terms)

        start_totals = jnp.zeros((3, span, span), jnp.float32)
        local_totals, probe_sum = lax.fori_loop(
            0, slot_count, visit_slot, (start_totals, probe_sum)
        )
        from_above = push_rim(local_totals[:, TS:, :], TGW)
        central = jnp.concatenate(
            [local_totals[:, :OVER, :] + from_above, local_totals[:, OVER:TS, :]], 1
        )
        from_left = push_rim(central[:, :, TS:], 1)
        from_left = jnp.where(column == 0, jnp.zeros_like(from_left), from_left)
        returned = jnp.concatenate([central[:, :, :OVER] + from_left, central[:, :, OVER:TS]], 2)
        estimate = estimate + (
            returned[0:2] + penalty * (grid_consensus - dual_tile - estimate)
        ) / (returned[2] + penalty)
    combined = estimate + dual_tile
    summed = lax.psum(combined.astype(jnp.bfloat16), "scan").astype(jnp.float32)
    settled = project_modulus(summed / lax.axis_size("scan"))
    probe_totals = lax.psum(probe_sum, "tile")
    probe_new = probe_field + probe_step * probe_totals[0:2] / jnp.sqrt(probe_totals[2] + 1.0)
    dual_new = dual_tile + estimate - settled
    return (settled[None], dual_new[None, None], probe_new[None])


def solution(mesh):
    placed = (
        P("tile", None, None, None),
        P("scan", "tile", None, None, None),
        P("scan", None, None, None),
        P("scan", "tile", None, None, None),
        P("scan", "tile", None, None),
        P("scan", "tile"),
    )
    return jax.shard_map(
        shards,
        mesh=mesh,
        in_specs=placed,
        out_specs=(
            P("tile", None, None, None),
            P("scan", "tile", None, None, None),
            P("scan", None, None, None),
        ),
        check_vma=False,
    )
```

profile of v0, /device:TPU:1, one launch (start us, length us, event | category | flops | bytes accessed | tf_op | source)
XLA Modules:
  0.0 1181.2 jit_solution(8311645982011932480)
XLA Ops:
  8.4 12.6 %collective-permute-start = (bf16[2,256,128]{2,1,0:T(8,128)(2,1)S(1)}, bf16[2,256,128]{2,1,0:T(8,128)(2,1)S(1)}, u32[]{:S(2)}, u32[]{:S(2)}) collective-permute-start(bf16[2,256,128]{2,1,0:T(8,128)(2,1)S(1)} %slice.386), channel_id=1, source_target_pairs={{8,0},{16,8},{24,16},{32,24},{40,32},{48,40},{56,48},{64,56},{72,6... | collective-permute-start | bytes 393224 | tf_op jit(solution)/shard_map/ppermute | solution.py:23
  24.6 10.1 collective-permute-done.1
  36.1 19.5 %while.28 = (s32[]{:T(128)}, f32[3,384,384]{2,1,0:T(8,128)}, f32[3,256,256]{2,1,0:T(8,128)S(1)}, s32[]{:T(128)}, s32[4,2]{0,1:T(2,128)S(1)}, /*index=5*/f32[2,25...) while((s32[]{:T(128)}, f32[3,384,384]{2,1,0:T(8,128)}, ...), condition=%wide.region_1.2_spmd, body=%wide.region_0.1_spmd.sunk | while | flops 543686656 | bytes 22413668 | solution.py:156
  44.5 1.8 maximum_add_fusion.6
  46.3 8.6 dynamic_update_slice.14
  56.7 2.2 collective-permute-start.2
  58.9 3.7 collective-permute-done.2
  64.7 50.3 %collective-permute-start.3 = (bf16[3,256,128]{2,1,0:T(8,128)(2,1)}, bf16[3,256,128]{2,1,0:T(8,128)(2,1)S(1)}, u32[]{:S(2)}, u32[]{:S(2)}) collective-permute-start(bf16[3,256,128]{2,1,0:T(8,128)(2,1)} %fusion.104), channel_id=1, source_target_pairs={{0,8},{8,16},{16,24},{24,32},{32,40},{40,48},{48,56},{56,64},{64,7... | collective-permute-start | bytes 589832 | tf_op jit(solution)/shard_map/ppermute | solution.py:23
  115.0 10.8 collective-permute-done.3
  128.0 2.0 collective-permute-start.4
  130.1 4.2 collective-permute-done.4
  135.7 10.9 collective-permute-done.5
  147.9 19.3 %while.29 = (s32[]{:T(128)}, f32[3,384,384]{2,1,0:T(8,128)}, f32[3,256,256]{2,1,0:T(8,128)S(1)}, s32[]{:T(128)}, s32[4,2]{0,1:T(2,128)S(1)}, /*index=5*/f32[2,25...) while((s32[]{:T(128)}, f32[3,384,384]{2,1,0:T(8,128)}, ...), condition=%wide.region_3.4_spmd, body=%wide.region_2.3_spmd.sunk | while | flops 543686656 | bytes 22413668 | solution.py:156
  156.1 1.8 maximum_add_fusion.7
  157.9 8.6 dynamic_update_slice.15
  167.2 1.4 slice.586
  168.6 10.0 collective-permute-start.6
  178.6 3.7 collective-permute-done.6
  183.7 50.2 %collective-permute-start.7 = (bf16[3,256,128]{2,1,0:T(8,128)(2,1)S(1)}, bf16[3,256,128]{2,1,0:T(8,128)(2,1)S(1)}, u32[]{:S(2)}, u32[]{:S(2)}) collective-permute-start(bf16[3,256,128]{2,1,0:T(8,128)(2,1)S(1)} %fusion.100), channel_id=1, source_target_pairs={{0,8},{8,16},{16,24},{24,32},{32,40},{40,48},{48,56},{56,64},{64,7... | collective-permute-start | bytes 589832 | tf_op jit(solution)/shard_map/ppermute | solution.py:23
  233.8 10.7 collective-permute-done.7
  247.9 126.3 %all-reduce.3.cloned.1.call-done = bf16[2,256,256]{2,1,0:T(8,128)(2,1)} async-done(((bf16[2,256,256]{2,1,0:T(8,128)(2,1)}), bf16[2,256,256]{2,1,0:T(8,128)(2,1)}) %all-reduce.3.cloned.1.call-update) | async-done | bytes 262160 | tf_op jit(solution)/shard_map/psum | solution.py:170
  375.3 2.0 subtract_bitcast_fusion
  377.3 794.1 %all-reduce.5.cloned.1.call-done = f32[3,256,256]{2,1,0:T(8,128)} async-done(((f32[3,256,256]{2,1,0:T(8,128)}), f32[3,256,256]{2,1,0:T(8,128)}) %all-reduce.5.cloned.1.call-update) | async-done | bytes 786448 | tf_op jit(solution)/shard_map/psum | solution.py:172
  1172.4 1.9 fusion.92
  (88 shorter events, 28.6 us)
Async XLA Ops:
  7.2 14.9 %copy-start.10 = (bf16[1,1,4,256,256]{4,3,2,1,0:T(8,128)(2,1)S(1)}, bf16[1,1,4,256,256]{4,3,2,1,0:T(8,128)(2,1)}, u32[]{:S(2)}) copy-start(bf16[1,1,4,256,256]{4,3,2,1,0:T(8,128)(2,1)} %param.13) | copy-start | bytes 1572868
  7.2 367.0 %all-reduce.3.cloned.1.call-start = ((), (), s32[]{:S(2)}) async-start(), calls=%async_computation | async-start | bytes 524288 | tf_op jit(solution)/shard_map/psum | solution.py:170
  8.3 16.2 %copy-start = (f32[1,2,256,256]{3,2,1,0:T(8,128)S(1)}, f32[1,2,256,256]{3,2,1,0:T(8,128)}, u32[]{:S(2)}) copy-start(f32[1,2,256,256]{3,2,1,0:T(8,128)} %param.12) | copy-start | bytes 1572868
  8.4 14.8 %collective-permute-start = (bf16[2,256,128]{2,1,0:T(8,128)(2,1)S(1)}, bf16[2,256,128]{2,1,0:T(8,128)(2,1)S(1)}, u32[]{:S(2)}, u32[]{:S(2)}) collective-permute-start(bf16[2,256,128]{2,1,0:T(8,128)(2,1)S(1)} %slice.386), channel_id=1, source_target_pairs={{8,0},{16,8},{24,16},{32,24},{40,32},{48,40},{56,48},{64,56},{72,6... | collective-permute-start | bytes 393224 | tf_op jit(solution)/shard_map/ppermute | solution.py:23
  23.2 11.5 collective-permute-start.1
  24.5 11.6 copy-start.11
  56.7 5.9 collective-permute-start.2
  64.7 61.1 %collective-permute-start.3 = (bf16[3,256,128]{2,1,0:T(8,128)(2,1)}, bf16[3,256,128]{2,1,0:T(8,128)(2,1)S(1)}, u32[]{:S(2)}, u32[]{:S(2)}) collective-permute-start(bf16[3,256,128]{2,1,0:T(8,128)(2,1)} %fusion.104), channel_id=1, source_target_pairs={{0,8},{8,16},{16,24},{24,32},{32,40},{40,48},{48,56},{56,64},{64,7... | collective-permute-start | bytes 589832 | tf_op jit(solution)/shard_map/ppermute | solution.py:23
  125.8 1.2 copy-start.4
  125.8 1.5 copy-start.8
  125.9 8.4 copy-start.2
  127.3 0.7 copy-start.6
  128.0 6.3 collective-permute-start.4
  134.4 12.2 %collective-permute-start.5 = (bf16[2,128,384]{2,1,0:T(8,128)(2,1)S(1)}, bf16[2,128,384]{2,1,0:T(8,128)(2,1)S(1)}, u32[]{:S(2)}, u32[]{:S(2)}) collective-permute-start(bf16[2,128,384]{2,1,0:T(8,128)(2,1)S(1)} %pad_maximum_fusion.4), channel_id=1, source_target_pairs={{32,0},{40,8},{48,16},{56,24},{64,32},{72,40},{80,48},{88,56},{96,... | collective-permute-start | bytes 589832 | tf_op jit(solution)/shard_map/ppermute | solution.py:23
  167.2 16.5 %copy-start.1 = (f32[3,256,256]{2,1,0:T(8,128)}, f32[3,256,256]{2,1,0:T(8,128)S(1)}, u32[]{:S(2)}) copy-start(f32[3,256,256]{2,1,0:T(8,128)S(1)} %get-tuple-element.280) | copy-start | bytes 2359300
  168.6 13.7 %collective-permute-start.6 = (bf16[3,128,384]{2,1,0:T(8,128)(2,1)S(1)}, bf16[3,128,384]{2,1,0:T(8,128)(2,1)S(1)}, u32[]{:S(2)}, u32[]{:S(2)}) collective-permute-start(bf16[3,128,384]{2,1,0:T(8,128)(2,1)S(1)} %slice.586), channel_id=1, source_target_pairs={{0,32},{8,40},{16,48},{24,56},{32,64},{40,72},{48,80},{56,88},{64,... | collective-permute-start | bytes 884744 | tf_op jit(solution)/shard_map/ppermute | solution.py:23
  183.7 60.9 %collective-permute-start.7 = (bf16[3,256,128]{2,1,0:T(8,128)(2,1)S(1)}, bf16[3,256,128]{2,1,0:T(8,128)(2,1)S(1)}, u32[]{:S(2)}, u32[]{:S(2)}) collective-permute-start(bf16[3,256,128]{2,1,0:T(8,128)(2,1)S(1)} %fusion.100), channel_id=1, source_target_pairs={{0,8},{8,16},{16,24},{24,32},{32,40},{40,48},{48,56},{56,64},{64,7... | collective-permute-start | bytes 589832 | tf_op jit(solution)/shard_map/ppermute | solution.py:23
  244.6 1.1 copy-start.3
  244.6 1.3 copy-start.5
  244.6 1.3 copy-start.7
  244.6 1.5 copy-start.9
  247.1 924.3 %all-reduce.5.cloned.1.call-start = ((), (), s32[]{:S(2)}) async-start(), calls=%async_computation.1 | async-start | bytes 1572864 | tf_op jit(solution)/shard_map/psum | solution.py:172
Sparse Core Ops, SparseCore 0:
  247.2 126.8 all-reduce.2
  377.7 793.6 all-reduce.4
where the time goes:
time: 1190 us; the launch traced here: 1180 us
  waiting for transfers between devices  975 us (82%)
  starting transfers between devices  130 us (11%)
  local copies, waits for them, and re-layouts  28.2 us (2%)
  other arithmetic  20.8 us (2%)
  between operations  14.4 us (1%)
    psum x1, waiting for transfers between devices, shards(): probe_totals = lax.psum(probe_sum, 'tile')  794 us
    ppermute x8, starting transfers between devices, passed_along(): return lax.ppermute(value, axis, pairs)  130 us
    psum x1, waiting for transfers between devices, shards(): summed = lax.psum(combined.astype(jnp.bfloat16), 'scan').astype(jnp.float32)  126 us
    ppermute x8, waiting for transfers between devices, passed_along(): return lax.ppermute(value, axis, pairs)  54.1 us
  transfers between devices with their start and end apart: 10, of which 9 were waited for; matrix products, arithmetic and copies ran while one was open for 0% of the time, Pallas kernels for 0%

commit v1 on v0

v1 whole, which is shorter than its diff:
```python
import functools
import math

import jax
import jax.numpy as jnp
import ml_dtypes
import numpy as np
from jax import lax
from jax.experimental import pallas as pl
from jax.experimental.pallas import tpu as pltpu
from jax.sharding import PartitionSpec as P

PS = 256
TS = 256
OVER = 128
SPAN = TS + OVER
TGW = 4
TILES = 96
RING = 12
RUN = 4
COLS = 4
OWNERS = 8
LANES = 128
penalty = 0.5
smoothing = 0.05
probe_step = 3.0
MESH = pl.DeviceIdType.MESH
VMEM = pl.BlockSpec(memory_space=pltpu.VMEM)
SMEM = pl.BlockSpec(memory_space=pltpu.SMEM)


def transform_tables():
    index = np.arange(PS, dtype=np.int64)
    angle = ((index[:, None] * index[None, :]) % PS).astype(np.float64) * (2.0 * math.pi / PS)
    scale = 1.0 / math.sqrt(PS)
    real = (np.cos(angle) * scale).astype(np.float32)
    imag = (-np.sin(angle) * scale).astype(np.float32)
    forward = np.block([[real, -imag], [imag, real]])
    return forward.astype(ml_dtypes.bfloat16), forward.T.astype(ml_dtypes.bfloat16)


def shifted_in(block, col, lane):
    amount = lax.rem(LANES - col, LANES)
    turned = [pltpu.roll(piece, amount, axis=1) for piece in block]
    keep = lane < LANES - col
    return [jnp.where(keep, turned[k], turned[k + 1]) for k in range(2)]


def shifted_out(left, right, col, lane):
    amount = lax.rem(col, LANES)
    left = pltpu.roll(left, amount, axis=1)
    right = pltpu.roll(right, amount, axis=1)
    past = lane >= col
    zero = jnp.zeros_like(left)
    return [jnp.where(past, left, zero), jnp.where(past, right, left), jnp.where(past, zero, right)]


def patches_kernel(first, R0, R1, *refs):
    if first:
        (off_ref, cnt_ref, wide_ref, probe_ref, amp_ref, m1_ref, m2_ref,
         center_ref, rr_ref, rb_ref, rd_ref, psum_ref,
         tot_ref, e_ref, r_ref, win_ref) = refs
        acc_ref = psum_ref
    else:
        (off_ref, cnt_ref, wide_ref, probe_ref, amp_ref, m1_ref, m2_ref, prev_ref,
         center_ref, rr_ref, rb_ref, rd_ref, psum_ref,
         tot_ref, e_ref, r_ref, win_ref, acc_ref) = refs
    channels = 3 if first else 2
    tot_ref[...] = jnp.zeros_like(tot_ref)
    if first:
        acc_ref[...] = jnp.zeros_like(acc_ref)
    else:
        acc_ref[...] = prev_ref[...]
    half = [pl.ds(0, LANES), pl.ds(LANES, LANES)]

    def visit(slot, carry):
        row = off_ref[slot, 0]
        col = off_ref[slot, 1]
        lane0 = lax.broadcasted_iota(jnp.int32, (R0, LANES), 1)
        lane1 = lax.broadcasted_iota(jnp.int32, (R1, LANES), 1)

        def gather(step, c):
            r = pl.multiple_of(step * R0, R0)
            real = shifted_in([wide_ref[0, k, pl.ds(row + r, R0), :] for k in range(3)], col, lane0)
            imag = shifted_in([wide_ref[1, k, pl.ds(row + r, R0), :] for k in range(3)], col, lane0)
            for h in range(2):
                wr, wi = real[h], imag[h]
                pr = probe_ref[0, pl.ds(r, R0), half[h]]
                pi = probe_ref[1, pl.ds(r, R0), half[h]]
                win_ref[0, pl.ds(r, R0), half[h]] = wr
                win_ref[1, pl.ds(r, R0), half[h]] = wi
                e_ref[pl.ds(r, R0), half[h]] = (pr * wr - pi * wi).astype(jnp.bfloat16)
                e_ref[pl.ds(PS + r, R0), half[h]] = (pr * wi + pi * wr).astype(jnp.bfloat16)
            return c

        lax.fori_loop(0, PS // R0, gather, 0)
        for r in range(0, PS, R1):
            re = jnp.dot(m1_ref[r:r + R1, :], e_ref[...], preferred_element_type=jnp.float32)
            im = jnp.dot(m1_ref[PS + r:PS + r + R1, :], e_ref[...], preferred_element_type=jnp.float32)
            inner = jnp.concatenate([re.astype(jnp.bfloat16), im.astype(jnp.bfloat16)], 1)
            wave = jnp.dot(inner, m2_ref[...], preferred_element_type=jnp.float32)
            wr, wi = wave[:, :PS], wave[:, PS:]
            factor = amp_ref[slot, r:r + R1, :].astype(jnp.float32) * lax.rsqrt(wr * wr + wi * wi + smoothing) - 1.0
            r_ref[r:r + R1, :] = (wr * factor).astype(jnp.bfloat16)
            r_ref[PS + r:PS + r + R1, :] = (wi * factor).astype(jnp.bfloat16)
        for r in range(0, PS, R1):
            re = jnp.dot(m2_ref[r:r + R1, :], r_ref[...], preferred_element_type=jnp.float32)
            im = jnp.dot(m2_ref[PS + r:PS + r + R1, :], r_ref[...], preferred_element_type=jnp.float32)
            inner = jnp.concatenate([re.astype(jnp.bfloat16), im.astype(jnp.bfloat16)], 1)
            back = jnp.dot(inner, m1_ref[...], preferred_element_type=jnp.float32)
            rows = pl.ds(r, R1)
            terms = [[], [], []]
            for h in range(2):
                br = back[:, h * LANES:(h + 1) * LANES]
                bi = back[:, PS + h * LANES:PS + (h + 1) * LANES]
                pr = probe_ref[0, rows, half[h]]
                pi = probe_ref[1, rows, half[h]]
                wr = win_ref[0, rows, half[h]]
                wi = win_ref[1, rows, half[h]]
                terms[0].append(pr * br + pi * bi)
                terms[1].append(pr * bi - pi * br)
                if first:
                    terms[2].append(pr * pr + pi * pi)
                acc_ref[0, rows, half[h]] += wr * br + wi * bi
                acc_ref[1, rows, half[h]] += wr * bi - wi * br
                acc_ref[2, rows, half[h]] += wr * wr + wi * wi
            for c in range(channels):
                out = shifted_out(terms[c][0], terms[c][1], col, lane1)
                for k in range(3):
                    tot_ref[c, k, pl.ds(row + r, R1), :] += out[k]
        return carry

    lax.fori_loop(0, cnt_ref[0, 0], visit, 0)
    for k in range(2):
        center_ref[:, :, half[k]] = tot_ref[:, k, :TS, :]
        rb_ref[:, :, half[k]] = tot_ref[:, k, TS:, :].astype(jnp.bfloat16)
    rr_ref[...] = tot_ref[:, 2, :TS, :].astype(jnp.bfloat16)
    rd_ref[...] = tot_ref[:, 2, TS:, :].astype(jnp.bfloat16)
    if not first:
        for part in range(8):
            rows = pl.ds(part * 32, 32)
            for c in range(3):
                psum_ref[part // 4, part % 4, c] = acc_ref[c, rows, :].astype(jnp.bfloat16)


def patches(first, corners, count, wide, probe, measured, m1, m2, prev=None, R0=256, R1=256):
    channels = 3 if first else 2
    shape = jax.ShapeDtypeStruct
    out_shape = (
        shape((channels, TS, TS), jnp.float32),
        shape((channels, TS, OVER), jnp.bfloat16),
        shape((channels, OVER, TS), jnp.bfloat16),
        shape((channels, OVER, OVER), jnp.bfloat16),
        shape((3, PS, PS), jnp.float32) if first else shape((2, 4, 3, 32, PS), jnp.bfloat16),
    )
    scratch = [
        pltpu.VMEM((channels, 3, SPAN, LANES), jnp.float32),
        pltpu.VMEM((2 * PS, PS), jnp.bfloat16),
        pltpu.VMEM((2 * PS, PS), jnp.bfloat16),
        pltpu.VMEM((2, PS, PS), jnp.float32),
    ]
    args = [corners, count, wide, probe, measured, m1, m2]
    if not first:
        args.append(prev)
        scratch.append(pltpu.VMEM((3, PS, PS), jnp.float32))
    return pl.pallas_call(
        functools.partial(patches_kernel, first, R0, R1),
        out_shape=out_shape,
        in_specs=[SMEM, SMEM] + [VMEM] * (len(args) - 2),
        out_specs=(VMEM,) * 5,
        scratch_shapes=scratch,
        compiler_params=pltpu.CompilerParams(vmem_limit_bytes=28 * 1024 * 1024),
        name="patches",
    )(*args)


def place():
    t = lax.axis_index("tile")
    return t, lax.rem(t, TGW)


def moved(t, by):
    return lax.rem(t + (by + TILES), TILES)


def remote(src, dst, sends, recvs, at, slot, target):
    return pltpu.make_async_remote_copy(
        src_ref=src, dst_ref=dst, send_sem=sends.at[at], recv_sem=recvs.at[slot],
        device_id=target, device_id_type=MESH,
    )


def greet(targets):
    barrier = pltpu.get_barrier_semaphore()
    for target in targets:
        pl.semaphore_signal(barrier, inc=1, device_id=target, device_id_type=MESH)
    pl.semaphore_wait(barrier, len(targets))


def as_float(flag):
    return jnp.where(flag, 1.0, 0.0).astype(jnp.float32)


def split_estimate(value, c, a, b, wide_ref, side_ref, top_ref, corner_ref):
    rounded = value.astype(jnp.bfloat16)
    rows, cols = pl.ds(a * OVER, OVER), pl.ds(b * OVER, OVER)
    wide_ref[c, b, rows, :] = rounded.astype(jnp.float32)
    if b == 0:
        side_ref[c, rows, :] = rounded
    if a == 0:
        top_ref[c, :, cols] = rounded
    if a == 0 and b == 0:
        corner_ref[c] = rounded


def take_rims(t, column, wide_ref, side_in, top_in, corner_in):
    right = as_float(column < TGW - 1)
    below = as_float(t < TILES - TGW)
    for c in range(2):
        wide_ref[c, 2, :TS, :] = side_in[c].astype(jnp.float32) * right
        for b in range(2):
            wide_ref[c, b, TS:, :] = top_in[c, :, b * OVER:(b + 1) * OVER].astype(jnp.float32) * below
        wide_ref[c, 2, TS:, :] = corner_in[c].astype(jnp.float32) * (right * below)


def pull_copies(t, side, top, corner, side_in, top_in, corner_in, sends, recvs, base):
    return (
        remote(corner, corner_in, sends, recvs, base, base, {"tile": moved(t, -TGW - 1)}),
        remote(top, top_in, sends, recvs, base + 1, base + 1, {"tile": moved(t, -TGW)}),
        remote(side, side_in, sends, recvs, base + 2, base + 2, {"tile": moved(t, -1)}),
    )


def push_copies(t, rr, rb, rd, left_in, above_in, corner_in, sends, recvs):
    return (
        remote(rb, above_in, sends, recvs, 0, 0, {"tile": moved(t, TGW)}),
        remote(rr, left_in, sends, recvs, 1, 1, {"tile": moved(t, 1)}),
        remote(rd, corner_in, sends, recvs, 2, 2, {"tile": moved(t, TGW + 1)}),
    )


def quadrant_total(c, a, b, center_ref, left_in, above_in, corner_in, left, above):
    rows, cols = pl.ds(a * OVER, OVER), pl.ds(b * OVER, OVER)
    value = center_ref[c, rows, cols]
    if a == 0:
        value = value + above_in[c, :, cols].astype(jnp.float32) * above
    if b == 0:
        value = value + left_in[c, rows, :].astype(jnp.float32) * left
    if a == 0 and b == 0:
        value = value + corner_in[c].astype(jnp.float32) * (left * above)
    return value


QUADRANTS = ((0, 0), (0, 1), (1, 0), (1, 1))


def open_kernel(cons_ref, wide_ref, side, top, corner, side_in, top_in, corner_in, sends, recvs):
    t, column = place()
    for a, b in QUADRANTS:
        for c in range(2):
            value = cons_ref[c, a * OVER:(a + 1) * OVER, b * OVER:(b + 1) * OVER]
            split_estimate(value, c, a, b, wide_ref, side, top, corner)
    greet([{"tile": moved(t, by)} for by in (1, TGW, TGW + 1)])
    copies = pull_copies(t, side, top, corner, side_in, top_in, corner_in, sends, recvs, 0)
    for copy in copies:
        copy.start()
    for copy in copies:
        copy.wait()
    take_rims(t, column, wide_ref, side_in, top_in, corner_in)


def middle_kernel(center_ref, rr, rb, rd, cons_ref, dual_ref, est_ref, inv_ref, wide_ref,
                  left_in, above_in, rim_in, side, top, corner, side_in, top_in, corner_in, sends, recvs):
    t, column = place()
    greet([{"tile": moved(t, by)} for by in (1, TGW, TGW + 1, -1, -TGW, -TGW - 1)])
    pushes = push_copies(t, rr, rb, rd, left_in, above_in, rim_in, sends, recvs)
    for copy in pushes:
        copy.start()
    for copy in pushes:
        copy.wait_recv()
    pulls = pull_copies(t, side, top, corner, side_in, top_in, corner_in, sends, recvs, 3)
    left = as_float(column > 0)
    above = as_float(t >= TGW)
    for at, (a, b) in enumerate(QUADRANTS):
        rows, cols = pl.ds(a * OVER, OVER), pl.ds(b * OVER, OVER)
        total = [quadrant_total(c, a, b, center_ref, left_in, above_in, rim_in, left, above) for c in range(3)]
        inv = 1.0 / (total[2] + penalty)
        inv_ref[rows, cols] = inv
        for c in range(2):
            value = cons_ref[c, rows, cols] + (total[c] - penalty * dual_ref[c, rows, cols]) * inv
            est_ref[c, rows, cols] = value
            split_estimate(value, c, a, b, wide_ref, side, top, corner)
        if at < 3:
            pulls[at].start()
    for copy in pulls:
        copy.wait_recv()
    take_rims(t, column, wide_ref, side_in, top_in, corner_in)
    for copy in pushes + pulls:
        copy.wait_send()


def close_kernel(center_ref, rr, rb, rd, cons_ref, dual_ref, est_ref, inv_ref, psum, probe_ref,
                 cons_out, dual_out, probe_out,
                 left_in, above_in, rim_in, half_in, half, run_in, ring_out, ring_in, grown,
                 mine, cols_in, part, part_in, settled, kept,
                 rim_s, rim_r, half_s, half_r, run_s, run_r, ring_s, ring_r, grow_s, grow_r,
                 wide_s, wide_r, back_s, back_r, col_s, col_r, pair_s, pair_r, out_s, out_r):
    t, column = place()
    core = lax.rem(t, 2)
    z = lax.rem(lax.div(t, 2), RING)
    y = lax.div(t, 2 * RING)
    scan = lax.axis_index("scan")
    yh = lax.rem(scan, 2)
    x = lax.div(scan, 2)
    tile_at = lambda y_, z_, c_: {"tile": (y_ * RING + z_) * 2 + c_}
    scan_at = lambda x_, h_: {"scan": x_ * 2 + h_}
    ys = [lax.rem(y + k, RUN) for k in range(1, RUN)]
    xs = [lax.rem(x + k, COLS) for k in range(1, COLS)]
    sibling = tile_at(y, z, 1 - core)
    twin = scan_at(x, 1 - yh)

    greet([{"tile": moved(t, by)} for by in (-1, -TGW, -TGW - 1)] + [sibling, twin]
          + [tile_at(k, z, core) for k in ys] + [scan_at(k, yh) for k in xs]
          + [tile_at(y, lax.rem(z + k, RING), core) for k in range(1, RING)])

    pushes = push_copies(t, rr, rb, rd, left_in, above_in, rim_in, rim_s, rim_r)
    for copy in pushes:
        copy.start()
    to_half = remote(psum.at[1 - core], half_in, half_s, half_r, 0, 0, sibling)
    to_half.start()

    to_half.wait_recv()
    for q in range(RUN):
        half[q] = (psum[core, q].astype(jnp.float32) + half_in[q].astype(jnp.float32)).astype(jnp.bfloat16)
    for k in ys:
        remote(half.at[k], run_in.at[y], run_s, run_r, k, y, tile_at(k, z, core)).start()

    for copy in pushes:
        copy.wait_recv()
    left = as_float(column > 0)
    above = as_float(t >= TGW)
    for a, b in QUADRANTS:
        rows, cols = pl.ds(a * OVER, OVER), pl.ds(b * OVER, OVER)
        inv = inv_ref[rows, cols]
        for c in range(2):
            total = quadrant_total(c, a, b, center_ref, left_in, above_in, rim_in, left, above)
            dual = dual_ref[c, rows, cols]
            estimate = est_ref[c, rows, cols]
            value = estimate + (total + penalty * (cons_ref[c, rows, cols] - dual - estimate)) * inv + dual
            kept[c, rows, cols] = value
            value = value.astype(jnp.bfloat16)
            for q in range(2):
                mine[2 * a + q, c, :, cols] = value[q * 64:(q + 1) * 64]
    for k in xs:
        remote(mine.at[k], cols_in.at[x], col_s, col_r, k, x, scan_at(k, yh)).start()

    for k in ys:
        remote(half.at[k], run_in.at[k], run_s, run_r, k, k, tile_at(k, z, core)).wait_recv()
    run_in[y] = half[y]
    for c in range(3):
        summed = run_in[0, c].astype(jnp.float32)
        for k in range(1, RUN):
            summed = summed + run_in[k, c].astype(jnp.float32)
        summed = summed.astype(jnp.bfloat16)
        for k in range(OWNERS):
            ring_out[k, c] = summed[(k // 2) * 8:(k // 2) * 8 + 8, (k % 2) * LANES:(k % 2 + 1) * LANES]

    def ring_step(k, c):
        other = lax.rem(z + k, RING)

        @pl.when(other < OWNERS)
        def _():
            remote(ring_out.at[other], ring_in.at[z], ring_s, ring_r, other, z, tile_at(y, other, core)).start()

        return c

    lax.fori_loop(1, RING, ring_step, 0)

    for k in xs:
        remote(mine.at[k], cols_in.at[k], col_s, col_r, k, k, scan_at(k, yh)).wait_recv()
    cols_in[x] = mine[x]
    for c in range(2):
        summed = cols_in[0, c].astype(jnp.float32)
        for k in range(1, COLS):
            summed = summed + cols_in[k, c].astype(jnp.float32)
        part[c] = summed.astype(jnp.bfloat16)
    to_twin = remote(part, part_in, pair_s, pair_r, 0, 0, twin)
    to_twin.start()

    @pl.when(z < OWNERS)
    def _():
        ring_in[z] = ring_out[z]

        def ring_wait(k, c):
            other = lax.rem(z + k, RING)
            remote(ring_in.at[other], ring_in.at[other], ring_s, ring_r, 0, other, tile_at(y, other, core)).wait_recv()
            return c

        lax.fori_loop(1, RING, ring_wait, 0)
        sums = []
        for c in range(3):
            summed = ring_in[0, c].astype(jnp.float32)
            for k in range(1, RING):
                summed = summed + ring_in[k, c].astype(jnp.float32)
            sums.append(summed)
        scale = probe_step * lax.rsqrt(sums[2] + 1.0)
        for c in range(2):
            grown[core, y, z, c] = (sums[c] * scale).astype(jnp.bfloat16)

        def grow_step(k, c):
            other = lax.rem(z + k, RING)
            own = grown.at[core, y, z]
            remote(own, own, grow_s, grow_r, other, z, tile_at(y, other, core)).start()
            return c

        lax.fori_loop(1, RING, grow_step, 0)

    to_twin.wait_recv()
    shares = []
    for c in range(2):
        shares.append((part[c].astype(jnp.float32) + part_in[c].astype(jnp.float32)) * 0.125)
    modulus = jnp.sqrt(shares[0] * shares[0] + shares[1] * shares[1])
    bound = 1.0 / jnp.maximum(modulus, 1.0)
    for c in range(2):
        settled[x, c] = (shares[c] * bound).astype(jnp.bfloat16)
    for k in xs:
        own = settled.at[x]
        remote(own, own, out_s, out_r, k, x, scan_at(k, yh)).start()

    def grow_wait(k, c):
        other = lax.rem(z + k, RING)

        @pl.when(other < OWNERS)
        def _():
            slot = grown.at[core, y, other]
            remote(slot, slot, grow_s, grow_r, 0, other, tile_at(y, other, core)).wait_recv()

        return c

    lax.fori_loop(1, RING, grow_wait, 0)
    for k in ys:
        own = grown.at[core, y]
        remote(own, own, wide_s, wide_r, k, y, tile_at(k, z, core)).start()

    for k in xs:
        slot = settled.at[k]
        remote(slot, slot, out_s, out_r, k, k, scan_at(k, yh)).wait_recv()
    for q in range(COLS):
        rows = pl.ds(q * 64, 64)
        for c in range(2):
            value = settled[q, c].astype(jnp.float32)
            cons_out[c, rows, :] = value
            dual_out[c, rows, :] = kept[c, rows, :] - value

    for k in ys:
        slot = grown.at[core, k]
        remote(slot, slot, wide_s, wide_r, k, k, tile_at(k, z, core)).wait_recv()
    own = grown.at[core]
    to_back = remote(own, own, back_s, back_r, 0, 0, sibling)
    to_back.start()
    slot = grown.at[1 - core]
    remote(slot, slot, back_s, back_r, 0, 0, sibling).wait_recv()
    for part_at in range(8):
        for k in range(OWNERS):
            rows = pl.ds(part_at * 32 + (k // 2) * 8, 8)
            cols = pl.ds((k % 2) * LANES, LANES)
            for c in range(2):
                step = grown[part_at // 4, part_at % 4, k, c].astype(jnp.float32)
                probe_out[c, rows, cols] = probe_ref[c, rows, cols] + step

    for copy in pushes:
        copy.wait_send()
    to_half.wait_send()
    to_twin.wait_send()
    to_back.wait_send()
    for k in ys:
        remote(half.at[k], run_in.at[y], run_s, run_r, k, y, tile_at(k, z, core)).wait_send()
        own = grown.at[core, y]
        remote(own, own, wide_s, wide_r, k, y, tile_at(k, z, core)).wait_send()
    for k in xs:
        remote(mine.at[k], cols_in.at[x], col_s, col_r, k, x, scan_at(k, yh)).wait_send()
        own = settled.at[x]
        remote(own, own, out_s, out_r, k, x, scan_at(k, yh)).wait_send()

    def ring_sent(k, c):
        other = lax.rem(z + k, RING)

        @pl.when(other < OWNERS)
        def _():
            remote(ring_out.at[other], ring_in.at[z], ring_s, ring_r, other, z, tile_at(y, other, core)).wait_send()

        @pl.when(z < OWNERS)
        def _():
            own = grown.at[core, y, z]
            remote(own, own, grow_s, grow_r, other, z, tile_at(y, other, core)).wait_send()

        return c

    lax.fori_loop(1, RING, ring_sent, 0)


def params(identity):
    return pltpu.CompilerParams(
        collective_id=identity, has_side_effects=True, vmem_limit_bytes=20 * 1024 * 1024
    )


def rim_buffers(channels):
    return [
        pltpu.VMEM((channels, TS, OVER), jnp.bfloat16),
        pltpu.VMEM((channels, OVER, TS), jnp.bfloat16),
        pltpu.VMEM((channels, OVER, OVER), jnp.bfloat16),
    ]


def copies_of(count):
    return [pltpu.SemaphoreType.DMA((count,)), pltpu.SemaphoreType.DMA((count,))]


WIDE = jax.ShapeDtypeStruct((2, 3, SPAN, LANES), jnp.float32)
FIELD = jax.ShapeDtypeStruct((2, TS, TS), jnp.float32)


def open_halo(cons):
    return pl.pallas_call(
        open_kernel, out_shape=WIDE, in_specs=[VMEM], out_specs=VMEM,
        scratch_shapes=rim_buffers(2) + rim_buffers(2) + copies_of(3),
        compiler_params=params(1), name="open_halo",
    )(cons)


def middle(center, rr, rb, rd, cons, dual):
    return pl.pallas_call(
        middle_kernel,
        out_shape=(FIELD, jax.ShapeDtypeStruct((TS, TS), jnp.float32), WIDE),
        in_specs=[VMEM] * 6, out_specs=(VMEM,) * 3,
        scratch_shapes=rim_buffers(3) + rim_buffers(2) + rim_buffers(2) + copies_of(6),
        compiler_params=params(2), name="middle",
    )(center, rr, rb, rd, cons, dual)


def close(center, rr, rb, rd, cons, dual, est, inv, psum, probe):
    buffer = lambda *shape: pltpu.VMEM(shape, jnp.bfloat16)
    scratch = rim_buffers(2) + [
        buffer(RUN, 3, 32, PS), buffer(RUN, 3, 32, PS), buffer(RUN, 3, 32, PS),
        buffer(OWNERS, 3, 8, LANES), buffer(RING, 3, 8, LANES), buffer(2, RUN, OWNERS, 2, 8, LANES),
        buffer(COLS, 2, 64, TS), buffer(COLS, 2, 64, TS), buffer(2, 64, TS), buffer(2, 64, TS),
        buffer(COLS, 2, 64, TS), pltpu.VMEM((2, TS, TS), jnp.float32),
    ]
    for count in (3, 1, RUN, RING, RING, RUN, 1, COLS, 1, COLS):
        scratch += copies_of(count)
    return pl.pallas_call(
        close_kernel, out_shape=(FIELD,) * 3, in_specs=[VMEM] * 10, out_specs=(VMEM,) * 3,
        scratch_shapes=scratch, compiler_params=params(3), name="close",
    )(center, rr, rb, rd, cons, dual, est, inv, psum, probe)


def shards(consensus, duals, probes, amplitudes, offsets, counts):
    m1, m2 = (jnp.asarray(table) for table in transform_tables())
    cons, dual, probe = consensus[0], duals[0, 0], probes[0]
    measured, corners = amplitudes[0, 0], offsets[0, 0]
    wide = open_halo(cons)
    center, rr, rb, rd, psum = patches(True, corners, counts, wide, probe, measured, m1, m2)
    est, inv, wide = middle(center, rr, rb, rd, cons, dual)
    center, rr, rb, rd, psum = patches(False, corners, counts, wide, probe, measured, m1, m2, psum)
    cons_new, dual_new, probe_new = close(center, rr, rb, rd, cons, dual, est, inv, psum, probe)
    return cons_new[None], dual_new[None, None], probe_new[None]


def solution(mesh):
    placed = (
        P("tile", None, None, None),
        P("scan", "tile", None, None, None),
        P("scan", None, None, None),
        P("scan", "tile", None, None, None),
        P("scan", "tile", None, None),
        P("scan", "tile"),
    )
    return jax.shard_map(
        shards,
        mesh=mesh,
        in_specs=placed,
        out_specs=(
            P("tile", None, None, None),
            P("scan", "tile", None, None, None),
            P("scan", None, None, None),
        ),
        check_vma=False,
    )
```

time: 1190 us -> 120 us (0.10)
  waiting for transfers between devices: 975 us -> 0 us
  starting transfers between devices: 130 us -> 0 us
  Pallas kernels: 0 us -> 113 us
  local copies, waits for them, and re-layouts: 28.2 us -> 5.24 us
  other arithmetic: 20.8 us -> 0 us
  between operations: 14.4 us -> 1.37 us
    psum x2 -> x0, waiting for transfers between devices: 920 us -> none  [the longest x1 794 us: shards(): probe_totals = lax.psum(probe_sum, 'tile')]
    ppermute x8 -> x0, starting transfers between devices: 130 us -> none  [passed_along(): return lax.ppermute(value, axis, pairs)]
    pallas_call x0 -> x5, Pallas kernels: none -> 113 us  [the longest x1 44.8 us: close(): pl.pallas_call(close_kernel, out_shape=(FIELD,) * 3, in_specs=[VMEM] * 10...]
    ppermute x8 -> x0, waiting for transfers between devices: 54.1 us -> none  [passed_along(): return lax.ppermute(value, axis, pairs)]
    dynamic_update_slice x2 -> x0, local copies, waits for them, and re-layouts: 17.3 us -> none  [visit_slot(): lax.dynamic_update_slice(local_totals, region + object_terms, (zero_index...]
  transfers between devices with their start and end apart: 10 -> 0, of which waited for: 9 -> 0; matrix products, arithmetic and copies ran while one was open for 0% -> 0% of each run, Pallas kernels for 0% -> 0%
where the time goes in v1:
time: 120 us
  Pallas kernels  113 us (94%)
  local copies, waits for them, and re-layouts  5.24 us (4%)
  between operations  1.37 us (1%)
    pallas_call x1, Pallas kernels, close(): pl.pallas_call(close_kernel, out_shape=(FIELD,) * 3, in_specs=[VMEM] * 10...  44.8 us
    pallas_call x1, Pallas kernels, middle(): pl.pallas_call(middle_kernel, out_shape=(FIELD, jax.ShapeDtypeStruct((TS,...  35.7 us
    pallas_call x1, Pallas kernels, open_halo(): pl.pallas_call(open_kernel, out_shape=WIDE, in_specs=[VMEM], out_specs=VM...  27.8 us
    pallas_call x2, Pallas kernels, patches(): pl.pallas_call(functools.partial(patches_kernel, first, R0, R1), out_shap...  4.8 us
    unnamed x17, local copies, waits for them, and re-layouts  4.48 us

profile of v1, /device:TPU:1, one launch (start us, length us, event | category | flops | bytes accessed | tf_op | source)
XLA Modules:
  0.0 119.7 jit_solution(6876300109909230928)
XLA Ops:
  1.3 0.8 copy.12.refs_0_
  2.0 0.0 copy-start
  2.0 1.0 copy-done
  3.1 0.0 copy-start.2
  3.1 0.0 copy-start.4
  3.1 0.0 copy-start.5
  3.1 27.8 %open_halo.1.refs_2_ = f32[2,3,384,128]{3,2,1,0:T(8,128)S(1)} custom-call(f32[2,256,256]{2,1,0:T(8,128)S(1)} %bitcast.8), custom_call_target="tpu_custom_call" | custom-call | tf_op jit(solution)/shard_map/open_halo/pallas_call | solution.py:525
  30.9 0.0 copy-done.2
  30.9 0.0 copy-done.4
  30.9 0.0 copy-done.5
  30.9 0.0 copy-start.6
  30.9 1.0 copy-done.6
  32.0 0.0 copy-start.1
  32.0 0.0 copy-start.3
  32.0 2.4 %patches.2 = (f32[3,256,256]{2,1,0:T(8,128)S(1)}, bf16[3,256,128]{2,1,0:T(8,128)(2,1)S(1)}, bf16[3,128,256]{2,1,0:T(8,128)(2,1)S(1)}, bf16[3,128,128]{2,1,0:T(8,128)(2,1)S(1)}, f32[3,256,256]{2,1,0:T(8,128)S(1)}) custom-call(s32[4,2]{1,0:T(4,128)S(1)} %copy.12.refs_0_, s32[1,1]{1,0:T(1,128)S(6)} %copy.16.refs_1_, f32[2,3,384,128]{3,2,1,0:T(8,128)S(1)} %open_halo.1.refs_2_, ...), custom_call_target="tpu_custom_call" | custom-call | tf_op jit(solution)/shard_map/patches/pallas_call | solution.py:166
  34.4 0.0 copy-done.1
  34.4 0.0 copy-done.3
  34.4 35.7 %middle.1 = (f32[2,256,256]{2,1,0:T(8,128)S(1)}, f32[256,256]{1,0:T(8,128)S(1)}, f32[2,3,384,128]{3,2,1,0:T(8,128)S(1)}) custom-call(f32[3,256,256]{2,1,0:T(8,128)S(1)} %get-tuple-element.19.center_ref, bf16[3,256,128]{2,1,0:T(8,128)(2,1)S(1)} %get-tuple-element.20.rr, bf16[3,128,256]{2,1,0:T(8,128)(2,1)S(1)} %get-tuple-element.21.rb, ...), custom_call_target="tpu_custom_call" | custom-call | tf_op jit(solution)/shard_map/middle/pallas_call | solution.py:533
  70.2 2.4 %patches.3 = (f32[2,256,256]{2,1,0:T(8,128)S(1)}, bf16[2,256,128]{2,1,0:T(8,128)(2,1)S(1)}, bf16[2,128,256]{2,1,0:T(8,128)(2,1)S(1)}, bf16[2,128,128]{2,1,0:T(8,128)(2,1)S(1)}, bf16[2,4,3,32,256]{4,3,2,1,0:T(8,128)(2,1)S(1)}) custom-call(s32[4,2]{1,0:T(4,128)S(1)} %copy.12.refs_0_, s32[1,1]{1,0:T(1,128)S(6)} %copy.16.refs_1_, ...), custom_call_target="tpu_custom_call" | custom-call | tf_op jit(solution)/shard_map/patches/pallas_call | solution.py:166
  72.5 44.8 %close.1 = (f32[2,256,256]{2,1,0:T(8,128)S(1)}, f32[2,256,256]{2,1,0:T(8,128)S(1)}, f32[2,256,256]{2,1,0:T(8,128)S(1)}) custom-call(f32[2,256,256]{2,1,0:T(8,128)S(1)} %get-tuple-element.25.center_ref, bf16[2,256,128]{2,1,0:T(8,128)(2,1)S(1)} %get-tuple-element.26.rr, bf16[2,128,256]{2,1,0:T(8,128)(2,1)S(1)} %get-tuple-element.27.rb, ...), custom_call_target="tpu_custom_call" | custom-call | tf_op jit(solution)/shard_map/close/pallas_call | solution.py:552
  117.4 0.8 copy.17
  118.2 0.8 copy.18
  119.0 0.8 copy.19
Async XLA Ops:
  2.0 1.0 copy-start
  3.1 27.8 %copy-start.2 = (f32[1,2,256,256]{3,2,1,0:T(8,128)S(1)}, f32[1,2,256,256]{3,2,1,0:T(8,128)}, u32[]{:S(2)}) copy-start(f32[1,2,256,256]{3,2,1,0:T(8,128)} %param.10) | copy-start | bytes 1572868
  3.1 27.8 %copy-start.4 = (bf16[1,1,4,256,256]{4,3,2,1,0:T(8,128)(2,1)S(1)}, bf16[1,1,4,256,256]{4,3,2,1,0:T(8,128)(2,1)}, u32[]{:S(2)}) copy-start(bf16[1,1,4,256,256]{4,3,2,1,0:T(8,128)(2,1)} %param.11) | copy-start | bytes 1572868
  3.1 27.8 %copy-start.5 = (bf16[512,512]{1,0:T(8,128)(2,1)S(1)}, bf16[512,512]{1,0:T(8,128)(2,1)}, u32[]{:S(2)}) copy-start(bf16[512,512]{1,0:T(8,128)(2,1)} %constant.5.clone.refs_6_) | copy-start | bytes 1572868
  30.9 1.0 copy-start.6
  32.0 2.4 %copy-start.1 = (f32[1,2,256,256]{3,2,1,0:T(8,128)S(1)}, f32[1,2,256,256]{3,2,1,0:T(8,128)}, u32[]{:S(2)}) copy-start(f32[1,2,256,256]{3,2,1,0:T(8,128)} %param.8) | copy-start | bytes 1572868
  32.0 2.4 %copy-start.3 = (f32[1,1,2,256,256]{4,3,2,1,0:T(8,128)S(1)}, f32[1,1,2,256,256]{4,3,2,1,0:T(8,128)}, u32[]{:S(2)}) copy-start(f32[1,1,2,256,256]{4,3,2,1,0:T(8,128)} %param.9) | copy-start | bytes 1572868

commit v2 on v0

v2 whole, which is shorter than its diff:
```python
import functools
import math

import jax
import jax.numpy as jnp
import ml_dtypes
import numpy as np
from jax import lax
from jax.experimental import pallas as pl
from jax.experimental.pallas import tpu as pltpu
from jax.sharding import PartitionSpec as P

PS = 256
TS = 256
OVER = 128
SPAN = TS + OVER
TGW = 4
SLOTS = 4
TILES = 96
RING = 12
RUN = 4
COLS = 4
OWNERS = 8
LANES = 128
penalty = 0.5
smoothing = 0.05
probe_step = 3.0
MESH = pl.DeviceIdType.MESH
VMEM = pl.BlockSpec(memory_space=pltpu.VMEM)
SMEM = pl.BlockSpec(memory_space=pltpu.SMEM)


def transform_tables():
    index = np.arange(PS, dtype=np.int64)
    angle = ((index[:, None] * index[None, :]) % PS).astype(np.float64) * (2.0 * math.pi / PS)
    scale = 1.0 / math.sqrt(PS)
    real = (np.cos(angle) * scale).astype(np.float32)
    imag = (-np.sin(angle) * scale).astype(np.float32)
    forward = np.block([[real, -imag], [imag, real]])
    return forward.astype(ml_dtypes.bfloat16), forward.T.astype(ml_dtypes.bfloat16)


def shifted_in(block, col, lane):
    amount = lax.rem(LANES - col, LANES)
    turned = [pltpu.roll(piece, amount, axis=1) for piece in block]
    keep = lane < LANES - col
    return [jnp.where(keep, turned[k], turned[k + 1]) for k in range(2)]


def shifted_out(left, right, col, lane):
    amount = lax.rem(col, LANES)
    left = pltpu.roll(left, amount, axis=1)
    right = pltpu.roll(right, amount, axis=1)
    past = lane >= col
    zero = jnp.zeros_like(left)
    return [jnp.where(past, left, zero), jnp.where(past, right, left), jnp.where(past, zero, right)]


def patches_kernel(first, *refs):
    if first:
        (off_ref, cnt_ref, near_ref, wide_ref, probe_ref, amp_ref, m1_ref, m2_ref,
         center_ref, rr_ref, rb_ref, acc_ref, inv_ref,
         tot_ref, e_ref, r_ref, win_ref, power_ref, weight_ref) = refs
    else:
        (off_ref, cnt_ref, wide_ref, probe_ref, amp_ref, m1_ref, m2_ref, prev_ref,
         center_ref, rr_ref, rb_ref, psum_ref,
         tot_ref, e_ref, r_ref, win_ref, acc_ref) = refs
    tot_ref[...] = jnp.zeros_like(tot_ref)
    if first:
        acc_ref[...] = jnp.zeros_like(acc_ref)
    else:
        acc_ref[...] = prev_ref[...]
    half = [pl.ds(0, LANES), pl.ds(LANES, LANES)]
    lane = lax.broadcasted_iota(jnp.int32, (PS, LANES), 1)

    def visit(slot, carry):
        row = off_ref[slot, 0]
        col = off_ref[slot, 1]
        real = shifted_in([wide_ref[0, k, pl.ds(row, PS), :] for k in range(3)], col, lane)
        imag = shifted_in([wide_ref[1, k, pl.ds(row, PS), :] for k in range(3)], col, lane)
        for h in range(2):
            wr, wi = real[h], imag[h]
            pr = probe_ref[0, :, half[h]]
            pi = probe_ref[1, :, half[h]]
            win_ref[0, :, half[h]] = wr
            win_ref[1, :, half[h]] = wi
            e_ref[:PS, half[h]] = (pr * wr - pi * wi).astype(jnp.bfloat16)
            e_ref[PS:, half[h]] = (pr * wi + pi * wr).astype(jnp.bfloat16)
        re = jnp.dot(m1_ref[:PS, :], e_ref[...], preferred_element_type=jnp.float32)
        im = jnp.dot(m1_ref[PS:, :], e_ref[...], preferred_element_type=jnp.float32)
        inner = jnp.concatenate([re.astype(jnp.bfloat16), im.astype(jnp.bfloat16)], 1)
        wave = jnp.dot(inner, m2_ref[...], preferred_element_type=jnp.float32)
        wr, wi = wave[:, :PS], wave[:, PS:]
        factor = amp_ref[slot].astype(jnp.float32) * lax.rsqrt(wr * wr + wi * wi + smoothing) - 1.0
        r_ref[:PS, :] = (wr * factor).astype(jnp.bfloat16)
        r_ref[PS:, :] = (wi * factor).astype(jnp.bfloat16)
        re = jnp.dot(m2_ref[:PS, :], r_ref[...], preferred_element_type=jnp.float32)
        im = jnp.dot(m2_ref[PS:, :], r_ref[...], preferred_element_type=jnp.float32)
        inner = jnp.concatenate([re.astype(jnp.bfloat16), im.astype(jnp.bfloat16)], 1)
        back = jnp.dot(inner, m1_ref[...], preferred_element_type=jnp.float32)
        terms = [[], []]
        for h in range(2):
            br = back[:, h * LANES:(h + 1) * LANES]
            bi = back[:, PS + h * LANES:PS + (h + 1) * LANES]
            pr = probe_ref[0, :, half[h]]
            pi = probe_ref[1, :, half[h]]
            wr = win_ref[0, :, half[h]]
            wi = win_ref[1, :, half[h]]
            terms[0].append(pr * br + pi * bi)
            terms[1].append(pr * bi - pi * br)
            acc_ref[0, :, half[h]] += wr * br + wi * bi
            acc_ref[1, :, half[h]] += wr * bi - wi * br
            acc_ref[2, :, half[h]] += wr * wr + wi * wi
        for c in range(2):
            out = shifted_out(terms[c][0], terms[c][1], col, lane)
            for k in range(3):
                tot_ref[c, k, pl.ds(row, PS), :] += out[k]
        return carry

    lax.fori_loop(0, cnt_ref[0, 0], visit, 0)
    for k in range(2):
        center_ref[:, :, half[k]] = tot_ref[:, k, :TS, :]
        rb_ref[k] = tot_ref[:, k, TS:, :].astype(jnp.bfloat16)
    rr_ref[...] = tot_ref[:, 2].astype(jnp.bfloat16)
    if first:
        weight_ref[...] = jnp.zeros_like(weight_ref)
        power_ref[...] = probe_ref[0] * probe_ref[0] + probe_ref[1] * probe_ref[1]

        def weigh(at, col, aside):
            out = shifted_out(power_ref[:, half[0]], power_ref[:, half[1]], col, lane)
            if aside:
                weight_ref[0, pl.ds(at, PS), :] += out[2]
            else:
                weight_ref[0, pl.ds(at, PS), :] += out[0]
                weight_ref[1, pl.ds(at, PS), :] += out[1]

        def own(slot, carry):
            weigh(off_ref[slot, 0] + TS, off_ref[slot, 1], False)
            return carry

        def left(slot, carry):
            weigh(near_ref[0, slot, 0] + TS, near_ref[0, slot, 1], True)
            return carry

        def above(slot, carry):
            weigh(near_ref[1, slot, 0], near_ref[1, slot, 1], False)
            return carry

        def corner(slot, carry):
            weigh(near_ref[2, slot, 0], near_ref[2, slot, 1], True)
            return carry

        lax.fori_loop(0, cnt_ref[0, 0], own, 0)
        lax.fori_loop(0, near_ref[0, SLOTS, 0], left, 0)
        lax.fori_loop(0, near_ref[1, SLOTS, 0], above, 0)
        lax.fori_loop(0, near_ref[2, SLOTS, 0], corner, 0)
        for k in range(2):
            inv_ref[:, half[k]] = 1.0 / (weight_ref[k, TS:2 * TS, :] + penalty)
    else:
        for part in range(8):
            rows = pl.ds(part * 32, 32)
            for c in range(3):
                psum_ref[part // 4, part % 4, c] = acc_ref[c, rows, :].astype(jnp.bfloat16)


def patches(first, corners, count, wide, probe, measured, m1, m2, near=None, prev=None):
    shape = jax.ShapeDtypeStruct
    out_shape = [
        shape((2, TS, TS), jnp.float32),
        shape((2, SPAN, OVER), jnp.bfloat16),
        shape((2, 2, OVER, OVER), jnp.bfloat16),
    ]
    scratch = [
        pltpu.VMEM((2, 3, SPAN, LANES), jnp.float32),
        pltpu.VMEM((2 * PS, PS), jnp.bfloat16),
        pltpu.VMEM((2 * PS, PS), jnp.bfloat16),
        pltpu.VMEM((2, PS, PS), jnp.float32),
    ]
    if first:
        args = [corners, count, near, wide, probe, measured, m1, m2]
        scalars = 3
        out_shape += [shape((3, PS, PS), jnp.float32), shape((TS, TS), jnp.float32)]
        scratch += [pltpu.VMEM((PS, PS), jnp.float32), pltpu.VMEM((2, TS + SPAN, LANES), jnp.float32)]
    else:
        args = [corners, count, wide, probe, measured, m1, m2, prev]
        scalars = 2
        out_shape += [shape((2, RUN, 3, 32, PS), jnp.bfloat16)]
        scratch += [pltpu.VMEM((3, PS, PS), jnp.float32)]
    return pl.pallas_call(
        functools.partial(patches_kernel, first),
        out_shape=tuple(out_shape),
        in_specs=[SMEM] * scalars + [VMEM] * (len(args) - scalars),
        out_specs=(VMEM,) * len(out_shape),
        scratch_shapes=scratch,
        compiler_params=pltpu.CompilerParams(vmem_limit_bytes=28 * 1024 * 1024),
        name="patches",
    )(*args)


def moved(t, by):
    return lax.rem(t + (by + TILES), TILES)


def remote(src, dst, sends, recvs, at, slot, target):
    return pltpu.make_async_remote_copy(
        src_ref=src, dst_ref=dst, send_sem=sends.at[at], recv_sem=recvs.at[slot],
        device_id=target, device_id_type=MESH,
    )


def greet(targets):
    barrier = pltpu.get_barrier_semaphore()
    for target in targets:
        pl.semaphore_signal(barrier, inc=1, device_id=target, device_id_type=MESH)
    pl.semaphore_wait(barrier, len(targets))


def start_if(flag, *copies):
    @pl.when(flag)
    def _():
        for copy in copies:
            copy.start()


def wait_if(flag, *copies):
    @pl.when(flag)
    def _():
        for copy in copies:
            copy.wait_recv()


def sent_if(flag, *copies):
    @pl.when(flag)
    def _():
        for copy in copies:
            copy.wait_send()


def clear_if(flag, *refs):
    @pl.when(flag)
    def _():
        for ref in refs:
            ref[...] = jnp.zeros_like(ref)


def sides(t):
    column = lax.rem(t, TGW)
    return column > 0, column < TGW - 1, t >= TGW, t < TILES - TGW


def block(at):
    return pl.ds(at * OVER, OVER)


class Pull:
    def __init__(self, t, quads, below_in, right_in, corner_in, sends, recvs, base):
        self.left, self.right, self.above, self.below = sides(t)
        self.refs = quads, below_in, right_in, corner_in
        up, back = {"tile": moved(t, -TGW)}, {"tile": moved(t, -1)}
        make = lambda src, dst, at, to: remote(src, dst, sends, recvs, at, at, to)
        self.up = [[make(quads.at[b, c], below_in.at[b, c], base + 2 * b + c, up) for c in range(2)] for b in range(2)]
        self.side = [[make(quads.at[2 * a, c], right_in.at[a, c], base + 4 + 2 * a + c, back) for c in range(2)] for a in range(2)]
        self.relay = [make(below_in.at[0, c], corner_in.at[c], base + 8 + c, back) for c in range(2)]

    def clear(self):
        quads, below_in, right_in, corner_in = self.refs
        clear_if(jnp.logical_not(self.right), right_in, corner_in)
        clear_if(jnp.logical_not(self.below), below_in)

    def offer(self, value, c, a, b, wide_ref):
        rounded = value.astype(jnp.bfloat16)
        wide_ref[c, b, block(a), :] = rounded.astype(jnp.float32)
        if not (a and b):
            self.refs[0][2 * a + b, c] = rounded

    def begin(self, c, a, b):
        if a == 0:
            start_if(self.above, self.up[b][c])
        if b == 0:
            start_if(self.left, self.side[a][c])

    def finish(self, wide_ref):
        quads, below_in, right_in, corner_in = self.refs
        for c in range(2):
            wait_if(self.below, self.up[0][c])
            start_if(self.left, self.relay[c])
        for c in range(2):
            wait_if(self.below, self.up[1][c])
            wait_if(self.right, self.side[0][c], self.side[1][c])
            for a in range(2):
                wide_ref[c, 2, block(a), :] = right_in[a, c].astype(jnp.float32)
            for b in range(2):
                wide_ref[c, b, TS:, :] = below_in[b, c].astype(jnp.float32)
        for c in range(2):
            wait_if(self.right, self.relay[c])
            wide_ref[c, 2, TS:, :] = corner_in[c].astype(jnp.float32)
        for c in range(2):
            sent_if(self.above, self.up[0][c], self.up[1][c])
            sent_if(self.left, self.side[0][c], self.side[1][c], self.relay[c])


QUADRANTS = ((1, 1), (1, 0), (0, 1), (0, 0))


def open_kernel(cons_ref, corner_ref, count_ref, wide_ref, near_ref,
                quads, below_in, right_in, corner_in, note, note_in, sends, recvs):
    t = lax.axis_index("tile")
    pull = Pull(t, quads, below_in, right_in, corner_in, sends, recvs, 0)
    pull.clear()
    note[...] = jnp.zeros_like(note)
    note[0:SLOTS, 0:2] = corner_ref[...]
    note[SLOTS:SLOTS + 1, 0:1] = count_ref[...]
    for a, b in QUADRANTS:
        for c in range(2):
            pull.offer(cons_ref[c, block(a), block(b)], c, a, b, wide_ref)
    greet([{"tile": moved(t, by)} for by in (1, TGW, -1, -TGW, -TGW - 1)])
    notes = [
        remote(note, note_in.at[k], sends, recvs, 10 + k, 10 + k, {"tile": moved(t, by)})
        for k, by in enumerate((1, TGW, TGW + 1))
    ]
    for b in range(2):
        for c in range(2):
            pull.begin(c, 0, b)
    for c in range(2):
        pull.begin(c, 1, 0)
    for copy in notes:
        copy.start()
    pull.finish(wide_ref)
    for copy in notes:
        copy.wait()
    for k, flag in enumerate((pull.left, pull.above, jnp.logical_and(pull.left, pull.above))):
        near_ref[k] = note_in[k] * jnp.where(flag, 1, 0)


def middle_kernel(center_ref, rr, rb, inv_ref, cons_ref, dual_ref, est_ref, wide_ref,
                  left_in, above_in, lowered, quads, below_in, right_in, corner_in, sends, recvs):
    t = lax.axis_index("tile")
    left, right, above, below = sides(t)
    pull = Pull(t, quads, below_in, right_in, corner_in, sends, recvs, 6)
    pull.clear()
    clear_if(jnp.logical_not(left), left_in)
    clear_if(jnp.logical_not(above), above_in)
    on, down = {"tile": moved(t, 1)}, {"tile": moved(t, TGW)}
    make = lambda src, dst, at, to: remote(src, dst, sends, recvs, at, at, to)
    push_on = [make(rr.at[c], left_in.at[c], c, on) for c in range(2)]
    push_far = [make(rb.at[1, c], above_in.at[1, c], 2 + c, down) for c in range(2)]
    push_low = [make(lowered.at[c], above_in.at[0, c], 4 + c, down) for c in range(2)]
    greet([{"tile": moved(t, by)} for by in (1, TGW, -1, -TGW)])

    def push(c):
        start_if(right, push_on[c])
        start_if(below, push_far[c])

    def relay(c):
        wait_if(left, push_on[c])
        lowered[c] = (rb[0, c].astype(jnp.float32) + left_in[c, TS:, :].astype(jnp.float32)).astype(jnp.bfloat16)
        start_if(below, push_low[c])

    def update(c, a, b):
        rows, cols = block(a), block(b)
        total = center_ref[c, rows, cols]
        if a == 0:
            total = total + above_in[b, c].astype(jnp.float32)
        if b == 0:
            total = total + left_in[c, rows, :].astype(jnp.float32)
        value = cons_ref[c, rows, cols] + (total - penalty * dual_ref[c, rows, cols]) * inv_ref[rows, cols]
        est_ref[c, rows, cols] = value
        pull.offer(value, c, a, b, wide_ref)
        pull.begin(c, a, b)

    push(0)
    update(0, 1, 1)
    relay(0)
    push(1)
    for c in range(2):
        if c == 1:
            update(1, 1, 1)
            relay(1)
        update(c, 1, 0)
        wait_if(above, push_far[c])
        update(c, 0, 1)
        wait_if(above, push_low[c])
        update(c, 0, 0)
    pull.finish(wide_ref)
    for c in range(2):
        sent_if(right, push_on[c])
        sent_if(below, push_far[c], push_low[c])


def close_kernel(center_ref, rr, rb, cons_ref, dual_ref, est_ref, inv_ref, psum, probe_ref,
                 cons_out, dual_out, probe_out,
                 left_in, above_in, lowered, half_in, half, run_in, ring_out, ring_in, grown,
                 mine, cols_in, part, part_in, settled, kept,
                 rim_s, rim_r, half_s, half_r, run_s, run_r, ring_s, ring_r, grow_s, grow_r,
                 wide_s, wide_r, back_s, back_r, col_s, col_r, pair_s, pair_r, out_s, out_r):
    t = lax.axis_index("tile")
    left, right, above, below = sides(t)
    core = lax.rem(t, 2)
    z = lax.rem(lax.div(t, 2), RING)
    y = lax.div(t, 2 * RING)
    scan = lax.axis_index("scan")
    yh = lax.rem(scan, 2)
    x = lax.div(scan, 2)
    tile_at = lambda y_, z_, c_: {"tile": (y_ * RING + z_) * 2 + c_}
    scan_at = lambda x_, h_: {"scan": x_ * 2 + h_}
    ys = [lax.rem(y + k, RUN) for k in range(1, RUN)]
    xs = [lax.rem(x + k, COLS) for k in range(1, COLS)]
    sibling = tile_at(y, z, 1 - core)
    twin = scan_at(x, 1 - yh)
    on, down = {"tile": moved(t, 1)}, {"tile": moved(t, TGW)}
    push_on = remote(rr, left_in, rim_s, rim_r, 0, 0, on)
    push_far = remote(rb.at[1], above_in.at[1], rim_s, rim_r, 1, 1, down)
    push_low = remote(lowered, above_in.at[0], rim_s, rim_r, 2, 2, down)
    to_half = remote(psum.at[1 - core], half_in, half_s, half_r, 0, 0, sibling)

    clear_if(jnp.logical_not(left), left_in)
    clear_if(jnp.logical_not(above), above_in)
    greet([{"tile": moved(t, by)} for by in (-1, -TGW)] + [sibling, twin]
          + [tile_at(k, z, core) for k in ys] + [scan_at(k, yh) for k in xs]
          + [tile_at(y, lax.rem(z + k, RING), core) for k in range(1, RING)])

    start_if(right, push_on)
    start_if(below, push_far)
    to_half.start()

    def cross(n, k, at, other):
        return remote(mine.at[n, k], cols_in.at[n, at], col_s, col_r, (n, k), (n, at), scan_at(other, yh))

    def pair(n):
        return remote(part.at[n], part_in.at[n], pair_s, pair_r, n, n, twin)

    def spread(n, k, at, other):
        own = settled.at[n, at]
        return remote(own, own, out_s, out_r, (n, k), (n, at), scan_at(other, yh))

    def update(n):
        a, b = QUADRANTS[n]
        rows, cols = block(a), block(b)
        inv = inv_ref[rows, cols]
        for c in range(2):
            total = center_ref[c, rows, cols]
            if a == 0:
                total = total + above_in[b, c].astype(jnp.float32)
            if b == 0:
                total = total + left_in[c, rows, :].astype(jnp.float32)
            dual = dual_ref[c, rows, cols]
            estimate = est_ref[c, rows, cols]
            value = estimate + (total + penalty * (cons_ref[c, rows, cols] - dual - estimate)) * inv + dual
            kept[c, rows, cols] = value
            value = value.astype(jnp.bfloat16)
            for q in range(COLS):
                mine[n, q, c] = value[q * 32:(q + 1) * 32]
        for k in xs:
            cross(n, k, x, k).start()

    def combine(n):
        for k in xs:
            cross(n, k, k, k).wait_recv()
        cols_in[n, x] = mine[n, x]
        for c in range(2):
            summed = cols_in[n, 0, c].astype(jnp.float32)
            for k in range(1, COLS):
                summed = summed + cols_in[n, k, c].astype(jnp.float32)
            part[n, c] = summed.astype(jnp.bfloat16)
        pair(n).start()

    def settle(n):
        pair(n).wait_recv()
        shares = [(part[n, c].astype(jnp.float32) + part_in[n, c].astype(jnp.float32)) * 0.125 for c in range(2)]
        modulus = jnp.sqrt(shares[0] * shares[0] + shares[1] * shares[1])
        bound = 1.0 / jnp.maximum(modulus, 1.0)
        for c in range(2):
            settled[n, x, c] = (shares[c] * bound).astype(jnp.bfloat16)
        for k in xs:
            spread(n, k, x, k).start()

    def give(n):
        a, b = QUADRANTS[n]
        for k in xs:
            spread(n, k, k, k).wait_recv()
        for q in range(COLS):
            rows, cols = pl.ds(a * OVER + q * 32, 32), block(b)
            for c in range(2):
                value = settled[n, q, c].astype(jnp.float32)
                cons_out[c, rows, cols] = value
                dual_out[c, rows, cols] = kept[c, rows, cols] - value

    def run_copy(k, at):
        return remote(half.at[k], run_in.at[at], run_s, run_r, k, at, tile_at(k, z, core))

    def ring_copy(other, at):
        return remote(ring_out.at[other], ring_in.at[at], ring_s, ring_r, other, at, tile_at(y, other, core))

    def grow_copy(other, at):
        own = grown.at[core, y, at]
        return remote(own, own, grow_s, grow_r, other, at, tile_at(y, other, core))

    def wide_copy(k, at):
        own = grown.at[core, at]
        return remote(own, own, wide_s, wide_r, k, at, tile_at(k, z, core))

    def back_copy(at):
        own = grown.at[at]
        return remote(own, own, back_s, back_r, 0, 0, sibling)

    def around(step):
        def body(k, carry):
            step(lax.rem(z + k, RING))
            return carry

        lax.fori_loop(1, RING, body, 0)

    def probe_run():
        to_half.wait_recv()
        for q in range(RUN):
            half[q] = (psum[core, q].astype(jnp.float32) + half_in[q].astype(jnp.float32)).astype(jnp.bfloat16)
        for k in ys:
            run_copy(k, y).start()

    def probe_ring():
        for k in ys:
            run_copy(k, k).wait_recv()
        run_in[y] = half[y]
        for c in range(3):
            summed = run_in[0, c].astype(jnp.float32)
            for k in range(1, RUN):
                summed = summed + run_in[k, c].astype(jnp.float32)
            summed = summed.astype(jnp.bfloat16)
            for k in range(OWNERS):
                ring_out[k, c] = summed[(k // 2) * 8:(k // 2) * 8 + 8, (k % 2) * LANES:(k % 2 + 1) * LANES]

        def step(other):
            @pl.when(other < OWNERS)
            def _():
                ring_copy(other, z).start()

        around(step)

    def probe_grow():
        @pl.when(z < OWNERS)
        def _():
            ring_in[z] = ring_out[z]
            around(lambda other: ring_copy(z, other).wait_recv())
            sums = []
            for c in range(3):
                summed = ring_in[0, c].astype(jnp.float32)
                for k in range(1, RING):
                    summed = summed + ring_in[k, c].astype(jnp.float32)
                sums.append(summed)
            scale = probe_step * lax.rsqrt(sums[2] + 1.0)
            for c in range(2):
                grown[core, y, z, c] = (sums[c] * scale).astype(jnp.bfloat16)
            around(lambda other: grow_copy(other, z).start())

    def probe_wide():
        def step(other):
            @pl.when(other < OWNERS)
            def _():
                grow_copy(other, other).wait_recv()

        around(step)
        for k in ys:
            wide_copy(k, y).start()

    def probe_back():
        for k in ys:
            wide_copy(k, k).wait_recv()
        back_copy(core).start()

    def probe_give():
        back_copy(1 - core).wait_recv()
        for part_at in range(8):
            for k in range(OWNERS):
                rows = pl.ds(part_at * 32 + (k // 2) * 8, 8)
                cols = pl.ds((k % 2) * LANES, LANES)
                for c in range(2):
                    step = grown[part_at // 4, part_at % 4, k, c].astype(jnp.float32)
                    probe_out[c, rows, cols] = probe_ref[c, rows, cols] + step

    update(0)
    probe_run()
    wait_if(left, push_on)
    for c in range(2):
        lowered[c] = (rb[0, c].astype(jnp.float32) + left_in[c, TS:, :].astype(jnp.float32)).astype(jnp.bfloat16)
    start_if(below, push_low)
    update(1)
    combine(0)
    probe_ring()
    wait_if(above, push_far)
    update(2)
    settle(0)
    combine(1)
    wait_if(above, push_low)
    update(3)
    combine(2)
    settle(1)
    probe_grow()
    combine(3)
    settle(2)
    probe_wide()
    settle(3)
    give(0)
    give(1)
    probe_back()
    give(2)
    give(3)
    probe_give()

    sent_if(right, push_on)
    sent_if(below, push_far, push_low)
    to_half.wait_send()
    back_copy(core).wait_send()
    for k in ys:
        run_copy(k, y).wait_send()
        wide_copy(k, y).wait_send()
    for n in range(4):
        pair(n).wait_send()
        for k in xs:
            cross(n, k, x, k).wait_send()
            spread(n, k, x, k).wait_send()

    def sent(other):
        @pl.when(other < OWNERS)
        def _():
            ring_copy(other, z).wait_send()

        @pl.when(z < OWNERS)
        def _():
            grow_copy(other, z).wait_send()

    around(sent)


def params(identity):
    return pltpu.CompilerParams(
        collective_id=identity, has_side_effects=True, vmem_limit_bytes=20 * 1024 * 1024
    )


def buffer(*shape):
    return pltpu.VMEM(shape, jnp.bfloat16)


def pull_buffers():
    return [
        buffer(3, 2, OVER, OVER), buffer(2, 2, OVER, OVER), buffer(2, 2, OVER, OVER), buffer(2, OVER, OVER)
    ]


def copies_of(*count):
    return [pltpu.SemaphoreType.DMA(count), pltpu.SemaphoreType.DMA(count)]


WIDE = jax.ShapeDtypeStruct((2, 3, SPAN, LANES), jnp.float32)
FIELD = jax.ShapeDtypeStruct((2, TS, TS), jnp.float32)


def open_halo(cons, corners, counts):
    return pl.pallas_call(
        open_kernel, out_shape=(WIDE, jax.ShapeDtypeStruct((3, 8, LANES), jnp.int32)),
        in_specs=[VMEM] * 3, out_specs=(VMEM,) * 2,
        scratch_shapes=pull_buffers() + [pltpu.VMEM((8, LANES), jnp.int32), pltpu.VMEM((3, 8, LANES), jnp.int32)]
        + copies_of(13),
        compiler_params=params(1), name="open_halo",
    )(cons, corners, counts)


def middle(center, rr, rb, inv, cons, dual):
    return pl.pallas_call(
        middle_kernel,
        out_shape=(FIELD, WIDE),
        in_specs=[VMEM] * 6, out_specs=(VMEM,) * 2,
        scratch_shapes=[buffer(2, SPAN, OVER), buffer(2, 2, OVER, OVER), buffer(2, OVER, OVER)]
        + pull_buffers() + copies_of(16),
        compiler_params=params(2), name="middle",
    )(center, rr, rb, inv, cons, dual)


def close(center, rr, rb, cons, dual, est, inv, psum, probe):
    scratch = [
        buffer(2, SPAN, OVER), buffer(2, 2, OVER, OVER), buffer(2, OVER, OVER),
        buffer(RUN, 3, 32, PS), buffer(RUN, 3, 32, PS), buffer(RUN, 3, 32, PS),
        buffer(OWNERS, 3, 8, LANES), buffer(RING, 3, 8, LANES), buffer(2, RUN, OWNERS, 2, 8, LANES),
        buffer(4, COLS, 2, 32, LANES), buffer(4, COLS, 2, 32, LANES), buffer(4, 2, 32, LANES),
        buffer(4, 2, 32, LANES), buffer(4, COLS, 2, 32, LANES), pltpu.VMEM((2, TS, TS), jnp.float32),
    ]
    for count in ((3,), (1,), (RUN,), (RING,), (RING,), (RUN,), (1,), (4, COLS), (4,), (4, COLS)):
        scratch += copies_of(*count)
    return pl.pallas_call(
        close_kernel, out_shape=(FIELD,) * 3, in_specs=[VMEM] * 9, out_specs=(VMEM,) * 3,
        scratch_shapes=scratch, compiler_params=params(3), name="close",
    )(center, rr, rb, cons, dual, est, inv, psum, probe)


def shards(consensus, duals, probes, amplitudes, offsets, counts):
    m1, m2 = (jnp.asarray(table) for table in transform_tables())
    cons, dual, probe = consensus[0], duals[0, 0], probes[0]
    measured, corners = amplitudes[0, 0], offsets[0, 0]
    wide, near = open_halo(cons, corners, counts)
    center, rr, rb, psum, inv = patches(True, corners, counts, wide, probe, measured, m1, m2, near=near)
    est, wide = middle(center, rr, rb, inv, cons, dual)
    center, rr, rb, psum = patches(False, corners, counts, wide, probe, measured, m1, m2, prev=psum)
    cons_new, dual_new, probe_new = close(center, rr, rb, cons, dual, est, inv, psum, probe)
    return cons_new[None], dual_new[None, None], probe_new[None]


def solution(mesh):
    placed = (
        P("tile", None, None, None),
        P("scan", "tile", None, None, None),
        P("scan", None, None, None),
        P("scan", "tile", None, None, None),
        P("scan", "tile", None, None),
        P("scan", "tile"),
    )
    return jax.shard_map(
        shards,
        mesh=mesh,
        in_specs=placed,
        out_specs=(
            P("tile", None, None, None),
            P("scan", "tile", None, None, None),
            P("scan", None, None, None),
        ),
        check_vma=False,
    )
```

time: 1190 us -> 107 us (0.09)
  waiting for transfers between devices: 975 us -> 0 us
  starting transfers between devices: 130 us -> 0 us
  Pallas kernels: 0 us -> 96.6 us
  other arithmetic: 20.8 us -> 0 us
  local copies, waits for them, and re-layouts: 28.2 us -> 8.38 us
  between operations: 14.4 us -> 1.41 us
    psum x2 -> x0, waiting for transfers between devices: 920 us -> none  [the longest x1 794 us: shards(): probe_totals = lax.psum(probe_sum, 'tile')]
    ppermute x8 -> x0, starting transfers between devices: 130 us -> none  [passed_along(): return lax.ppermute(value, axis, pairs)]
    pallas_call x0 -> x5, Pallas kernels: none -> 96.6 us  [the longest x1 43.9 us: close(): pl.pallas_call(close_kernel, out_shape=(FIELD,) * 3, in_specs=[VMEM] * 9,...]
    ppermute x8 -> x0, waiting for transfers between devices: 54.1 us -> none  [passed_along(): return lax.ppermute(value, axis, pairs)]
    dynamic_update_slice x2 -> x0, local copies, waits for them, and re-layouts: 17.3 us -> none  [visit_slot(): lax.dynamic_update_slice(local_totals, region + object_terms, (zero_index...]
  transfers between devices with their start and end apart: 10 -> 0, of which waited for: 9 -> 0; matrix products, arithmetic and copies ran while one was open for 0% -> 0% of each run, Pallas kernels for 0% -> 0%
where the time goes in v2:
time: 107 us; the launch traced here: 106 us
  Pallas kernels  96.6 us (90%)
  local copies, waits for them, and re-layouts  8.38 us (8%)
  between operations  1.41 us (1%)
    pallas_call x1, Pallas kernels, close(): pl.pallas_call(close_kernel, out_shape=(FIELD,) * 3, in_specs=[VMEM] * 9,...  43.9 us
    pallas_call x1, Pallas kernels, middle(): pl.pallas_call(middle_kernel, out_shape=(FIELD, WIDE), in_specs=[VMEM] *...  24.4 us
    pallas_call x1, Pallas kernels, open_halo(): pl.pallas_call(open_kernel, out_shape=(WIDE, jax.ShapeDtypeStruct((3, 8,...  22.7 us
    unnamed x25, local copies, waits for them, and re-layouts  7.62 us
    pallas_call x2, Pallas kernels, patches(): pl.pallas_call(functools.partial(patches_kernel, first), out_shape=tuple(...  5.6 us

profile of v2, /device:TPU:1, one launch (start us, length us, event | category | flops | bytes accessed | tf_op | source)
XLA Modules:
  0.0 106.4 jit_solution(5989832376643492454)
XLA Ops:
  1.3 0.8 copy.13.corner_ref.refs_0_
  2.0 1.0 copy-done
  3.1 22.7 %open_halo.1 = (f32[2,3,384,128]{3,2,1,0:T(8,128)S(1)}, s32[3,8,128]{2,1,0:T(8,128)S(1)}) custom-call(f32[2,256,256]{2,1,0:T(8,128)S(1)} %bitcast.8, s32[4,2]{1,0:T(4,128)S(1)} %copy.13.corner_ref.refs_0_, s32[1,1]{1,0:T(1,128)S(6)} %copy.17.count_ref.refs_1_), custom_call_target="tpu_custom_call" | custom-call | tf_op jit(solution)/shard_map/open_halo/pallas_call | solution.py:659
  25.8 0.0 copy-start.2
  25.8 1.0 copy-done.2
  26.8 1.0 copy-done.5
  27.9 1.0 copy-done.7
  28.9 1.0 copy-done.9
  30.0 3.2 %patches.2 = (f32[2,256,256]{2,1,0:T(8,128)S(1)}, bf16[2,384,128]{2,1,0:T(8,128)(2,1)S(1)}, bf16[2,2,128,128]{3,2,1,0:T(8,128)(2,1)S(1)}, f32[3,256,256]{2,1,0:T(8,128)S(1)}, f32[256,256]{1,0:T(8,128)S(1)}) custom-call(s32[4,2]{1,0:T(4,128)S(1)} %copy.13.corner_ref.refs_0_, s32[1,1]{1,0:T(1,128)S(6)} %copy.17.count_ref.refs_1_, ...), custom_call_target="tpu_custom_call" | custom-call | tf_op jit(solution)/shard_map/patches/pallas_call | solution.py:189
  33.2 0.0 copy-start.3
  33.2 0.0 copy-start.6
  33.2 0.0 copy-start.8
  33.2 0.0 copy-start.10
  33.3 0.0 copy-done.1
  33.3 0.0 copy-done.4
  33.3 24.4 %middle.1 = (f32[2,256,256]{2,1,0:T(8,128)S(1)}, f32[2,3,384,128]{3,2,1,0:T(8,128)S(1)}) custom-call(f32[2,256,256]{2,1,0:T(8,128)S(1)} %get-tuple-element.21.center_ref, bf16[2,384,128]{2,1,0:T(8,128)(2,1)S(1)} %get-tuple-element.22.rr, bf16[2,2,128,128]{3,2,1,0:T(8,128)(2,1)S(1)} %get-tuple-element.23.rb, f32[256,256]{1,0:T(8,128)S(1)} %get-tuple-element.24.inv_ref, ...), custom_call_target="tpu_custom_call" | custom-call | tf_op jit(solution)/shard_map/middle/pallas_call | solution.py:669
  57.7 0.0 copy-done.3
  57.7 0.0 copy-done.6
  57.7 0.0 copy-done.8
  57.7 2.4 %patches.3 = (f32[2,256,256]{2,1,0:T(8,128)S(1)}, bf16[2,384,128]{2,1,0:T(8,128)(2,1)S(1)}, bf16[2,2,128,128]{3,2,1,0:T(8,128)(2,1)S(1)}, bf16[2,4,3,32,256]{4,3,2,1,0:T(8,128)(2,1)S(1)}) custom-call(s32[4,2]{1,0:T(4,128)S(1)} %copy.13.corner_ref.refs_0_, s32[1,1]{1,0:T(1,128)S(6)} %copy.17.count_ref.refs_1_, ...), custom_call_target="tpu_custom_call" | custom-call | tf_op jit(solution)/shard_map/patches/pallas_call | solution.py:189
  60.1 43.9 %close.1 = (f32[2,256,256]{2,1,0:T(8,128)S(1)}, f32[2,256,256]{2,1,0:T(8,128)S(1)}, f32[2,256,256]{2,1,0:T(8,128)S(1)}) custom-call(f32[2,256,256]{2,1,0:T(8,128)S(1)} %get-tuple-element.27.center_ref, bf16[2,384,128]{2,1,0:T(8,128)(2,1)S(1)} %get-tuple-element.28.rr, bf16[2,2,128,128]{3,2,1,0:T(8,128)(2,1)S(1)} %get-tuple-element.29.rb, ...), custom_call_target="tpu_custom_call" | custom-call | tf_op jit(solution)/shard_map/close/pallas_call | solution.py:689
  104.0 0.8 copy.18
  104.8 0.8 copy.19
  105.6 0.8 copy.20
  (7 shorter events, 0.0 us)
Async XLA Ops:
  2.0 1.0 copy-start
  25.8 1.0 copy-start.2
  26.8 1.0 copy-start.5
  27.9 1.0 copy-start.7
  28.9 1.0 copy-start.9
  30.0 3.3 %copy-start.1 = (f32[1,2,256,256]{3,2,1,0:T(8,128)S(1)}, f32[1,2,256,256]{3,2,1,0:T(8,128)}, u32[]{:S(2)}) copy-start(f32[1,2,256,256]{3,2,1,0:T(8,128)} %param.8) | copy-start | bytes 1572868
  30.0 3.3 %copy-start.4 = (f32[1,1,2,256,256]{4,3,2,1,0:T(8,128)S(1)}, f32[1,1,2,256,256]{4,3,2,1,0:T(8,128)}, u32[]{:S(2)}) copy-start(f32[1,1,2,256,256]{4,3,2,1,0:T(8,128)} %param.9) | copy-start | bytes 1572868
  33.2 24.5 %copy-start.3 = (f32[1,2,256,256]{3,2,1,0:T(8,128)S(1)}, f32[1,2,256,256]{3,2,1,0:T(8,128)}, u32[]{:S(2)}) copy-start(f32[1,2,256,256]{3,2,1,0:T(8,128)} %param.10) | copy-start | bytes 1572868
  33.2 24.5 %copy-start.6 = (bf16[1,1,4,256,256]{4,3,2,1,0:T(8,128)(2,1)S(1)}, bf16[1,1,4,256,256]{4,3,2,1,0:T(8,128)(2,1)}, u32[]{:S(2)}) copy-start(bf16[1,1,4,256,256]{4,3,2,1,0:T(8,128)(2,1)} %param.11) | copy-start | bytes 1572868
  33.2 24.5 %copy-start.8 = (bf16[512,512]{1,0:T(8,128)(2,1)S(1)}, bf16[512,512]{1,0:T(8,128)(2,1)}, u32[]{:S(2)}) copy-start(bf16[512,512]{1,0:T(8,128)(2,1)} %constant.5.clone.refs_7_.refs_6_) | copy-start | bytes 1572868
  33.2 24.5 %copy-start.10 = (bf16[512,512]{1,0:T(8,128)(2,1)S(1)}, bf16[512,512]{1,0:T(8,128)(2,1)}, u32[]{:S(2)}) copy-start(bf16[512,512]{1,0:T(8,128)(2,1)} %constant.4.clone.refs_6_.refs_5_) | copy-start | bytes 1572868

commit v3 on v2

--- a/solution.py
+++ b/solution.py
@@ -20,7 +20,7 @@
 RING = 12
 RUN = 4
 COLS = 4
-OWNERS = 8
+LAPS = 3
 LANES = 128
 penalty = 0.5
 smoothing = 0.05
@@ -74,8 +74,8 @@
     lane = lax.broadcasted_iota(jnp.int32, (PS, LANES), 1)
 
     def visit(slot, carry):
-        row = off_ref[slot, 0]
-        col = off_ref[slot, 1]
+        row = off_ref[0, slot]
+        col = off_ref[1, slot]
         real = shifted_in([wide_ref[0, k, pl.ds(row, PS), :] for k in range(3)], col, lane)
         imag = shifted_in([wide_ref[1, k, pl.ds(row, PS), :] for k in range(3)], col, lane)
         for h in range(2):
@@ -135,25 +135,25 @@
                 weight_ref[1, pl.ds(at, PS), :] += out[1]
 
         def own(slot, carry):
-            weigh(off_ref[slot, 0] + TS, off_ref[slot, 1], False)
+            weigh(off_ref[0, slot] + TS, off_ref[1, slot], False)
             return carry
 
         def left(slot, carry):
-            weigh(near_ref[0, slot, 0] + TS, near_ref[0, slot, 1], True)
+            weigh(near_ref[0, 0, slot] + TS, near_ref[0, 1, slot], True)
             return carry
 
         def above(slot, carry):
-            weigh(near_ref[1, slot, 0], near_ref[1, slot, 1], False)
+            weigh(near_ref[1, 0, slot], near_ref[1, 1, slot], False)
             return carry
 
         def corner(slot, carry):
-            weigh(near_ref[2, slot, 0], near_ref[2, slot, 1], True)
+            weigh(near_ref[2, 0, slot], near_ref[2, 1, slot], True)
             return carry
 
         lax.fori_loop(0, cnt_ref[0, 0], own, 0)
-        lax.fori_loop(0, near_ref[0, SLOTS, 0], left, 0)
-        lax.fori_loop(0, near_ref[1, SLOTS, 0], above, 0)
-        lax.fori_loop(0, near_ref[2, SLOTS, 0], corner, 0)
+        lax.fori_loop(0, near_ref[0, 2, 0], left, 0)
+        lax.fori_loop(0, near_ref[1, 2, 0], above, 0)
+        lax.fori_loop(0, near_ref[2, 2, 0], corner, 0)
         for k in range(2):
             inv_ref[:, half[k]] = 1.0 / (weight_ref[k, TS:2 * TS, :] + penalty)
     else:
@@ -161,6 +161,10 @@
             rows = pl.ds(part * 32, 32)
             for c in range(3):
                 psum_ref[part // 4, part % 4, c] = acc_ref[c, rows, :].astype(jnp.bfloat16)
+
+
+def busy(microseconds):
+    return pl.CostEstimate(flops=microseconds * 1_000_000_000, bytes_accessed=microseconds * 3_000_000, transcendentals=0)
 
 
 def patches(first, corners, count, wide, probe, measured, m1, m2, near=None, prev=None):
@@ -192,8 +196,8 @@
         in_specs=[SMEM] * scalars + [VMEM] * (len(args) - scalars),
         out_specs=(VMEM,) * len(out_shape),
         scratch_shapes=scratch,
-        compiler_params=pltpu.CompilerParams(vmem_limit_bytes=28 * 1024 * 1024),
-        name="patches",
+        compiler_params=pltpu.CompilerParams(vmem_limit_bytes=16 * 1024 * 1024),
+        name="patches", cost_estimate=busy(8),
     )(*args)
 
 
@@ -255,17 +259,20 @@
 class Pull:
     def __init__(self, t, quads, below_in, right_in, corner_in, sends, recvs, base):
         self.left, self.right, self.above, self.below = sides(t)
+        self.gives = jnp.logical_and(self.left, self.above)
+        self.takes = jnp.logical_and(self.right, self.below)
         self.refs = quads, below_in, right_in, corner_in
-        up, back = {"tile": moved(t, -TGW)}, {"tile": moved(t, -1)}
+        up, back, far = ({"tile": moved(t, by)} for by in (-TGW, -1, -TGW - 1))
         make = lambda src, dst, at, to: remote(src, dst, sends, recvs, at, at, to)
         self.up = [[make(quads.at[b, c], below_in.at[b, c], base + 2 * b + c, up) for c in range(2)] for b in range(2)]
         self.side = [[make(quads.at[2 * a, c], right_in.at[a, c], base + 4 + 2 * a + c, back) for c in range(2)] for a in range(2)]
-        self.relay = [make(below_in.at[0, c], corner_in.at[c], base + 8 + c, back) for c in range(2)]
+        self.corner = [make(quads.at[0, c], corner_in.at[c], base + 8 + c, far) for c in range(2)]
 
     def clear(self):
         quads, below_in, right_in, corner_in = self.refs
-        clear_if(jnp.logical_not(self.right), right_in, corner_in)
+        clear_if(jnp.logical_not(self.right), right_in)
         clear_if(jnp.logical_not(self.below), below_in)
+        clear_if(jnp.logical_not(self.takes), corner_in)
 
     def offer(self, value, c, a, b, wide_ref):
         rounded = value.astype(jnp.bfloat16)
@@ -274,6 +281,8 @@
             self.refs[0][2 * a + b, c] = rounded
 
     def begin(self, c, a, b):
+        if a == 0 and b == 0:
+            start_if(self.gives, self.corner[c])
         if a == 0:
             start_if(self.above, self.up[b][c])
         if b == 0:
@@ -282,53 +291,43 @@
     def finish(self, wide_ref):
         quads, below_in, right_in, corner_in = self.refs
         for c in range(2):
-            wait_if(self.below, self.up[0][c])
-            start_if(self.left, self.relay[c])
-        for c in range(2):
-            wait_if(self.below, self.up[1][c])
             wait_if(self.right, self.side[0][c], self.side[1][c])
             for a in range(2):
                 wide_ref[c, 2, block(a), :] = right_in[a, c].astype(jnp.float32)
+            wait_if(self.below, self.up[0][c], self.up[1][c])
             for b in range(2):
                 wide_ref[c, b, TS:, :] = below_in[b, c].astype(jnp.float32)
-        for c in range(2):
-            wait_if(self.right, self.relay[c])
+            wait_if(self.takes, self.corner[c])
             wide_ref[c, 2, TS:, :] = corner_in[c].astype(jnp.float32)
         for c in range(2):
             sent_if(self.above, self.up[0][c], self.up[1][c])
-            sent_if(self.left, self.side[0][c], self.side[1][c], self.relay[c])
-
-
-QUADRANTS = ((1, 1), (1, 0), (0, 1), (0, 0))
+            sent_if(self.left, self.side[0][c], self.side[1][c])
+            sent_if(self.gives, self.corner[c])
 
 
 def open_kernel(cons_ref, corner_ref, count_ref, wide_ref, near_ref,
                 quads, below_in, right_in, corner_in, note, note_in, sends, recvs):
     t = lax.axis_index("tile")
     pull = Pull(t, quads, below_in, right_in, corner_in, sends, recvs, 0)
-    pull.clear()
+    greet([{"tile": moved(t, by)} for by in (1, TGW, TGW + 1, -1, -TGW, -TGW - 1)])
     note[...] = jnp.zeros_like(note)
-    note[0:SLOTS, 0:2] = corner_ref[...]
-    note[SLOTS:SLOTS + 1, 0:1] = count_ref[...]
-    for a, b in QUADRANTS:
-        for c in range(2):
-            pull.offer(cons_ref[c, block(a), block(b)], c, a, b, wide_ref)
-    greet([{"tile": moved(t, by)} for by in (1, TGW, -1, -TGW, -TGW - 1)])
+    note[0:2, 0:SLOTS] = corner_ref[...]
+    note[2:3, 0:1] = count_ref[...]
     notes = [
         remote(note, note_in.at[k], sends, recvs, 10 + k, 10 + k, {"tile": moved(t, by)})
         for k, by in enumerate((1, TGW, TGW + 1))
     ]
-    for b in range(2):
+    for a, b in ((0, 0), (0, 1), (1, 0), (1, 1)):
         for c in range(2):
-            pull.begin(c, 0, b)
-    for c in range(2):
-        pull.begin(c, 1, 0)
+            pull.offer(cons_ref[c, block(a), block(b)], c, a, b, wide_ref)
+            pull.begin(c, a, b)
     for copy in notes:
         copy.start()
+    pull.clear()
     pull.finish(wide_ref)
     for copy in notes:
         copy.wait()
-    for k, flag in enumerate((pull.left, pull.above, jnp.logical_and(pull.left, pull.above))):
+    for k, flag in enumerate((pull.left, pull.above, pull.gives)):
         near_ref[k] = note_in[k] * jnp.where(flag, 1, 0)
 
 
@@ -345,7 +344,7 @@
     push_on = [make(rr.at[c], left_in.at[c], c, on) for c in range(2)]
     push_far = [make(rb.at[1, c], above_in.at[1, c], 2 + c, down) for c in range(2)]
     push_low = [make(lowered.at[c], above_in.at[0, c], 4 + c, down) for c in range(2)]
-    greet([{"tile": moved(t, by)} for by in (1, TGW, -1, -TGW)])
+    greet([{"tile": moved(t, by)} for by in (1, TGW, TGW + 1, -1, -TGW)])
 
     def push(c):
         start_if(right, push_on[c])
@@ -389,9 +388,9 @@
 
 def close_kernel(center_ref, rr, rb, cons_ref, dual_ref, est_ref, inv_ref, psum, probe_ref,
                  cons_out, dual_out, probe_out,
-                 left_in, above_in, lowered, half_in, half, run_in, ring_out, ring_in, grown,
+                 left_in, above_in, lowered, half_in, half, run_in, ring_out, ring_in, tri_out, tri_in, grown,
                  mine, cols_in, part, part_in, settled, kept,
-                 rim_s, rim_r, half_s, half_r, run_s, run_r, ring_s, ring_r, grow_s, grow_r,
+                 rim_s, rim_r, half_s, half_r, run_s, run_r, ring_s, ring_r, tri_s, tri_r, grow_s, grow_r,
                  wide_s, wide_r, back_s, back_r, col_s, col_r, pair_s, pair_r, out_s, out_r):
     t = lax.axis_index("tile")
     left, right, above, below = sides(t)
@@ -405,6 +404,11 @@
     scan_at = lambda x_, h_: {"scan": x_ * 2 + h_}
     ys = [lax.rem(y + k, RUN) for k in range(1, RUN)]
     xs = [lax.rem(x + k, COLS) for k in range(1, COLS)]
+    lap, seat = lax.div(z, RUN), lax.rem(z, RUN)
+    seats = [lax.rem(seat + k, RUN) for k in range(1, RUN)]
+    laps = [lax.rem(lap + k, LAPS) for k in range(1, LAPS)]
+    at_seat = lambda k: tile_at(y, lap * RUN + k, core)
+    at_lap = lambda k: tile_at(y, k * RUN + seat, core)
     sibling = tile_at(y, z, 1 - core)
     twin = scan_at(x, 1 - yh)
     on, down = {"tile": moved(t, 1)}, {"tile": moved(t, TGW)}
@@ -417,7 +421,7 @@
     clear_if(jnp.logical_not(above), above_in)
     greet([{"tile": moved(t, by)} for by in (-1, -TGW)] + [sibling, twin]
           + [tile_at(k, z, core) for k in ys] + [scan_at(k, yh) for k in xs]
-          + [tile_at(y, lax.rem(z + k, RING), core) for k in range(1, RING)])
+          + [at_seat(k) for k in seats] + [at_lap(k) for k in laps])
 
     start_if(right, push_on)
     start_if(below, push_far)
@@ -433,8 +437,7 @@
         own = settled.at[n, at]
         return remote(own, own, out_s, out_r, (n, k), (n, at), scan_at(other, yh))
 
-    def update(n):
-        a, b = QUADRANTS[n]
+    def update(a, b):
         rows, cols = block(a), block(b)
         inv = inv_ref[rows, cols]
         for c in range(2):
@@ -449,7 +452,9 @@
             kept[c, rows, cols] = value
             value = value.astype(jnp.bfloat16)
             for q in range(COLS):
-                mine[n, q, c] = value[q * 32:(q + 1) * 32]
+                mine[a, q, c, :, cols] = value[q * 32:(q + 1) * 32]
+
+    def share(n):
         for k in xs:
             cross(n, k, x, k).start()
 
@@ -475,25 +480,27 @@
             spread(n, k, x, k).start()
 
     def give(n):
-        a, b = QUADRANTS[n]
         for k in xs:
             spread(n, k, k, k).wait_recv()
         for q in range(COLS):
-            rows, cols = pl.ds(a * OVER + q * 32, 32), block(b)
+            rows = pl.ds(n * OVER + q * 32, 32)
             for c in range(2):
                 value = settled[n, q, c].astype(jnp.float32)
-                cons_out[c, rows, cols] = value
-                dual_out[c, rows, cols] = kept[c, rows, cols] - value
+                cons_out[c, rows, :] = value
+                dual_out[c, rows, :] = kept[c, rows, :] - value
 
     def run_copy(k, at):
         return remote(half.at[k], run_in.at[at], run_s, run_r, k, at, tile_at(k, z, core))
 
-    def ring_copy(other, at):
-        return remote(ring_out.at[other], ring_in.at[at], ring_s, ring_r, other, at, tile_at(y, other, core))
-
-    def grow_copy(other, at):
+    def ring_copy(k, at):
+        return remote(ring_out.at[k], ring_in.at[at], ring_s, ring_r, k, at, at_seat(k))
+
+    def tri_copy(k, at):
+        return remote(tri_out, tri_in.at[at], tri_s, tri_r, k, at, at_lap(k))
+
+    def grow_copy(k, at):
         own = grown.at[core, y, at]
-        return remote(own, own, grow_s, grow_r, other, at, tile_at(y, other, core))
+        return remote(own, own, grow_s, grow_r, k, at, at_seat(k))
 
     def wide_copy(k, at):
         own = grown.at[core, at]
@@ -502,13 +509,6 @@
     def back_copy(at):
         own = grown.at[at]
         return remote(own, own, back_s, back_r, 0, 0, sibling)
-
-    def around(step):
-        def body(k, carry):
-            step(lax.rem(z + k, RING))
-            return carry
-
-        lax.fori_loop(1, RING, body, 0)
 
     def probe_run():
         to_half.wait_recv()
@@ -526,39 +526,42 @@
             for k in range(1, RUN):
                 summed = summed + run_in[k, c].astype(jnp.float32)
             summed = summed.astype(jnp.bfloat16)
-            for k in range(OWNERS):
-                ring_out[k, c] = summed[(k // 2) * 8:(k // 2) * 8 + 8, (k % 2) * LANES:(k % 2 + 1) * LANES]
-
-        def step(other):
-            @pl.when(other < OWNERS)
-            def _():
-                ring_copy(other, z).start()
-
-        around(step)
+            for k in range(RUN):
+                ring_out[k, c] = summed[k * 8:k * 8 + 8]
+        for k in seats:
+            ring_copy(k, seat).start()
+
+    def probe_tri():
+        for k in seats:
+            ring_copy(k, k).wait_recv()
+        ring_in[seat] = ring_out[seat]
+        for c in range(3):
+            summed = ring_in[0, c].astype(jnp.float32)
+            for k in range(1, RUN):
+                summed = summed + ring_in[k, c].astype(jnp.float32)
+            tri_out[c] = summed.astype(jnp.bfloat16)
+        for k in laps:
+            tri_copy(k, lap).start()
 
     def probe_grow():
-        @pl.when(z < OWNERS)
-        def _():
-            ring_in[z] = ring_out[z]
-            around(lambda other: ring_copy(z, other).wait_recv())
-            sums = []
-            for c in range(3):
-                summed = ring_in[0, c].astype(jnp.float32)
-                for k in range(1, RING):
-                    summed = summed + ring_in[k, c].astype(jnp.float32)
-                sums.append(summed)
-            scale = probe_step * lax.rsqrt(sums[2] + 1.0)
-            for c in range(2):
-                grown[core, y, z, c] = (sums[c] * scale).astype(jnp.bfloat16)
-            around(lambda other: grow_copy(other, z).start())
+        for k in laps:
+            tri_copy(k, k).wait_recv()
+        tri_in[lap] = tri_out[...]
+        sums = []
+        for c in range(3):
+            summed = tri_in[0, c].astype(jnp.float32)
+            for k in range(1, LAPS):
+                summed = summed + tri_in[k, c].astype(jnp.float32)
+            sums.append(summed)
+        scale = probe_step * lax.rsqrt(sums[2] + 1.0)
+        for c in range(2):
+            grown[core, y, seat, c] = (sums[c] * scale).astype(jnp.bfloat16)
+        for k in seats:
+            grow_copy(k, seat).start()
 
     def probe_wide():
-        def step(other):
-            @pl.when(other < OWNERS)
-            def _():
-                grow_copy(other, other).wait_recv()
-
-        around(step)
+        for k in seats:
+            grow_copy(k, k).wait_recv()
         for k in ys:
             wide_copy(k, y).start()
 
@@ -570,40 +573,36 @@
     def probe_give():
         back_copy(1 - core).wait_recv()
         for part_at in range(8):
-            for k in range(OWNERS):
-                rows = pl.ds(part_at * 32 + (k // 2) * 8, 8)
-                cols = pl.ds((k % 2) * LANES, LANES)
+            for k in range(RUN):
+                rows = pl.ds(part_at * 32 + k * 8, 8)
                 for c in range(2):
                     step = grown[part_at // 4, part_at % 4, k, c].astype(jnp.float32)
-                    probe_out[c, rows, cols] = probe_ref[c, rows, cols] + step
-
-    update(0)
+                    probe_out[c, rows, :] = probe_ref[c, rows, :] + step
+
+    update(1, 1)
     probe_run()
     wait_if(left, push_on)
     for c in range(2):
         lowered[c] = (rb[0, c].astype(jnp.float32) + left_in[c, TS:, :].astype(jnp.float32)).astype(jnp.bfloat16)
     start_if(below, push_low)
-    update(1)
-    combine(0)
+    update(1, 0)
+    share(1)
     probe_ring()
     wait_if(above, push_far)
-    update(2)
-    settle(0)
+    update(0, 1)
     combine(1)
     wait_if(above, push_low)
-    update(3)
-    combine(2)
+    update(0, 0)
+    share(0)
+    probe_tri()
+    combine(0)
     settle(1)
     probe_grow()
-    combine(3)
-    settle(2)
+    settle(0)
     probe_wide()
-    settle(3)
-    give(0)
     give(1)
     probe_back()
-    give(2)
-    give(3)
+    give(0)
     probe_give()
 
     sent_if(right, push_on)
@@ -613,27 +612,21 @@
     for k in ys:
         run_copy(k, y).wait_send()
         wide_copy(k, y).wait_send()
-    for n in range(4):
+    for k in seats:
+        ring_copy(k, seat).wait_send()
+        grow_copy(k, seat).wait_send()
+    for k in laps:
+        tri_copy(k, lap).wait_send()
+    for n in range(2):
         pair(n).wait_send()
         for k in xs:
             cross(n, k, x, k).wait_send()
             spread(n, k, x, k).wait_send()
 
-    def sent(other):
-        @pl.when(other < OWNERS)
-        def _():
-            ring_copy(other, z).wait_send()
-
-        @pl.when(z < OWNERS)
-        def _():
-            grow_copy(other, z).wait_send()
-
-    around(sent)
-
-
-def params(identity):
+
+def params(identity, grant):
     return pltpu.CompilerParams(
-        collective_id=identity, has_side_effects=True, vmem_limit_bytes=20 * 1024 * 1024
+        collective_id=identity, has_side_effects=True, vmem_limit_bytes=grant * 1024 * 1024
     )
 
 
@@ -661,7 +654,7 @@
         in_specs=[VMEM] * 3, out_specs=(VMEM,) * 2,
         scratch_shapes=pull_buffers() + [pltpu.VMEM((8, LANES), jnp.int32), pltpu.VMEM((3, 8, LANES), jnp.int32)]
         + copies_of(13),
-        compiler_params=params(1), name="open_halo",
+        compiler_params=params(1, 6), name="open_halo", cost_estimate=busy(10),
     )(cons, corners, counts)
 
 
@@ -672,7 +665,7 @@
         in_specs=[VMEM] * 6, out_specs=(VMEM,) * 2,
         scratch_shapes=[buffer(2, SPAN, OVER), buffer(2, 2, OVER, OVER), buffer(2, OVER, OVER)]
         + pull_buffers() + copies_of(16),
-        compiler_params=params(2), name="middle",
+        compiler_params=params(2, 10), name="middle", cost_estimate=busy(15),
     )(center, rr, rb, inv, cons, dual)
 
 
@@ -680,22 +673,23 @@
     scratch = [
         buffer(2, SPAN, OVER), buffer(2, 2, OVER, OVER), buffer(2, OVER, OVER),
         buffer(RUN, 3, 32, PS), buffer(RUN, 3, 32, PS), buffer(RUN, 3, 32, PS),
-        buffer(OWNERS, 3, 8, LANES), buffer(RING, 3, 8, LANES), buffer(2, RUN, OWNERS, 2, 8, LANES),
-        buffer(4, COLS, 2, 32, LANES), buffer(4, COLS, 2, 32, LANES), buffer(4, 2, 32, LANES),
-        buffer(4, 2, 32, LANES), buffer(4, COLS, 2, 32, LANES), pltpu.VMEM((2, TS, TS), jnp.float32),
+        buffer(RUN, 3, 8, PS), buffer(RUN, 3, 8, PS), buffer(3, 8, PS), buffer(LAPS, 3, 8, PS),
+        buffer(2, RUN, RUN, 2, 8, PS),
+        buffer(2, COLS, 2, 32, TS), buffer(2, COLS, 2, 32, TS), buffer(2, 2, 32, TS),
+        buffer(2, 2, 32, TS), buffer(2, COLS, 2, 32, TS), pltpu.VMEM((2, TS, TS), jnp.float32),
     ]
-    for count in ((3,), (1,), (RUN,), (RING,), (RING,), (RUN,), (1,), (4, COLS), (4,), (4, COLS)):
+    for count in ((3,), (1,), (RUN,), (RUN,), (LAPS,), (RUN,), (RUN,), (1,), (2, COLS), (2,), (2, COLS)):
         scratch += copies_of(*count)
     return pl.pallas_call(
         close_kernel, out_shape=(FIELD,) * 3, in_specs=[VMEM] * 9, out_specs=(VMEM,) * 3,
-        scratch_shapes=scratch, compiler_params=params(3), name="close",
+        scratch_shapes=scratch, compiler_params=params(3, 12), name="close", cost_estimate=busy(25),
     )(center, rr, rb, cons, dual, est, inv, psum, probe)
 
 
 def shards(consensus, duals, probes, amplitudes, offsets, counts):
     m1, m2 = (jnp.asarray(table) for table in transform_tables())
     cons, dual, probe = consensus[0], duals[0, 0], probes[0]
-    measured, corners = amplitudes[0, 0], offsets[0, 0]
+    measured, corners = amplitudes[0, 0], jnp.swapaxes(offsets[0, 0], 0, 1)
     wide, near = open_halo(cons, corners, counts)
     center, rr, rb, psum, inv = patches(True, corners, counts, wide, probe, measured, m1, m2, near=near)
     est, wide = middle(center, rr, rb, inv, cons, dual)

time: 107 us -> 100 us (0.935)
  local copies, waits for them, and re-layouts: 8.38 us -> 4.13 us
  Pallas kernels: 96.6 us -> 94.3 us
    pallas_call x1, Pallas kernels: 43.9 us -> 39.6 us  [close(): pl.pallas_call(close_kernel, out_shape=(FIELD,) * 3, in_specs=[VMEM] * 9,...]
    unnamed x25 -> x21, local copies, waits for them, and re-layouts: 7.62 us -> 4.13 us
    pallas_call x1, Pallas kernels: 24.4 us -> 26 us  [middle(): pl.pallas_call(middle_kernel, out_shape=(FIELD, WIDE), in_specs=[VMEM] *...]
where the time goes in v3:
time: 100 us; the launch traced here: 99.9 us
  Pallas kernels  94.3 us (94%)
  local copies, waits for them, and re-layouts  4.13 us (4%)
  between operations  1.41 us (1%)
    pallas_call x1, Pallas kernels, close(): pl.pallas_call(close_kernel, out_shape=(FIELD,) * 3, in_specs=[VMEM] * 9,...  39.6 us
    pallas_call x1, Pallas kernels, middle(): pl.pallas_call(middle_kernel, out_shape=(FIELD, WIDE), in_specs=[VMEM] *...  26 us
    pallas_call x1, Pallas kernels, open_halo(): pl.pallas_call(open_kernel, out_shape=(WIDE, jax.ShapeDtypeStruct((3, 8,...  23.1 us
    pallas_call x2, Pallas kernels, patches(): pl.pallas_call(functools.partial(patches_kernel, first), out_shape=tuple(...  5.61 us
    unnamed x21, local copies, waits for them, and re-layouts  4.13 us

profile of v3, /device:TPU:1, one launch (start us, length us, event | category | flops | bytes accessed | tf_op | source)
XLA Modules:
  0.0 99.9 jit_solution(17850381681773440891)
XLA Ops:
  1.3 0.0 copy-start.1
  1.3 1.0 %copy-done.1 = f32[1,2,256,256]{3,2,1,0:T(8,128)S(1)} copy-done((f32[1,2,256,256]{3,2,1,0:T(8,128)S(1)}, f32[1,2,256,256]{3,2,1,0:T(8,128)}, u32[]{:S(2)}) %copy-start.1) | copy-done | bytes 524312
  2.3 0.0 copy-start.5
  2.3 0.7 copy-done.5
  3.0 0.0 copy-start
  3.0 0.0 copy-start.3
  3.0 0.0 copy-start.8
  3.0 23.1 %open_halo.1 = (f32[2,3,384,128]{3,2,1,0:T(8,128)S(1)}, s32[3,8,128]{2,1,0:T(8,128)S(1)}) custom-call(f32[2,256,256]{2,1,0:T(8,128)S(1)} %bitcast.15, s32[2,4]{1,0:T(2,128)S(1)} %bitcast.23, s32[1,1]{1,0:T(1,128)S(6)} %copy.14.count_ref.refs_1_), custom_call_target="tpu_custom_call" | custom-call | flops 10000000000 | bytes 30000000 | tf_op jit(solution)/shard_map/open_halo/pallas_call | solution.py:652
  26.2 0.0 copy-done
  26.2 0.0 copy-done.3
  26.2 0.0 copy-done.6
  26.2 0.0 copy-done.7
  26.2 0.0 copy-done.8
  26.2 0.0 copy-start.2
  26.2 0.0 copy-start.4
  26.2 3.3 %patches.2 = (f32[2,256,256]{2,1,0:T(8,128)S(1)}, bf16[2,384,128]{2,1,0:T(8,128)(2,1)S(1)}, bf16[2,2,128,128]{3,2,1,0:T(8,128)(2,1)S(1)}, f32[3,256,256]{2,1,0:T(8,128)S(1)}, f32[256,256]{1,0:T(8,128)S(1)}) custom-call(s32[2,4]{1,0:T(2,128)S(1)} %bitcast.24, s32[1,1]{1,0:T(1,128)S(6)} %copy.14.count_ref.refs_1_, s32[3,8,128]{2,1,0:T(8,128)S(1)} %get-tuple-element.19.refs_2_, ...), custom_call_target="tpu_custom_call" | custom-call | flops 8000000000 | bytes 24000000 | tf_op jit(solution)/shard_map/patches/pallas_call | solution.py:193
  29.5 0.0 copy-done.2
  29.5 0.0 copy-done.4
  29.5 26.0 %middle.1 = (f32[2,256,256]{2,1,0:T(8,128)S(1)}, f32[2,3,384,128]{3,2,1,0:T(8,128)S(1)}) custom-call(f32[2,256,256]{2,1,0:T(8,128)S(1)} %get-tuple-element.21.center_ref, bf16[2,384,128]{2,1,0:T(8,128)(2,1)S(1)} %get-tuple-element.22.rr, bf16[2,2,128,128]{3,2,1,0:T(8,128)(2,1)S(1)} %get-tuple-element.23.rb, f32[256,256]{1,0:T(8,128)S(1)} %get-tuple-element.24.inv_ref, ...), custom_call_target="tpu_custom_call" | custom-call | flops 15000000512 | bytes 45000000 | tf_op jit(solution)/shard_map/middle/pallas_call | solution.py:662
  55.6 2.4 %patches.3 = (f32[2,256,256]{2,1,0:T(8,128)S(1)}, bf16[2,384,128]{2,1,0:T(8,128)(2,1)S(1)}, bf16[2,2,128,128]{3,2,1,0:T(8,128)(2,1)S(1)}, bf16[2,4,3,32,256]{4,3,2,1,0:T(8,128)(2,1)S(1)}) custom-call(s32[2,4]{1,0:T(2,128)S(1)} %bitcast.25, s32[1,1]{1,0:T(1,128)S(6)} %copy.14.count_ref.refs_1_, f32[2,3,384,128]{3,2,1,0:T(8,128)S(1)} %get-tuple-element.25.refs_2_, ...), custom_call_target="tpu_custom_call" | custom-call | flops 8000000000 | bytes 24000000 | tf_op jit(solution)/shard_map/patches/pallas_call | solution.py:193
  57.9 39.6 %close.1 = (f32[2,256,256]{2,1,0:T(8,128)S(1)}, f32[2,256,256]{2,1,0:T(8,128)S(1)}, f32[2,256,256]{2,1,0:T(8,128)S(1)}) custom-call(f32[2,256,256]{2,1,0:T(8,128)S(1)} %get-tuple-element.27.center_ref, bf16[2,384,128]{2,1,0:T(8,128)(2,1)S(1)} %get-tuple-element.28.rr, bf16[2,2,128,128]{3,2,1,0:T(8,128)(2,1)S(1)} %get-tuple-element.29.rb, ...), custom_call_target="tpu_custom_call" | custom-call | flops 24999999488 | bytes 75000000 | tf_op jit(solution)/shard_map/close/pallas_call | solution.py:683
  97.5 0.8 copy.15
  98.3 0.8 copy.16
  99.1 0.8 copy.17
  (2 shorter events, 0.0 us)
Async XLA Ops:
  1.3 1.0 %copy-start.1 = (f32[1,2,256,256]{3,2,1,0:T(8,128)S(1)}, f32[1,2,256,256]{3,2,1,0:T(8,128)}, u32[]{:S(2)}) copy-start(f32[1,2,256,256]{3,2,1,0:T(8,128)} %param.8) | copy-start | bytes 1572868
  2.3 0.7 copy-start.5
  3.0 23.2 %copy-start = (bf16[1,1,4,256,256]{4,3,2,1,0:T(8,128)(2,1)S(1)}, bf16[1,1,4,256,256]{4,3,2,1,0:T(8,128)(2,1)}, u32[]{:S(2)}) copy-start(bf16[1,1,4,256,256]{4,3,2,1,0:T(8,128)(2,1)} %param.11) | copy-start | bytes 1572868
  3.0 23.2 %copy-start.3 = (f32[1,2,256,256]{3,2,1,0:T(8,128)S(1)}, f32[1,2,256,256]{3,2,1,0:T(8,128)}, u32[]{:S(2)}) copy-start(f32[1,2,256,256]{3,2,1,0:T(8,128)} %param.10) | copy-start | bytes 1572868
  3.0 23.2 %copy-start.6 = (s32[1,1,4,2]{2,3,1,0:T(2,128)S(1)}, s32[1,1,4,2]{2,3,1,0:T(2,128)}, u32[]{:S(2)}) copy-start(s32[1,1,4,2]{2,3,1,0:T(2,128)} %param.12) | copy-start | bytes 100
  3.0 23.2 %copy-start.7 = (bf16[512,512]{1,0:T(8,128)(2,1)S(1)}, bf16[512,512]{1,0:T(8,128)(2,1)}, u32[]{:S(2)}) copy-start(bf16[512,512]{1,0:T(8,128)(2,1)} %constant.5.clone.refs_7_.refs_6_) | copy-start | bytes 1572868
  3.0 23.2 %copy-start.8 = (bf16[512,512]{1,0:T(8,128)(2,1)S(1)}, bf16[512,512]{1,0:T(8,128)(2,1)}, u32[]{:S(2)}) copy-start(bf16[512,512]{1,0:T(8,128)(2,1)} %constant.4.clone.refs_6_.refs_5_) | copy-start | bytes 1572868
  26.2 3.3 %copy-start.2 = (f32[1,2,256,256]{3,2,1,0:T(8,128)S(1)}, f32[1,2,256,256]{3,2,1,0:T(8,128)}, u32[]{:S(2)}) copy-start(f32[1,2,256,256]{3,2,1,0:T(8,128)} %param.8) | copy-start | bytes 1572868
  26.2 3.3 %copy-start.4 = (f32[1,1,2,256,256]{4,3,2,1,0:T(8,128)S(1)}, f32[1,1,2,256,256]{4,3,2,1,0:T(8,128)}, u32[]{:S(2)}) copy-start(f32[1,1,2,256,256]{4,3,2,1,0:T(8,128)} %param.9) | copy-start | bytes 1572868

commit v4 on v3

--- a/solution.py
+++ b/solution.py
@@ -73,7 +73,7 @@
     half = [pl.ds(0, LANES), pl.ds(LANES, LANES)]
     lane = lax.broadcasted_iota(jnp.int32, (PS, LANES), 1)
 
-    def visit(slot, carry):
+    def gather(slot, at):
         row = off_ref[0, slot]
         col = off_ref[1, slot]
         real = shifted_in([wide_ref[0, k, pl.ds(row, PS), :] for k in range(3)], col, lane)
@@ -82,30 +82,36 @@
             wr, wi = real[h], imag[h]
             pr = probe_ref[0, :, half[h]]
             pi = probe_ref[1, :, half[h]]
-            win_ref[0, :, half[h]] = wr
-            win_ref[1, :, half[h]] = wi
-            e_ref[:PS, half[h]] = (pr * wr - pi * wi).astype(jnp.bfloat16)
-            e_ref[PS:, half[h]] = (pr * wi + pi * wr).astype(jnp.bfloat16)
-        re = jnp.dot(m1_ref[:PS, :], e_ref[...], preferred_element_type=jnp.float32)
-        im = jnp.dot(m1_ref[PS:, :], e_ref[...], preferred_element_type=jnp.float32)
+            win_ref[at, 0, :, half[h]] = wr
+            win_ref[at, 1, :, half[h]] = wi
+            e_ref[at, :PS, half[h]] = (pr * wr - pi * wi).astype(jnp.bfloat16)
+            e_ref[at, PS:, half[h]] = (pr * wi + pi * wr).astype(jnp.bfloat16)
+
+    def transform(left_ref, right_ref, field_ref, at):
+        re = jnp.dot(left_ref[:PS, :], field_ref[at], preferred_element_type=jnp.float32)
+        im = jnp.dot(left_ref[PS:, :], field_ref[at], preferred_element_type=jnp.float32)
         inner = jnp.concatenate([re.astype(jnp.bfloat16), im.astype(jnp.bfloat16)], 1)
-        wave = jnp.dot(inner, m2_ref[...], preferred_element_type=jnp.float32)
+        return jnp.dot(inner, right_ref[...], preferred_element_type=jnp.float32)
+
+    def replace(slot, at):
+        wave = transform(m1_ref, m2_ref, e_ref, at)
         wr, wi = wave[:, :PS], wave[:, PS:]
         factor = amp_ref[slot].astype(jnp.float32) * lax.rsqrt(wr * wr + wi * wi + smoothing) - 1.0
-        r_ref[:PS, :] = (wr * factor).astype(jnp.bfloat16)
-        r_ref[PS:, :] = (wi * factor).astype(jnp.bfloat16)
-        re = jnp.dot(m2_ref[:PS, :], r_ref[...], preferred_element_type=jnp.float32)
-        im = jnp.dot(m2_ref[PS:, :], r_ref[...], preferred_element_type=jnp.float32)
-        inner = jnp.concatenate([re.astype(jnp.bfloat16), im.astype(jnp.bfloat16)], 1)
-        back = jnp.dot(inner, m1_ref[...], preferred_element_type=jnp.float32)
+        r_ref[at, :PS, :] = (wr * factor).astype(jnp.bfloat16)
+        r_ref[at, PS:, :] = (wi * factor).astype(jnp.bfloat16)
+
+    def scatter(slot, at):
+        row = off_ref[0, slot]
+        col = off_ref[1, slot]
+        back = transform(m2_ref, m1_ref, r_ref, at)
         terms = [[], []]
         for h in range(2):
             br = back[:, h * LANES:(h + 1) * LANES]
             bi = back[:, PS + h * LANES:PS + (h + 1) * LANES]
             pr = probe_ref[0, :, half[h]]
             pi = probe_ref[1, :, half[h]]
-            wr = win_ref[0, :, half[h]]
-            wi = win_ref[1, :, half[h]]
+            wr = win_ref[at, 0, :, half[h]]
+            wi = win_ref[at, 1, :, half[h]]
             terms[0].append(pr * br + pi * bi)
             terms[1].append(pr * bi - pi * br)
             acc_ref[0, :, half[h]] += wr * br + wi * bi
@@ -115,9 +121,19 @@
             out = shifted_out(terms[c][0], terms[c][1], col, lane)
             for k in range(3):
                 tot_ref[c, k, pl.ds(row, PS), :] += out[k]
-        return carry
-
-    lax.fori_loop(0, cnt_ref[0, 0], visit, 0)
+
+    def visit(slots):
+        for stage in (gather, replace, scatter):
+            for at, slot in enumerate(slots):
+                stage(slot, at)
+
+    count = cnt_ref[0, 0]
+
+    for full in range(1, SLOTS + 1):
+        @pl.when(count == full)
+        def _(full=full):
+            visit(list(range(full)))
+
     for k in range(2):
         center_ref[:, :, half[k]] = tot_ref[:, k, :TS, :]
         rb_ref[k] = tot_ref[:, k, TS:, :].astype(jnp.bfloat16)
@@ -126,13 +142,15 @@
         weight_ref[...] = jnp.zeros_like(weight_ref)
         power_ref[...] = probe_ref[0] * probe_ref[0] + probe_ref[1] * probe_ref[1]
 
-        def weigh(at, col, aside):
-            out = shifted_out(power_ref[:, half[0]], power_ref[:, half[1]], col, lane)
+        def weigh(at, col, aside, skip=0):
+            rows = pl.ds(skip, PS - skip)
+            out = shifted_out(power_ref[rows, half[0]], power_ref[rows, half[1]], col, lane[skip:])
+            at = pl.ds(at + skip, PS - skip)
             if aside:
-                weight_ref[0, pl.ds(at, PS), :] += out[2]
+                weight_ref[0, at, :] += out[2]
             else:
-                weight_ref[0, pl.ds(at, PS), :] += out[0]
-                weight_ref[1, pl.ds(at, PS), :] += out[1]
+                weight_ref[0, at, :] += out[0]
+                weight_ref[1, at, :] += out[1]
 
         def own(slot, carry):
             weigh(off_ref[0, slot] + TS, off_ref[1, slot], False)
@@ -143,11 +161,11 @@
             return carry
 
         def above(slot, carry):
-            weigh(near_ref[1, 0, slot], near_ref[1, 1, slot], False)
+            weigh(near_ref[1, 0, slot], near_ref[1, 1, slot], False, OVER)
             return carry
 
         def corner(slot, carry):
-            weigh(near_ref[2, 0, slot], near_ref[2, 1, slot], True)
+            weigh(near_ref[2, 0, slot], near_ref[2, 1, slot], True, OVER)
             return carry
 
         lax.fori_loop(0, cnt_ref[0, 0], own, 0)
@@ -176,9 +194,9 @@
     ]
     scratch = [
         pltpu.VMEM((2, 3, SPAN, LANES), jnp.float32),
-        pltpu.VMEM((2 * PS, PS), jnp.bfloat16),
-        pltpu.VMEM((2 * PS, PS), jnp.bfloat16),
-        pltpu.VMEM((2, PS, PS), jnp.float32),
+        pltpu.VMEM((4, 2 * PS, PS), jnp.bfloat16),
+        pltpu.VMEM((4, 2 * PS, PS), jnp.bfloat16),
+        pltpu.VMEM((4, 2, PS, PS), jnp.float32),
     ]
     if first:
         args = [corners, count, near, wide, probe, measured, m1, m2]
@@ -212,11 +230,14 @@
     )
 
 
-def greet(targets):
-    barrier = pltpu.get_barrier_semaphore()
+def hail(targets):
     for target in targets:
-        pl.semaphore_signal(barrier, inc=1, device_id=target, device_id_type=MESH)
-    pl.semaphore_wait(barrier, len(targets))
+        pl.semaphore_signal(pltpu.get_barrier_semaphore(), inc=1, device_id=target, device_id_type=MESH)
+    return len(targets)
+
+
+def meet(count):
+    pl.semaphore_wait(pltpu.get_barrier_semaphore(), count)
 
 
 def start_if(flag, *copies):
@@ -308,22 +329,30 @@
 def open_kernel(cons_ref, corner_ref, count_ref, wide_ref, near_ref,
                 quads, below_in, right_in, corner_in, note, note_in, sends, recvs):
     t = lax.axis_index("tile")
+    hailed = hail([{"tile": moved(t, by)} for by in (1, TGW, TGW + 1, -1, -TGW, -TGW - 1)])
     pull = Pull(t, quads, below_in, right_in, corner_in, sends, recvs, 0)
-    greet([{"tile": moved(t, by)} for by in (1, TGW, TGW + 1, -1, -TGW, -TGW - 1)])
-    note[...] = jnp.zeros_like(note)
-    note[0:2, 0:SLOTS] = corner_ref[...]
-    note[2:3, 0:1] = count_ref[...]
+    pull.clear()
+    line = lax.broadcasted_iota(jnp.int32, note.shape, 0)
+    lane = lax.broadcasted_iota(jnp.int32, note.shape, 1)
+    filled = jnp.where(jnp.logical_and(line == 2, lane == 0), count_ref[0, 0], 0)
+    for axis in range(2):
+        for slot in range(SLOTS):
+            filled = jnp.where(jnp.logical_and(line == axis, lane == slot), corner_ref[axis, slot], filled)
+    note[...] = filled
     notes = [
         remote(note, note_in.at[k], sends, recvs, 10 + k, 10 + k, {"tile": moved(t, by)})
         for k, by in enumerate((1, TGW, TGW + 1))
     ]
-    for a, b in ((0, 0), (0, 1), (1, 0), (1, 1)):
+    quarters = ((0, 0), (0, 1), (1, 0), (1, 1))
+    for a, b in quarters:
         for c in range(2):
             pull.offer(cons_ref[c, block(a), block(b)], c, a, b, wide_ref)
+    meet(hailed)
+    for a, b in quarters:
+        for c in range(2):
             pull.begin(c, a, b)
     for copy in notes:
         copy.start()
-    pull.clear()
     pull.finish(wide_ref)
     for copy in notes:
         copy.wait()
@@ -335,6 +364,7 @@
                   left_in, above_in, lowered, quads, below_in, right_in, corner_in, sends, recvs):
     t = lax.axis_index("tile")
     left, right, above, below = sides(t)
+    hailed = hail([{"tile": moved(t, by)} for by in (1, TGW, TGW + 1, -1, -TGW)])
     pull = Pull(t, quads, below_in, right_in, corner_in, sends, recvs, 6)
     pull.clear()
     clear_if(jnp.logical_not(left), left_in)
@@ -344,7 +374,6 @@
     push_on = [make(rr.at[c], left_in.at[c], c, on) for c in range(2)]
     push_far = [make(rb.at[1, c], above_in.at[1, c], 2 + c, down) for c in range(2)]
     push_low = [make(lowered.at[c], above_in.at[0, c], 4 + c, down) for c in range(2)]
-    greet([{"tile": moved(t, by)} for by in (1, TGW, TGW + 1, -1, -TGW)])
 
     def push(c):
         start_if(right, push_on[c])
@@ -367,13 +396,14 @@
         pull.offer(value, c, a, b, wide_ref)
         pull.begin(c, a, b)
 
+    update(0, 1, 1)
+    update(1, 1, 1)
+    meet(hailed)
     push(0)
-    update(0, 1, 1)
     relay(0)
     push(1)
     for c in range(2):
         if c == 1:
-            update(1, 1, 1)
             relay(1)
         update(c, 1, 0)
         wait_if(above, push_far[c])
@@ -386,10 +416,10 @@
         sent_if(below, push_far[c], push_low[c])
 
 
-def close_kernel(center_ref, rr, rb, cons_ref, dual_ref, est_ref, inv_ref, psum, probe_ref,
-                 cons_out, dual_out, probe_out,
+def close_kernel(center_ref, rr, rb, cons_ref, dual_ref, est_ref, inv_ref, psum,
+                 settled_out, kept, grown_out,
                  left_in, above_in, lowered, half_in, half, run_in, ring_out, ring_in, tri_out, tri_in, grown,
-                 mine, cols_in, part, part_in, settled, kept,
+                 mine, cols_in, part, part_in, settled,
                  rim_s, rim_r, half_s, half_r, run_s, run_r, ring_s, ring_r, tri_s, tri_r, grow_s, grow_r,
                  wide_s, wide_r, back_s, back_r, col_s, col_r, pair_s, pair_r, out_s, out_r):
     t = lax.axis_index("tile")
@@ -417,15 +447,11 @@
     push_low = remote(lowered, above_in.at[0], rim_s, rim_r, 2, 2, down)
     to_half = remote(psum.at[1 - core], half_in, half_s, half_r, 0, 0, sibling)
 
+    hailed = hail([{"tile": moved(t, by)} for by in (-1, -TGW)] + [sibling, twin]
+                  + [tile_at(k, z, core) for k in ys] + [scan_at(k, yh) for k in xs]
+                  + [at_seat(k) for k in seats] + [at_lap(k) for k in laps])
     clear_if(jnp.logical_not(left), left_in)
     clear_if(jnp.logical_not(above), above_in)
-    greet([{"tile": moved(t, by)} for by in (-1, -TGW)] + [sibling, twin]
-          + [tile_at(k, z, core) for k in ys] + [scan_at(k, yh) for k in xs]
-          + [at_seat(k) for k in seats] + [at_lap(k) for k in laps])
-
-    start_if(right, push_on)
-    start_if(below, push_far)
-    to_half.start()
 
     def cross(n, k, at, other):
         return remote(mine.at[n, k], cols_in.at[n, at], col_s, col_r, (n, k), (n, at), scan_at(other, yh))
@@ -482,12 +508,7 @@
     def give(n):
         for k in xs:
             spread(n, k, k, k).wait_recv()
-        for q in range(COLS):
-            rows = pl.ds(n * OVER + q * 32, 32)
-            for c in range(2):
-                value = settled[n, q, c].astype(jnp.float32)
-                cons_out[c, rows, :] = value
-                dual_out[c, rows, :] = kept[c, rows, :] - value
+        settled_out[n] = settled[n]
 
     def run_copy(k, at):
         return remote(half.at[k], run_in.at[at], run_s, run_r, k, at, tile_at(k, z, core))
@@ -512,10 +533,10 @@
 
     def probe_run():
         to_half.wait_recv()
-        for q in range(RUN):
-            half[q] = (psum[core, q].astype(jnp.float32) + half_in[q].astype(jnp.float32)).astype(jnp.bfloat16)
-        for k in ys:
-            run_copy(k, y).start()
+        for k in ys + [y]:
+            half[k] = (psum[core, k].astype(jnp.float32) + half_in[k].astype(jnp.float32)).astype(jnp.bfloat16)
+            if k is not y:
+                run_copy(k, y).start()
 
     def probe_ring():
         for k in ys:
@@ -572,14 +593,13 @@
 
     def probe_give():
         back_copy(1 - core).wait_recv()
-        for part_at in range(8):
-            for k in range(RUN):
-                rows = pl.ds(part_at * 32 + k * 8, 8)
-                for c in range(2):
-                    step = grown[part_at // 4, part_at % 4, k, c].astype(jnp.float32)
-                    probe_out[c, rows, :] = probe_ref[c, rows, :] + step
+        grown_out[...] = grown[...]
 
     update(1, 1)
+    meet(hailed)
+    to_half.start()
+    start_if(right, push_on)
+    start_if(below, push_far)
     probe_run()
     wait_if(left, push_on)
     for c in range(2):
@@ -598,8 +618,8 @@
     combine(0)
     settle(1)
     probe_grow()
+    probe_wide()
     settle(0)
-    probe_wide()
     give(1)
     probe_back()
     give(0)
@@ -651,7 +671,7 @@
 def open_halo(cons, corners, counts):
     return pl.pallas_call(
         open_kernel, out_shape=(WIDE, jax.ShapeDtypeStruct((3, 8, LANES), jnp.int32)),
-        in_specs=[VMEM] * 3, out_specs=(VMEM,) * 2,
+        in_specs=[VMEM, SMEM, SMEM], out_specs=(VMEM,) * 2,
         scratch_shapes=pull_buffers() + [pltpu.VMEM((8, LANES), jnp.int32), pltpu.VMEM((3, 8, LANES), jnp.int32)]
         + copies_of(13),
         compiler_params=params(1, 6), name="open_halo", cost_estimate=busy(10),
@@ -669,21 +689,50 @@
     )(center, rr, rb, inv, cons, dual)
 
 
-def close(center, rr, rb, cons, dual, est, inv, psum, probe):
+def close(center, rr, rb, cons, dual, est, inv, psum):
     scratch = [
         buffer(2, SPAN, OVER), buffer(2, 2, OVER, OVER), buffer(2, OVER, OVER),
         buffer(RUN, 3, 32, PS), buffer(RUN, 3, 32, PS), buffer(RUN, 3, 32, PS),
         buffer(RUN, 3, 8, PS), buffer(RUN, 3, 8, PS), buffer(3, 8, PS), buffer(LAPS, 3, 8, PS),
         buffer(2, RUN, RUN, 2, 8, PS),
         buffer(2, COLS, 2, 32, TS), buffer(2, COLS, 2, 32, TS), buffer(2, 2, 32, TS),
-        buffer(2, 2, 32, TS), buffer(2, COLS, 2, 32, TS), pltpu.VMEM((2, TS, TS), jnp.float32),
+        buffer(2, 2, 32, TS), buffer(2, COLS, 2, 32, TS),
     ]
     for count in ((3,), (1,), (RUN,), (RUN,), (LAPS,), (RUN,), (RUN,), (1,), (2, COLS), (2,), (2, COLS)):
         scratch += copies_of(*count)
     return pl.pallas_call(
-        close_kernel, out_shape=(FIELD,) * 3, in_specs=[VMEM] * 9, out_specs=(VMEM,) * 3,
+        close_kernel,
+        out_shape=(
+            jax.ShapeDtypeStruct((2, COLS, 2, 32, TS), jnp.bfloat16), FIELD,
+            jax.ShapeDtypeStruct((2, RUN, RUN, 2, 8, PS), jnp.bfloat16),
+        ),
+        in_specs=[VMEM] * 8, out_specs=(VMEM,) * 3,
         scratch_shapes=scratch, compiler_params=params(3, 12), name="close", cost_estimate=busy(25),
-    )(center, rr, rb, cons, dual, est, inv, psum, probe)
+    )(center, rr, rb, cons, dual, est, inv, psum)
+
+
+def finish_kernel(settled, kept, grown, probe_ref, cons_out, dual_out, probe_out):
+    for n in range(2):
+        for q in range(COLS):
+            rows = pl.ds(n * OVER + q * 32, 32)
+            for c in range(2):
+                value = settled[n, q, c].astype(jnp.float32)
+                cons_out[c, rows, :] = value
+                dual_out[c, rows, :] = kept[c, rows, :] - value
+    for part_at in range(8):
+        for k in range(RUN):
+            rows = pl.ds(part_at * 32 + k * 8, 8)
+            for c in range(2):
+                step = grown[part_at // 4, part_at % 4, k, c].astype(jnp.float32)
+                probe_out[c, rows, :] = probe_ref[c, rows, :] + step
+
+
+def finish(settled, kept, grown, probe):
+    return pl.pallas_call(
+        finish_kernel, out_shape=(FIELD,) * 3, in_specs=[VMEM] * 4, out_specs=(VMEM,) * 3,
+        compiler_params=pltpu.CompilerParams(vmem_limit_bytes=8 * 1024 * 1024),
+        name="finish", cost_estimate=busy(1),
+    )(settled, kept, grown, probe)
 
 
 def shards(consensus, duals, probes, amplitudes, offsets, counts):
@@ -694,7 +743,8 @@
     center, rr, rb, psum, inv = patches(True, corners, counts, wide, probe, measured, m1, m2, near=near)
     est, wide = middle(center, rr, rb, inv, cons, dual)
     center, rr, rb, psum = patches(False, corners, counts, wide, probe, measured, m1, m2, prev=psum)
-    cons_new, dual_new, probe_new = close(center, rr, rb, cons, dual, est, inv, psum, probe)
+    settled, kept, grown = close(center, rr, rb, cons, dual, est, inv, psum)
+    cons_new, dual_new, probe_new = finish(settled, kept, grown, probe)
     return cons_new[None], dual_new[None, None], probe_new[None]
 
 

time: 100 us -> 94.6 us (0.946)
  Pallas kernels: 94.3 us -> 91.2 us
  local copies, waits for them, and re-layouts: 4.13 us -> 1.75 us
    pallas_call x1, Pallas kernels: 26 us -> 20.3 us  [middle(): pl.pallas_call(middle_kernel, out_shape=(FIELD, WIDE), in_specs=[VMEM] *...]
    pallas_call x2, Pallas kernels: 5.61 us -> 11 us  [patches(): pl.pallas_call(functools.partial(patches_kernel, first), out_shape=tuple(...]
    pallas_call x1 -> x2, Pallas kernels: 39.6 us -> 36.2 us  [the longest x1 35 us: close(): pl.pallas_call(close_kernel, out_shape=(jax.ShapeDtypeStruct((2, COLS, 2,...]
    unnamed x21 -> x18, local copies, waits for them, and re-layouts: 4.13 us -> 1.75 us
where the time goes in v4:
time: 94.6 us; the launch traced here: 94.4 us
  Pallas kernels  91.2 us (96%)
  local copies, waits for them, and re-layouts  1.75 us (2%)
  between operations  1.41 us (1%)
    pallas_call x1, Pallas kernels, close(): pl.pallas_call(close_kernel, out_shape=(jax.ShapeDtypeStruct((2, COLS, 2,...  35 us
    pallas_call x1, Pallas kernels, open_halo(): pl.pallas_call(open_kernel, out_shape=(WIDE, jax.ShapeDtypeStruct((3, 8,...  23.7 us
    pallas_call x1, Pallas kernels, middle(): pl.pallas_call(middle_kernel, out_shape=(FIELD, WIDE), in_specs=[VMEM] *...  20.3 us
    pallas_call x2, Pallas kernels, patches(): pl.pallas_call(functools.partial(patches_kernel, first), out_shape=tuple(...  11 us

profile of v4, /device:TPU:1, one launch (start us, length us, event | category | flops | bytes accessed | tf_op | source)
XLA Modules:
  0.0 94.4 jit_solution(8501523332724115091)
XLA Ops:
  1.3 0.0 copy-start.1
  1.3 1.0 %copy-done.1 = f32[1,2,256,256]{3,2,1,0:T(8,128)S(1)} copy-done((f32[1,2,256,256]{3,2,1,0:T(8,128)S(1)}, f32[1,2,256,256]{3,2,1,0:T(8,128)}, u32[]{:S(2)}) %copy-start.1) | copy-done | bytes 524312
  2.3 0.0 copy-start.5
  2.3 0.7 copy-done.5
  3.0 0.0 copy-start
  3.0 0.0 copy-start.4
  3.0 0.0 copy-start.6
  3.0 0.0 copy-start.7
  3.0 0.0 copy-start.8
  3.0 23.7 %open_halo.1 = (f32[2,3,384,128]{3,2,1,0:T(8,128)S(1)}, s32[3,8,128]{2,1,0:T(8,128)S(1)}) custom-call(f32[2,256,256]{2,1,0:T(8,128)S(1)} %bitcast.12, s32[2,4]{1,0:T(2,128)S(1)} %bitcast.20, s32[1,1]{1,0:T(1,128)S(6)} %copy.11.count_ref.refs_1_), custom_call_target="tpu_custom_call" | custom-call | flops 10000000000 | bytes 30000000 | tf_op jit(solution)/shard_map/open_halo/pallas_call | solution.py:672
  26.7 0.0 copy-done
  26.7 0.0 copy-done.4
  26.7 0.0 copy-done.6
  26.7 0.0 copy-done.7
  26.7 0.0 copy-done.8
  26.7 0.0 copy-start.2
  26.8 0.0 copy-start.3
  26.8 6.1 %patches.2 = (f32[2,256,256]{2,1,0:T(8,128)S(1)}, bf16[2,384,128]{2,1,0:T(8,128)(2,1)S(1)}, bf16[2,2,128,128]{3,2,1,0:T(8,128)(2,1)S(1)}, f32[3,256,256]{2,1,0:T(8,128)S(1)}, f32[256,256]{1,0:T(8,128)S(1)}) custom-call(s32[2,4]{1,0:T(2,128)S(1)} %bitcast.21, s32[1,1]{1,0:T(1,128)S(6)} %copy.11.count_ref.refs_1_, s32[3,8,128]{2,1,0:T(8,128)S(1)} %get-tuple-element.22.refs_2_, ...), custom_call_target="tpu_custom_call" | custom-call | flops 8000000000 | bytes 24000000 | tf_op jit(solution)/shard_map/patches/pallas_call | solution.py:211
  32.9 0.0 copy-done.2
  32.9 0.0 copy-done.3
  32.9 20.3 %middle.1 = (f32[2,256,256]{2,1,0:T(8,128)S(1)}, f32[2,3,384,128]{3,2,1,0:T(8,128)S(1)}) custom-call(f32[2,256,256]{2,1,0:T(8,128)S(1)} %get-tuple-element.24.center_ref, bf16[2,384,128]{2,1,0:T(8,128)(2,1)S(1)} %get-tuple-element.25.rr, bf16[2,2,128,128]{3,2,1,0:T(8,128)(2,1)S(1)} %get-tuple-element.26.rb, f32[256,256]{1,0:T(8,128)S(1)} %get-tuple-element.27.inv_ref, ...), custom_call_target="tpu_custom_call" | custom-call | flops 15000000512 | bytes 45000000 | tf_op jit(solution)/shard_map/middle/pallas_call | solution.py:682
  53.2 4.9 %patches.3 = (f32[2,256,256]{2,1,0:T(8,128)S(1)}, bf16[2,384,128]{2,1,0:T(8,128)(2,1)S(1)}, bf16[2,2,128,128]{3,2,1,0:T(8,128)(2,1)S(1)}, bf16[2,4,3,32,256]{4,3,2,1,0:T(8,128)(2,1)S(1)}) custom-call(s32[2,4]{1,0:T(2,128)S(1)} %bitcast.22, s32[1,1]{1,0:T(1,128)S(6)} %copy.11.count_ref.refs_1_, f32[2,3,384,128]{3,2,1,0:T(8,128)S(1)} %get-tuple-element.28.refs_2_, ...), custom_call_target="tpu_custom_call" | custom-call | flops 8000000000 | bytes 24000000 | tf_op jit(solution)/shard_map/patches/pallas_call | solution.py:211
  58.2 35.0 %close.1 = (bf16[2,4,2,32,256]{4,3,2,1,0:T(8,128)(2,1)S(1)}, f32[2,256,256]{2,1,0:T(8,128)S(1)}, bf16[2,4,4,2,8,256]{5,4,3,2,1,0:T(8,128)(2,1)S(1)}) custom-call(f32[2,256,256]{2,1,0:T(8,128)S(1)} %get-tuple-element.30.center_ref, bf16[2,384,128]{2,1,0:T(8,128)(2,1)S(1)} %get-tuple-element.31.rr, bf16[2,2,128,128]{3,2,1,0:T(8,128)(2,1)S(1)} %get-tuple-element.32.rb, ...), custom_call_target="tpu_custom_call" | custom-call | flops 24999999488 | bytes 75000000 | tf_op jit(solution)/shard_map/close/pallas_call | solution.py:703
  93.1 1.3 %finish.1 = (f32[2,256,256]{2,1,0:T(8,128)}, f32[2,256,256]{2,1,0:T(8,128)}, f32[2,256,256]{2,1,0:T(8,128)}) custom-call(bf16[2,4,2,32,256]{4,3,2,1,0:T(8,128)(2,1)S(1)} %get-tuple-element.35.settled, f32[2,256,256]{2,1,0:T(8,128)S(1)} %get-tuple-element.36.kept, bf16[2,4,4,2,8,256]{5,4,3,2,1,0:T(8,128)(2,1)S(1)} %get-tuple-element.37.grown, ...), custom_call_target="tpu_custom_call" | custom-call | flops 1000000000 | bytes 3000000 | tf_op jit(solution)/shard_map/finish/pallas_call | solution.py:731
Async XLA Ops:
  1.3 1.0 %copy-start.1 = (f32[1,2,256,256]{3,2,1,0:T(8,128)S(1)}, f32[1,2,256,256]{3,2,1,0:T(8,128)}, u32[]{:S(2)}) copy-start(f32[1,2,256,256]{3,2,1,0:T(8,128)} %param.8) | copy-start | bytes 1572868
  2.3 0.7 copy-start.5
  3.0 23.7 %copy-start = (bf16[1,1,4,256,256]{4,3,2,1,0:T(8,128)(2,1)S(1)}, bf16[1,1,4,256,256]{4,3,2,1,0:T(8,128)(2,1)}, u32[]{:S(2)}) copy-start(bf16[1,1,4,256,256]{4,3,2,1,0:T(8,128)(2,1)} %param.11) | copy-start | bytes 1572868
  3.0 23.7 %copy-start.4 = (f32[1,2,256,256]{3,2,1,0:T(8,128)S(1)}, f32[1,2,256,256]{3,2,1,0:T(8,128)}, u32[]{:S(2)}) copy-start(f32[1,2,256,256]{3,2,1,0:T(8,128)} %param.10) | copy-start | bytes 1572868
  3.0 23.7 %copy-start.6 = (s32[1,1,4,2]{2,3,1,0:T(2,128)S(1)}, s32[1,1,4,2]{2,3,1,0:T(2,128)}, u32[]{:S(2)}) copy-start(s32[1,1,4,2]{2,3,1,0:T(2,128)} %param.12) | copy-start | bytes 100
  3.0 23.7 %copy-start.7 = (bf16[512,512]{1,0:T(8,128)(2,1)S(1)}, bf16[512,512]{1,0:T(8,128)(2,1)}, u32[]{:S(2)}) copy-start(bf16[512,512]{1,0:T(8,128)(2,1)} %constant.5.clone.refs_7_.refs_6_) | copy-start | bytes 1572868
  3.0 23.7 %copy-start.8 = (bf16[512,512]{1,0:T(8,128)(2,1)S(1)}, bf16[512,512]{1,0:T(8,128)(2,1)}, u32[]{:S(2)}) copy-start(bf16[512,512]{1,0:T(8,128)(2,1)} %constant.4.clone.refs_6_.refs_5_) | copy-start | bytes 1572868
  26.7 6.1 %copy-start.2 = (f32[1,2,256,256]{3,2,1,0:T(8,128)S(1)}, f32[1,2,256,256]{3,2,1,0:T(8,128)}, u32[]{:S(2)}) copy-start(f32[1,2,256,256]{3,2,1,0:T(8,128)} %param.8) | copy-start | bytes 1572868
  26.8 6.1 %copy-start.3 = (f32[1,1,2,256,256]{4,3,2,1,0:T(8,128)S(1)}, f32[1,1,2,256,256]{4,3,2,1,0:T(8,128)}, u32[]{:S(2)}) copy-start(f32[1,1,2,256,256]{4,3,2,1,0:T(8,128)} %param.9) | copy-start | bytes 1572868

commit v5 on v4

--- a/solution.py
+++ b/solution.py
@@ -280,20 +280,17 @@
 class Pull:
     def __init__(self, t, quads, below_in, right_in, corner_in, sends, recvs, base):
         self.left, self.right, self.above, self.below = sides(t)
-        self.gives = jnp.logical_and(self.left, self.above)
-        self.takes = jnp.logical_and(self.right, self.below)
         self.refs = quads, below_in, right_in, corner_in
-        up, back, far = ({"tile": moved(t, by)} for by in (-TGW, -1, -TGW - 1))
+        up, back = {"tile": moved(t, -TGW)}, {"tile": moved(t, -1)}
         make = lambda src, dst, at, to: remote(src, dst, sends, recvs, at, at, to)
         self.up = [[make(quads.at[b, c], below_in.at[b, c], base + 2 * b + c, up) for c in range(2)] for b in range(2)]
         self.side = [[make(quads.at[2 * a, c], right_in.at[a, c], base + 4 + 2 * a + c, back) for c in range(2)] for a in range(2)]
-        self.corner = [make(quads.at[0, c], corner_in.at[c], base + 8 + c, far) for c in range(2)]
+        self.relay = [make(below_in.at[0, c], corner_in.at[c], base + 8 + c, back) for c in range(2)]
 
     def clear(self):
         quads, below_in, right_in, corner_in = self.refs
-        clear_if(jnp.logical_not(self.right), right_in)
+        clear_if(jnp.logical_not(self.right), right_in, corner_in)
         clear_if(jnp.logical_not(self.below), below_in)
-        clear_if(jnp.logical_not(self.takes), corner_in)
 
     def offer(self, value, c, a, b, wide_ref):
         rounded = value.astype(jnp.bfloat16)
@@ -302,8 +299,6 @@
             self.refs[0][2 * a + b, c] = rounded
 
     def begin(self, c, a, b):
-        if a == 0 and b == 0:
-            start_if(self.gives, self.corner[c])
         if a == 0:
             start_if(self.above, self.up[b][c])
         if b == 0:
@@ -312,24 +307,27 @@
     def finish(self, wide_ref):
         quads, below_in, right_in, corner_in = self.refs
         for c in range(2):
+            wait_if(self.below, self.up[0][c])
+            start_if(self.left, self.relay[c])
+        for c in range(2):
             wait_if(self.right, self.side[0][c], self.side[1][c])
             for a in range(2):
                 wide_ref[c, 2, block(a), :] = right_in[a, c].astype(jnp.float32)
-            wait_if(self.below, self.up[0][c], self.up[1][c])
+            wait_if(self.below, self.up[1][c])
             for b in range(2):
                 wide_ref[c, b, TS:, :] = below_in[b, c].astype(jnp.float32)
-            wait_if(self.takes, self.corner[c])
+        for c in range(2):
+            wait_if(self.right, self.relay[c])
             wide_ref[c, 2, TS:, :] = corner_in[c].astype(jnp.float32)
         for c in range(2):
             sent_if(self.above, self.up[0][c], self.up[1][c])
-            sent_if(self.left, self.side[0][c], self.side[1][c])
-            sent_if(self.gives, self.corner[c])
+            sent_if(self.left, self.side[0][c], self.side[1][c], self.relay[c])
 
 
 def open_kernel(cons_ref, corner_ref, count_ref, wide_ref, near_ref,
                 quads, below_in, right_in, corner_in, note, note_in, sends, recvs):
     t = lax.axis_index("tile")
-    hailed = hail([{"tile": moved(t, by)} for by in (1, TGW, TGW + 1, -1, -TGW, -TGW - 1)])
+    hailed = hail([{"tile": moved(t, by)} for by in (1, TGW, -1, -TGW, -TGW - 1)])
     pull = Pull(t, quads, below_in, right_in, corner_in, sends, recvs, 0)
     pull.clear()
     line = lax.broadcasted_iota(jnp.int32, note.shape, 0)
@@ -348,15 +346,14 @@
         for c in range(2):
             pull.offer(cons_ref[c, block(a), block(b)], c, a, b, wide_ref)
     meet(hailed)
-    for a, b in quarters:
-        for c in range(2):
-            pull.begin(c, a, b)
+    start_if(pull.above, *pull.up[0], *pull.up[1])
+    start_if(pull.left, *pull.side[0], *pull.side[1])
     for copy in notes:
         copy.start()
     pull.finish(wide_ref)
     for copy in notes:
         copy.wait()
-    for k, flag in enumerate((pull.left, pull.above, pull.gives)):
+    for k, flag in enumerate((pull.left, pull.above, jnp.logical_and(pull.left, pull.above))):
         near_ref[k] = note_in[k] * jnp.where(flag, 1, 0)
 
 
@@ -364,7 +361,7 @@
                   left_in, above_in, lowered, quads, below_in, right_in, corner_in, sends, recvs):
     t = lax.axis_index("tile")
     left, right, above, below = sides(t)
-    hailed = hail([{"tile": moved(t, by)} for by in (1, TGW, TGW + 1, -1, -TGW)])
+    hailed = hail([{"tile": moved(t, by)} for by in (1, TGW, -1, -TGW)])
     pull = Pull(t, quads, below_in, right_in, corner_in, sends, recvs, 6)
     pull.clear()
     clear_if(jnp.logical_not(left), left_in)

time: 94.6 us -> 93.5 us (0.988)
  Pallas kernels: 91.2 us -> 90.1 us
    pallas_call x2, Pallas kernels: 11 us -> 5.82 us  [patches(): pl.pallas_call(functools.partial(patches_kernel, first), out_shape=tuple(...]
    pallas_call x1, Pallas kernels: 20.3 us -> 25.2 us  [middle(): pl.pallas_call(middle_kernel, out_shape=(FIELD, WIDE), in_specs=[VMEM] *...]
where the time goes in v5:
time: 93.5 us; the launch traced here: 93.3 us
  Pallas kernels  90.1 us (96%)
  local copies, waits for them, and re-layouts  1.75 us (2%)
  between operations  1.41 us (2%)
    pallas_call x1, Pallas kernels, close(): pl.pallas_call(close_kernel, out_shape=(jax.ShapeDtypeStruct((2, COLS, 2,...  34.5 us
    pallas_call x1, Pallas kernels, middle(): pl.pallas_call(middle_kernel, out_shape=(FIELD, WIDE), in_specs=[VMEM] *...  25.2 us
    pallas_call x1, Pallas kernels, open_halo(): pl.pallas_call(open_kernel, out_shape=(WIDE, jax.ShapeDtypeStruct((3, 8,...  23.3 us
    pallas_call x2, Pallas kernels, patches(): pl.pallas_call(functools.partial(patches_kernel, first), out_shape=tuple(...  5.82 us

profile of v5, /device:TPU:1, one launch (start us, length us, event | category | flops | bytes accessed | tf_op | source)
XLA Modules:
  0.0 93.3 jit_solution(9379645746064397229)
XLA Ops:
  1.3 0.0 copy-start.1
  1.3 1.0 %copy-done.1 = f32[1,2,256,256]{3,2,1,0:T(8,128)S(1)} copy-done((f32[1,2,256,256]{3,2,1,0:T(8,128)S(1)}, f32[1,2,256,256]{3,2,1,0:T(8,128)}, u32[]{:S(2)}) %copy-start.1) | copy-done | bytes 524312
  2.3 0.0 copy-start.5
  2.3 0.7 copy-done.5
  3.0 0.0 copy-start
  3.0 0.0 copy-start.4
  3.0 0.0 copy-start.6
  3.0 0.0 copy-start.7
  3.0 0.0 copy-start.8
  3.0 23.3 %open_halo.1 = (f32[2,3,384,128]{3,2,1,0:T(8,128)S(1)}, s32[3,8,128]{2,1,0:T(8,128)S(1)}) custom-call(f32[2,256,256]{2,1,0:T(8,128)S(1)} %bitcast.12, s32[2,4]{1,0:T(2,128)S(1)} %bitcast.20, s32[1,1]{1,0:T(1,128)S(6)} %copy.11.count_ref.refs_1_), custom_call_target="tpu_custom_call" | custom-call | flops 10000000000 | bytes 30000000 | tf_op jit(solution)/shard_map/open_halo/pallas_call | solution.py:669
  26.4 0.0 copy-done
  26.4 0.0 copy-done.4
  26.4 0.0 copy-done.6
  26.4 0.0 copy-done.7
  26.4 0.0 copy-done.8
  26.4 0.0 copy-start.2
  26.4 0.0 copy-start.3
  26.4 3.3 %patches.2 = (f32[2,256,256]{2,1,0:T(8,128)S(1)}, bf16[2,384,128]{2,1,0:T(8,128)(2,1)S(1)}, bf16[2,2,128,128]{3,2,1,0:T(8,128)(2,1)S(1)}, f32[3,256,256]{2,1,0:T(8,128)S(1)}, f32[256,256]{1,0:T(8,128)S(1)}) custom-call(s32[2,4]{1,0:T(2,128)S(1)} %bitcast.21, s32[1,1]{1,0:T(1,128)S(6)} %copy.11.count_ref.refs_1_, s32[3,8,128]{2,1,0:T(8,128)S(1)} %get-tuple-element.22.refs_2_, ...), custom_call_target="tpu_custom_call" | custom-call | flops 8000000000 | bytes 24000000 | tf_op jit(solution)/shard_map/patches/pallas_call | solution.py:211
  29.7 0.0 copy-done.2
  29.7 0.0 copy-done.3
  29.7 25.2 %middle.1 = (f32[2,256,256]{2,1,0:T(8,128)S(1)}, f32[2,3,384,128]{3,2,1,0:T(8,128)S(1)}) custom-call(f32[2,256,256]{2,1,0:T(8,128)S(1)} %get-tuple-element.24.center_ref, bf16[2,384,128]{2,1,0:T(8,128)(2,1)S(1)} %get-tuple-element.25.rr, bf16[2,2,128,128]{3,2,1,0:T(8,128)(2,1)S(1)} %get-tuple-element.26.rb, f32[256,256]{1,0:T(8,128)S(1)} %get-tuple-element.27.inv_ref, ...), custom_call_target="tpu_custom_call" | custom-call | flops 15000000512 | bytes 45000000 | tf_op jit(solution)/shard_map/middle/pallas_call | solution.py:679
  54.9 2.5 %patches.3 = (f32[2,256,256]{2,1,0:T(8,128)S(1)}, bf16[2,384,128]{2,1,0:T(8,128)(2,1)S(1)}, bf16[2,2,128,128]{3,2,1,0:T(8,128)(2,1)S(1)}, bf16[2,4,3,32,256]{4,3,2,1,0:T(8,128)(2,1)S(1)}) custom-call(s32[2,4]{1,0:T(2,128)S(1)} %bitcast.22, s32[1,1]{1,0:T(1,128)S(6)} %copy.11.count_ref.refs_1_, f32[2,3,384,128]{3,2,1,0:T(8,128)S(1)} %get-tuple-element.28.refs_2_, ...), custom_call_target="tpu_custom_call" | custom-call | flops 8000000000 | bytes 24000000 | tf_op jit(solution)/shard_map/patches/pallas_call | solution.py:211
  57.5 34.5 %close.1 = (bf16[2,4,2,32,256]{4,3,2,1,0:T(8,128)(2,1)S(1)}, f32[2,256,256]{2,1,0:T(8,128)S(1)}, bf16[2,4,4,2,8,256]{5,4,3,2,1,0:T(8,128)(2,1)S(1)}) custom-call(f32[2,256,256]{2,1,0:T(8,128)S(1)} %get-tuple-element.30.center_ref, bf16[2,384,128]{2,1,0:T(8,128)(2,1)S(1)} %get-tuple-element.31.rr, bf16[2,2,128,128]{3,2,1,0:T(8,128)(2,1)S(1)} %get-tuple-element.32.rb, ...), custom_call_target="tpu_custom_call" | custom-call | flops 24999999488 | bytes 75000000 | tf_op jit(solution)/shard_map/close/pallas_call | solution.py:700
  92.0 1.3 %finish.1 = (f32[2,256,256]{2,1,0:T(8,128)}, f32[2,256,256]{2,1,0:T(8,128)}, f32[2,256,256]{2,1,0:T(8,128)}) custom-call(bf16[2,4,2,32,256]{4,3,2,1,0:T(8,128)(2,1)S(1)} %get-tuple-element.35.settled, f32[2,256,256]{2,1,0:T(8,128)S(1)} %get-tuple-element.36.kept, bf16[2,4,4,2,8,256]{5,4,3,2,1,0:T(8,128)(2,1)S(1)} %get-tuple-element.37.grown, ...), custom_call_target="tpu_custom_call" | custom-call | flops 1000000000 | bytes 3000000 | tf_op jit(solution)/shard_map/finish/pallas_call | solution.py:728
Async XLA Ops:
  1.3 1.0 %copy-start.1 = (f32[1,2,256,256]{3,2,1,0:T(8,128)S(1)}, f32[1,2,256,256]{3,2,1,0:T(8,128)}, u32[]{:S(2)}) copy-start(f32[1,2,256,256]{3,2,1,0:T(8,128)} %param.8) | copy-start | bytes 1572868
  2.3 0.7 copy-start.5
  3.0 23.4 %copy-start = (bf16[1,1,4,256,256]{4,3,2,1,0:T(8,128)(2,1)S(1)}, bf16[1,1,4,256,256]{4,3,2,1,0:T(8,128)(2,1)}, u32[]{:S(2)}) copy-start(bf16[1,1,4,256,256]{4,3,2,1,0:T(8,128)(2,1)} %param.11) | copy-start | bytes 1572868
  3.0 23.4 %copy-start.4 = (f32[1,2,256,256]{3,2,1,0:T(8,128)S(1)}, f32[1,2,256,256]{3,2,1,0:T(8,128)}, u32[]{:S(2)}) copy-start(f32[1,2,256,256]{3,2,1,0:T(8,128)} %param.10) | copy-start | bytes 1572868
  3.0 23.4 %copy-start.6 = (s32[1,1,4,2]{2,3,1,0:T(2,128)S(1)}, s32[1,1,4,2]{2,3,1,0:T(2,128)}, u32[]{:S(2)}) copy-start(s32[1,1,4,2]{2,3,1,0:T(2,128)} %param.12) | copy-start | bytes 100
  3.0 23.4 %copy-start.7 = (bf16[512,512]{1,0:T(8,128)(2,1)S(1)}, bf16[512,512]{1,0:T(8,128)(2,1)}, u32[]{:S(2)}) copy-start(bf16[512,512]{1,0:T(8,128)(2,1)} %constant.5.clone.refs_7_.refs_6_) | copy-start | bytes 1572868
  3.0 23.4 %copy-start.8 = (bf16[512,512]{1,0:T(8,128)(2,1)S(1)}, bf16[512,512]{1,0:T(8,128)(2,1)}, u32[]{:S(2)}) copy-start(bf16[512,512]{1,0:T(8,128)(2,1)} %constant.4.clone.refs_6_.refs_5_) | copy-start | bytes 1572868
  26.4 3.3 %copy-start.2 = (f32[1,2,256,256]{3,2,1,0:T(8,128)S(1)}, f32[1,2,256,256]{3,2,1,0:T(8,128)}, u32[]{:S(2)}) copy-start(f32[1,2,256,256]{3,2,1,0:T(8,128)} %param.8) | copy-start | bytes 1572868
  26.4 3.3 %copy-start.3 = (f32[1,1,2,256,256]{4,3,2,1,0:T(8,128)S(1)}, f32[1,1,2,256,256]{4,3,2,1,0:T(8,128)}, u32[]{:S(2)}) copy-start(f32[1,1,2,256,256]{4,3,2,1,0:T(8,128)} %param.9) | copy-start | bytes 1572868

commit v6 on v5

--- a/solution.py
+++ b/solution.py
@@ -317,11 +317,12 @@
             for b in range(2):
                 wide_ref[c, b, TS:, :] = below_in[b, c].astype(jnp.float32)
         for c in range(2):
+            sent_if(self.above, self.up[0][c], self.up[1][c])
+            sent_if(self.left, self.side[0][c], self.side[1][c])
+        for c in range(2):
             wait_if(self.right, self.relay[c])
             wide_ref[c, 2, TS:, :] = corner_in[c].astype(jnp.float32)
-        for c in range(2):
-            sent_if(self.above, self.up[0][c], self.up[1][c])
-            sent_if(self.left, self.side[0][c], self.side[1][c], self.relay[c])
+        sent_if(self.left, *self.relay)
 
 
 def open_kernel(cons_ref, corner_ref, count_ref, wide_ref, near_ref,
@@ -407,10 +408,10 @@
         update(c, 0, 1)
         wait_if(above, push_low[c])
         update(c, 0, 0)
-    pull.finish(wide_ref)
     for c in range(2):
         sent_if(right, push_on[c])
         sent_if(below, push_far[c], push_low[c])
+    pull.finish(wide_ref)
 
 
 def close_kernel(center_ref, rr, rb, cons_ref, dual_ref, est_ref, inv_ref, psum,
@@ -444,7 +445,7 @@
     push_low = remote(lowered, above_in.at[0], rim_s, rim_r, 2, 2, down)
     to_half = remote(psum.at[1 - core], half_in, half_s, half_r, 0, 0, sibling)
 
-    hailed = hail([{"tile": moved(t, by)} for by in (-1, -TGW)] + [sibling, twin]
+    hailed = hail([sibling] + [{"tile": moved(t, by)} for by in (-1, -TGW)] + [twin]
                   + [tile_at(k, z, core) for k in ys] + [scan_at(k, yh) for k in xs]
                   + [at_seat(k) for k in seats] + [at_lap(k) for k in laps])
     clear_if(jnp.logical_not(left), left_in)
@@ -615,30 +616,34 @@
     combine(0)
     settle(1)
     probe_grow()
+    for k in ys:
+        run_copy(k, y).wait_send()
+    to_half.wait_send()
+    sent_if(right, push_on)
+    sent_if(below, push_far, push_low)
+    pair(1).wait_send()
+    for k in xs:
+        cross(1, k, x, k).wait_send()
     probe_wide()
     settle(0)
-    give(1)
-    probe_back()
-    give(0)
-    probe_give()
-
-    sent_if(right, push_on)
-    sent_if(below, push_far, push_low)
-    to_half.wait_send()
-    back_copy(core).wait_send()
-    for k in ys:
-        run_copy(k, y).wait_send()
-        wide_copy(k, y).wait_send()
     for k in seats:
         ring_copy(k, seat).wait_send()
         grow_copy(k, seat).wait_send()
     for k in laps:
         tri_copy(k, lap).wait_send()
+    pair(0).wait_send()
+    for k in xs:
+        cross(0, k, x, k).wait_send()
+    give(1)
+    probe_back()
+    for k in ys:
+        wide_copy(k, y).wait_send()
+    give(0)
     for n in range(2):
-        pair(n).wait_send()
         for k in xs:
-            cross(n, k, x, k).wait_send()
             spread(n, k, x, k).wait_send()
+    probe_give()
+    back_copy(core).wait_send()
 
 
 def params(identity, grant):

time: 93.5 us -> 92.9 us (level)
  no operation moved by 1% of the time
where the time goes in v6:
time: 92.9 us; the launch traced here: 92.7 us
  Pallas kernels  89.5 us (96%)
  local copies, waits for them, and re-layouts  1.75 us (2%)
  between operations  1.41 us (2%)
    pallas_call x1, Pallas kernels, close(): pl.pallas_call(close_kernel, out_shape=(jax.ShapeDtypeStruct((2, COLS, 2,...  34.8 us
    pallas_call x1, Pallas kernels, middle(): pl.pallas_call(middle_kernel, out_shape=(FIELD, WIDE), in_specs=[VMEM] *...  24.3 us
    pallas_call x1, Pallas kernels, open_halo(): pl.pallas_call(open_kernel, out_shape=(WIDE, jax.ShapeDtypeStruct((3, 8,...  23.3 us
    pallas_call x2, Pallas kernels, patches(): pl.pallas_call(functools.partial(patches_kernel, first), out_shape=tuple(...  5.82 us

profile of v6, /device:TPU:1, one launch (start us, length us, event | category | flops | bytes accessed | tf_op | source)
XLA Modules:
  0.0 92.7 jit_solution(5007493287976988424)
XLA Ops:
  1.3 0.0 copy-start.1
  1.3 1.0 %copy-done.1 = f32[1,2,256,256]{3,2,1,0:T(8,128)S(1)} copy-done((f32[1,2,256,256]{3,2,1,0:T(8,128)S(1)}, f32[1,2,256,256]{3,2,1,0:T(8,128)}, u32[]{:S(2)}) %copy-start.1) | copy-done | bytes 524312
  2.3 0.0 copy-start.5
  2.3 0.7 copy-done.5
  3.0 0.0 copy-start
  3.0 0.0 copy-start.4
  3.0 0.0 copy-start.6
  3.0 0.0 copy-start.7
  3.0 0.0 copy-start.8
  3.0 23.3 %open_halo.1 = (f32[2,3,384,128]{3,2,1,0:T(8,128)S(1)}, s32[3,8,128]{2,1,0:T(8,128)S(1)}) custom-call(f32[2,256,256]{2,1,0:T(8,128)S(1)} %bitcast.12, s32[2,4]{1,0:T(2,128)S(1)} %bitcast.20, s32[1,1]{1,0:T(1,128)S(6)} %copy.11.count_ref.refs_1_), custom_call_target="tpu_custom_call" | custom-call | flops 10000000000 | bytes 30000000 | tf_op jit(solution)/shard_map/open_halo/pallas_call | solution.py:674
  26.3 0.0 copy-done
  26.4 0.0 copy-done.4
  26.4 0.0 copy-done.6
  26.4 0.0 copy-done.7
  26.4 0.0 copy-done.8
  26.4 0.0 copy-start.2
  26.4 0.0 copy-start.3
  26.4 3.3 %patches.2 = (f32[2,256,256]{2,1,0:T(8,128)S(1)}, bf16[2,384,128]{2,1,0:T(8,128)(2,1)S(1)}, bf16[2,2,128,128]{3,2,1,0:T(8,128)(2,1)S(1)}, f32[3,256,256]{2,1,0:T(8,128)S(1)}, f32[256,256]{1,0:T(8,128)S(1)}) custom-call(s32[2,4]{1,0:T(2,128)S(1)} %bitcast.21, s32[1,1]{1,0:T(1,128)S(6)} %copy.11.count_ref.refs_1_, s32[3,8,128]{2,1,0:T(8,128)S(1)} %get-tuple-element.22.refs_2_, ...), custom_call_target="tpu_custom_call" | custom-call | flops 8000000000 | bytes 24000000 | tf_op jit(solution)/shard_map/patches/pallas_call | solution.py:211
  29.7 0.0 copy-done.2
  29.7 0.0 copy-done.3
  29.7 24.3 %middle.1 = (f32[2,256,256]{2,1,0:T(8,128)S(1)}, f32[2,3,384,128]{3,2,1,0:T(8,128)S(1)}) custom-call(f32[2,256,256]{2,1,0:T(8,128)S(1)} %get-tuple-element.24.center_ref, bf16[2,384,128]{2,1,0:T(8,128)(2,1)S(1)} %get-tuple-element.25.rr, bf16[2,2,128,128]{3,2,1,0:T(8,128)(2,1)S(1)} %get-tuple-element.26.rb, f32[256,256]{1,0:T(8,128)S(1)} %get-tuple-element.27.inv_ref, ...), custom_call_target="tpu_custom_call" | custom-call | flops 15000000512 | bytes 45000000 | tf_op jit(solution)/shard_map/middle/pallas_call | solution.py:684
  54.0 2.5 %patches.3 = (f32[2,256,256]{2,1,0:T(8,128)S(1)}, bf16[2,384,128]{2,1,0:T(8,128)(2,1)S(1)}, bf16[2,2,128,128]{3,2,1,0:T(8,128)(2,1)S(1)}, bf16[2,4,3,32,256]{4,3,2,1,0:T(8,128)(2,1)S(1)}) custom-call(s32[2,4]{1,0:T(2,128)S(1)} %bitcast.22, s32[1,1]{1,0:T(1,128)S(6)} %copy.11.count_ref.refs_1_, f32[2,3,384,128]{3,2,1,0:T(8,128)S(1)} %get-tuple-element.28.refs_2_, ...), custom_call_target="tpu_custom_call" | custom-call | flops 8000000000 | bytes 24000000 | tf_op jit(solution)/shard_map/patches/pallas_call | solution.py:211
  56.6 34.8 %close.1 = (bf16[2,4,2,32,256]{4,3,2,1,0:T(8,128)(2,1)S(1)}, f32[2,256,256]{2,1,0:T(8,128)S(1)}, bf16[2,4,4,2,8,256]{5,4,3,2,1,0:T(8,128)(2,1)S(1)}) custom-call(f32[2,256,256]{2,1,0:T(8,128)S(1)} %get-tuple-element.30.center_ref, bf16[2,384,128]{2,1,0:T(8,128)(2,1)S(1)} %get-tuple-element.31.rr, bf16[2,2,128,128]{3,2,1,0:T(8,128)(2,1)S(1)} %get-tuple-element.32.rb, ...), custom_call_target="tpu_custom_call" | custom-call | flops 24999999488 | bytes 75000000 | tf_op jit(solution)/shard_map/close/pallas_call | solution.py:705
  91.4 1.3 %finish.1 = (f32[2,256,256]{2,1,0:T(8,128)}, f32[2,256,256]{2,1,0:T(8,128)}, f32[2,256,256]{2,1,0:T(8,128)}) custom-call(bf16[2,4,2,32,256]{4,3,2,1,0:T(8,128)(2,1)S(1)} %get-tuple-element.35.settled, f32[2,256,256]{2,1,0:T(8,128)S(1)} %get-tuple-element.36.kept, bf16[2,4,4,2,8,256]{5,4,3,2,1,0:T(8,128)(2,1)S(1)} %get-tuple-element.37.grown, ...), custom_call_target="tpu_custom_call" | custom-call | flops 1000000000 | bytes 3000000 | tf_op jit(solution)/shard_map/finish/pallas_call | solution.py:733
Async XLA Ops:
  1.3 1.0 %copy-start.1 = (f32[1,2,256,256]{3,2,1,0:T(8,128)S(1)}, f32[1,2,256,256]{3,2,1,0:T(8,128)}, u32[]{:S(2)}) copy-start(f32[1,2,256,256]{3,2,1,0:T(8,128)} %param.8) | copy-start | bytes 1572868
  2.3 0.7 copy-start.5
  3.0 23.3 %copy-start = (bf16[1,1,4,256,256]{4,3,2,1,0:T(8,128)(2,1)S(1)}, bf16[1,1,4,256,256]{4,3,2,1,0:T(8,128)(2,1)}, u32[]{:S(2)}) copy-start(bf16[1,1,4,256,256]{4,3,2,1,0:T(8,128)(2,1)} %param.11) | copy-start | bytes 1572868
  3.0 23.4 %copy-start.4 = (f32[1,2,256,256]{3,2,1,0:T(8,128)S(1)}, f32[1,2,256,256]{3,2,1,0:T(8,128)}, u32[]{:S(2)}) copy-start(f32[1,2,256,256]{3,2,1,0:T(8,128)} %param.10) | copy-start | bytes 1572868
  3.0 23.4 %copy-start.6 = (s32[1,1,4,2]{2,3,1,0:T(2,128)S(1)}, s32[1,1,4,2]{2,3,1,0:T(2,128)}, u32[]{:S(2)}) copy-start(s32[1,1,4,2]{2,3,1,0:T(2,128)} %param.12) | copy-start | bytes 100
  3.0 23.4 %copy-start.7 = (bf16[512,512]{1,0:T(8,128)(2,1)S(1)}, bf16[512,512]{1,0:T(8,128)(2,1)}, u32[]{:S(2)}) copy-start(bf16[512,512]{1,0:T(8,128)(2,1)} %constant.5.clone.refs_7_.refs_6_) | copy-start | bytes 1572868
  3.0 23.4 %copy-start.8 = (bf16[512,512]{1,0:T(8,128)(2,1)S(1)}, bf16[512,512]{1,0:T(8,128)(2,1)}, u32[]{:S(2)}) copy-start(bf16[512,512]{1,0:T(8,128)(2,1)} %constant.4.clone.refs_6_.refs_5_) | copy-start | bytes 1572868
  26.4 3.3 %copy-start.2 = (f32[1,2,256,256]{3,2,1,0:T(8,128)S(1)}, f32[1,2,256,256]{3,2,1,0:T(8,128)}, u32[]{:S(2)}) copy-start(f32[1,2,256,256]{3,2,1,0:T(8,128)} %param.8) | copy-start | bytes 1572868
  26.4 3.3 %copy-start.3 = (f32[1,1,2,256,256]{4,3,2,1,0:T(8,128)S(1)}, f32[1,1,2,256,256]{4,3,2,1,0:T(8,128)}, u32[]{:S(2)}) copy-start(f32[1,1,2,256,256]{4,3,2,1,0:T(8,128)} %param.9) | copy-start | bytes 1572868

commit v7 on v6

--- a/solution.py
+++ b/solution.py
@@ -373,10 +373,6 @@
     push_far = [make(rb.at[1, c], above_in.at[1, c], 2 + c, down) for c in range(2)]
     push_low = [make(lowered.at[c], above_in.at[0, c], 4 + c, down) for c in range(2)]
 
-    def push(c):
-        start_if(right, push_on[c])
-        start_if(below, push_far[c])
-
     def relay(c):
         wait_if(left, push_on[c])
         lowered[c] = (rb[0, c].astype(jnp.float32) + left_in[c, TS:, :].astype(jnp.float32)).astype(jnp.bfloat16)
@@ -397,15 +393,16 @@
     update(0, 1, 1)
     update(1, 1, 1)
     meet(hailed)
-    push(0)
+    start_if(right, *push_on)
+    start_if(below, *push_far)
     relay(0)
-    push(1)
+    relay(1)
     for c in range(2):
-        if c == 1:
-            relay(1)
         update(c, 1, 0)
+    for c in range(2):
         wait_if(above, push_far[c])
         update(c, 0, 1)
+    for c in range(2):
         wait_if(above, push_low[c])
         update(c, 0, 0)
     for c in range(2):

time: 92.9 us -> 91.7 us (0.987)
  Pallas kernels: 89.5 us -> 88.3 us
    pallas_call x1, Pallas kernels: 24.3 us -> 22.7 us  [middle(): pl.pallas_call(middle_kernel, out_shape=(FIELD, WIDE), in_specs=[VMEM] *...]
where the time goes in v7:
time: 91.7 us; the launch traced here: 91.4 us
  Pallas kernels  88.3 us (96%)
  local copies, waits for them, and re-layouts  1.75 us (2%)
  between operations  1.41 us (2%)
    pallas_call x1, Pallas kernels, close(): pl.pallas_call(close_kernel, out_shape=(jax.ShapeDtypeStruct((2, COLS, 2,...  35.1 us
    pallas_call x1, Pallas kernels, open_halo(): pl.pallas_call(open_kernel, out_shape=(WIDE, jax.ShapeDtypeStruct((3, 8,...  23.3 us
    pallas_call x1, Pallas kernels, middle(): pl.pallas_call(middle_kernel, out_shape=(FIELD, WIDE), in_specs=[VMEM] *...  22.7 us
    pallas_call x2, Pallas kernels, patches(): pl.pallas_call(functools.partial(patches_kernel, first), out_shape=tuple(...  5.82 us

profile of v7, /device:TPU:1, one launch (start us, length us, event | category | flops | bytes accessed | tf_op | source)
XLA Modules:
  0.0 91.4 jit_solution(16561344517857234237)
XLA Ops:
  1.3 0.0 copy-start.1
  1.3 1.0 %copy-done.1 = f32[1,2,256,256]{3,2,1,0:T(8,128)S(1)} copy-done((f32[1,2,256,256]{3,2,1,0:T(8,128)S(1)}, f32[1,2,256,256]{3,2,1,0:T(8,128)}, u32[]{:S(2)}) %copy-start.1) | copy-done | bytes 524312
  2.3 0.0 copy-start.5
  2.3 0.7 copy-done.5
  3.0 0.0 copy-start
  3.0 0.0 copy-start.4
  3.0 0.0 copy-start.6
  3.0 0.0 copy-start.7
  3.0 0.0 copy-start.8
  3.0 23.3 %open_halo.1 = (f32[2,3,384,128]{3,2,1,0:T(8,128)S(1)}, s32[3,8,128]{2,1,0:T(8,128)S(1)}) custom-call(f32[2,256,256]{2,1,0:T(8,128)S(1)} %bitcast.12, s32[2,4]{1,0:T(2,128)S(1)} %bitcast.20, s32[1,1]{1,0:T(1,128)S(6)} %copy.11.count_ref.refs_1_), custom_call_target="tpu_custom_call" | custom-call | flops 10000000000 | bytes 30000000 | tf_op jit(solution)/shard_map/open_halo/pallas_call | solution.py:671
  26.3 0.0 copy-done
  26.4 0.0 copy-done.4
  26.4 0.0 copy-done.6
  26.4 0.0 copy-done.7
  26.4 0.0 copy-done.8
  26.4 0.0 copy-start.2
  26.4 0.0 copy-start.3
  26.4 3.3 %patches.2 = (f32[2,256,256]{2,1,0:T(8,128)S(1)}, bf16[2,384,128]{2,1,0:T(8,128)(2,1)S(1)}, bf16[2,2,128,128]{3,2,1,0:T(8,128)(2,1)S(1)}, f32[3,256,256]{2,1,0:T(8,128)S(1)}, f32[256,256]{1,0:T(8,128)S(1)}) custom-call(s32[2,4]{1,0:T(2,128)S(1)} %bitcast.21, s32[1,1]{1,0:T(1,128)S(6)} %copy.11.count_ref.refs_1_, s32[3,8,128]{2,1,0:T(8,128)S(1)} %get-tuple-element.22.refs_2_, ...), custom_call_target="tpu_custom_call" | custom-call | flops 8000000000 | bytes 24000000 | tf_op jit(solution)/shard_map/patches/pallas_call | solution.py:211
  29.7 0.0 copy-done.2
  29.7 0.0 copy-done.3
  29.7 22.7 %middle.1 = (f32[2,256,256]{2,1,0:T(8,128)S(1)}, f32[2,3,384,128]{3,2,1,0:T(8,128)S(1)}) custom-call(f32[2,256,256]{2,1,0:T(8,128)S(1)} %get-tuple-element.24.center_ref, bf16[2,384,128]{2,1,0:T(8,128)(2,1)S(1)} %get-tuple-element.25.rr, bf16[2,2,128,128]{3,2,1,0:T(8,128)(2,1)S(1)} %get-tuple-element.26.rb, f32[256,256]{1,0:T(8,128)S(1)} %get-tuple-element.27.inv_ref, ...), custom_call_target="tpu_custom_call" | custom-call | flops 15000000512 | bytes 45000000 | tf_op jit(solution)/shard_map/middle/pallas_call | solution.py:681
  52.5 2.5 %patches.3 = (f32[2,256,256]{2,1,0:T(8,128)S(1)}, bf16[2,384,128]{2,1,0:T(8,128)(2,1)S(1)}, bf16[2,2,128,128]{3,2,1,0:T(8,128)(2,1)S(1)}, bf16[2,4,3,32,256]{4,3,2,1,0:T(8,128)(2,1)S(1)}) custom-call(s32[2,4]{1,0:T(2,128)S(1)} %bitcast.22, s32[1,1]{1,0:T(1,128)S(6)} %copy.11.count_ref.refs_1_, f32[2,3,384,128]{3,2,1,0:T(8,128)S(1)} %get-tuple-element.28.refs_2_, ...), custom_call_target="tpu_custom_call" | custom-call | flops 8000000000 | bytes 24000000 | tf_op jit(solution)/shard_map/patches/pallas_call | solution.py:211
  55.0 35.1 %close.1 = (bf16[2,4,2,32,256]{4,3,2,1,0:T(8,128)(2,1)S(1)}, f32[2,256,256]{2,1,0:T(8,128)S(1)}, bf16[2,4,4,2,8,256]{5,4,3,2,1,0:T(8,128)(2,1)S(1)}) custom-call(f32[2,256,256]{2,1,0:T(8,128)S(1)} %get-tuple-element.30.center_ref, bf16[2,384,128]{2,1,0:T(8,128)(2,1)S(1)} %get-tuple-element.31.rr, bf16[2,2,128,128]{3,2,1,0:T(8,128)(2,1)S(1)} %get-tuple-element.32.rb, ...), custom_call_target="tpu_custom_call" | custom-call | flops 24999999488 | bytes 75000000 | tf_op jit(solution)/shard_map/close/pallas_call | solution.py:702
  90.1 1.3 %finish.1 = (f32[2,256,256]{2,1,0:T(8,128)}, f32[2,256,256]{2,1,0:T(8,128)}, f32[2,256,256]{2,1,0:T(8,128)}) custom-call(bf16[2,4,2,32,256]{4,3,2,1,0:T(8,128)(2,1)S(1)} %get-tuple-element.35.settled, f32[2,256,256]{2,1,0:T(8,128)S(1)} %get-tuple-element.36.kept, bf16[2,4,4,2,8,256]{5,4,3,2,1,0:T(8,128)(2,1)S(1)} %get-tuple-element.37.grown, ...), custom_call_target="tpu_custom_call" | custom-call | flops 1000000000 | bytes 3000000 | tf_op jit(solution)/shard_map/finish/pallas_call | solution.py:730
Async XLA Ops:
  1.3 1.0 %copy-start.1 = (f32[1,2,256,256]{3,2,1,0:T(8,128)S(1)}, f32[1,2,256,256]{3,2,1,0:T(8,128)}, u32[]{:S(2)}) copy-start(f32[1,2,256,256]{3,2,1,0:T(8,128)} %param.8) | copy-start | bytes 1572868
  2.3 0.7 copy-start.5
  3.0 23.3 %copy-start = (bf16[1,1,4,256,256]{4,3,2,1,0:T(8,128)(2,1)S(1)}, bf16[1,1,4,256,256]{4,3,2,1,0:T(8,128)(2,1)}, u32[]{:S(2)}) copy-start(bf16[1,1,4,256,256]{4,3,2,1,0:T(8,128)(2,1)} %param.11) | copy-start | bytes 1572868
  3.0 23.4 %copy-start.4 = (f32[1,2,256,256]{3,2,1,0:T(8,128)S(1)}, f32[1,2,256,256]{3,2,1,0:T(8,128)}, u32[]{:S(2)}) copy-start(f32[1,2,256,256]{3,2,1,0:T(8,128)} %param.10) | copy-start | bytes 1572868
  3.0 23.4 %copy-start.6 = (s32[1,1,4,2]{2,3,1,0:T(2,128)S(1)}, s32[1,1,4,2]{2,3,1,0:T(2,128)}, u32[]{:S(2)}) copy-start(s32[1,1,4,2]{2,3,1,0:T(2,128)} %param.12) | copy-start | bytes 100
  3.0 23.4 %copy-start.7 = (bf16[512,512]{1,0:T(8,128)(2,1)S(1)}, bf16[512,512]{1,0:T(8,128)(2,1)}, u32[]{:S(2)}) copy-start(bf16[512,512]{1,0:T(8,128)(2,1)} %constant.5.clone.refs_7_.refs_6_) | copy-start | bytes 1572868
  3.0 23.4 %copy-start.8 = (bf16[512,512]{1,0:T(8,128)(2,1)S(1)}, bf16[512,512]{1,0:T(8,128)(2,1)}, u32[]{:S(2)}) copy-start(bf16[512,512]{1,0:T(8,128)(2,1)} %constant.4.clone.refs_6_.refs_5_) | copy-start | bytes 1572868
  26.4 3.3 %copy-start.2 = (f32[1,2,256,256]{3,2,1,0:T(8,128)S(1)}, f32[1,2,256,256]{3,2,1,0:T(8,128)}, u32[]{:S(2)}) copy-start(f32[1,2,256,256]{3,2,1,0:T(8,128)} %param.8) | copy-start | bytes 1572868
  26.4 3.3 %copy-start.3 = (f32[1,1,2,256,256]{4,3,2,1,0:T(8,128)S(1)}, f32[1,1,2,256,256]{4,3,2,1,0:T(8,128)}, u32[]{:S(2)}) copy-start(f32[1,1,2,256,256]{4,3,2,1,0:T(8,128)} %param.9) | copy-start | bytes 1572868

commit v8 on v7

--- a/solution.py
+++ b/solution.py
@@ -611,8 +611,8 @@
     share(0)
     probe_tri()
     combine(0)
+    probe_grow()
     settle(1)
-    probe_grow()
     for k in ys:
         run_copy(k, y).wait_send()
     to_half.wait_send()

time: 91.7 us -> 90.3 us (0.985)
  Pallas kernels: 88.3 us -> 86.8 us
    pallas_call x1, Pallas kernels: 22.7 us -> 21.2 us  [middle(): pl.pallas_call(middle_kernel, out_shape=(FIELD, WIDE), in_specs=[VMEM] *...]
where the time goes in v8:
time: 90.3 us; the launch traced here: 90 us
  Pallas kernels  86.8 us (96%)
  local copies, waits for them, and re-layouts  1.75 us (2%)
  between operations  1.41 us (2%)
    pallas_call x1, Pallas kernels, close(): pl.pallas_call(close_kernel, out_shape=(jax.ShapeDtypeStruct((2, COLS, 2,...  35.2 us
    pallas_call x1, Pallas kernels, open_halo(): pl.pallas_call(open_kernel, out_shape=(WIDE, jax.ShapeDtypeStruct((3, 8,...  23.3 us
    pallas_call x1, Pallas kernels, middle(): pl.pallas_call(middle_kernel, out_shape=(FIELD, WIDE), in_specs=[VMEM] *...  21.2 us
    pallas_call x2, Pallas kernels, patches(): pl.pallas_call(functools.partial(patches_kernel, first), out_shape=tuple(...  5.82 us

profile of v8, /device:TPU:1, one launch (start us, length us, event | category | flops | bytes accessed | tf_op | source)
XLA Modules:
  0.0 90.0 jit_solution(9943486154095605814)
XLA Ops:
  1.3 0.0 copy-start.1
  1.3 1.0 %copy-done.1 = f32[1,2,256,256]{3,2,1,0:T(8,128)S(1)} copy-done((f32[1,2,256,256]{3,2,1,0:T(8,128)S(1)}, f32[1,2,256,256]{3,2,1,0:T(8,128)}, u32[]{:S(2)}) %copy-start.1) | copy-done | bytes 524312
  2.3 0.0 copy-start.5
  2.3 0.7 copy-done.5
  3.0 0.0 copy-start
  3.0 0.0 copy-start.4
  3.0 0.0 copy-start.6
  3.0 0.0 copy-start.7
  3.0 0.0 copy-start.8
  3.0 23.3 %open_halo.1 = (f32[2,3,384,128]{3,2,1,0:T(8,128)S(1)}, s32[3,8,128]{2,1,0:T(8,128)S(1)}) custom-call(f32[2,256,256]{2,1,0:T(8,128)S(1)} %bitcast.12, s32[2,4]{1,0:T(2,128)S(1)} %bitcast.20, s32[1,1]{1,0:T(1,128)S(6)} %copy.11.count_ref.refs_1_), custom_call_target="tpu_custom_call" | custom-call | flops 10000000000 | bytes 30000000 | tf_op jit(solution)/shard_map/open_halo/pallas_call | solution.py:671
  26.3 0.0 copy-done
  26.4 0.0 copy-done.4
  26.4 0.0 copy-done.6
  26.4 0.0 copy-done.7
  26.4 0.0 copy-done.8
  26.4 0.0 copy-start.2
  26.4 0.0 copy-start.3
  26.4 3.3 %patches.2 = (f32[2,256,256]{2,1,0:T(8,128)S(1)}, bf16[2,384,128]{2,1,0:T(8,128)(2,1)S(1)}, bf16[2,2,128,128]{3,2,1,0:T(8,128)(2,1)S(1)}, f32[3,256,256]{2,1,0:T(8,128)S(1)}, f32[256,256]{1,0:T(8,128)S(1)}) custom-call(s32[2,4]{1,0:T(2,128)S(1)} %bitcast.21, s32[1,1]{1,0:T(1,128)S(6)} %copy.11.count_ref.refs_1_, s32[3,8,128]{2,1,0:T(8,128)S(1)} %get-tuple-element.22.refs_2_, ...), custom_call_target="tpu_custom_call" | custom-call | flops 8000000000 | bytes 24000000 | tf_op jit(solution)/shard_map/patches/pallas_call | solution.py:211
  29.7 0.0 copy-done.2
  29.7 0.0 copy-done.3
  29.7 21.2 %middle.1 = (f32[2,256,256]{2,1,0:T(8,128)S(1)}, f32[2,3,384,128]{3,2,1,0:T(8,128)S(1)}) custom-call(f32[2,256,256]{2,1,0:T(8,128)S(1)} %get-tuple-element.24.center_ref, bf16[2,384,128]{2,1,0:T(8,128)(2,1)S(1)} %get-tuple-element.25.rr, bf16[2,2,128,128]{3,2,1,0:T(8,128)(2,1)S(1)} %get-tuple-element.26.rb, f32[256,256]{1,0:T(8,128)S(1)} %get-tuple-element.27.inv_ref, ...), custom_call_target="tpu_custom_call" | custom-call | flops 15000000512 | bytes 45000000 | tf_op jit(solution)/shard_map/middle/pallas_call | solution.py:681
  51.0 2.5 %patches.3 = (f32[2,256,256]{2,1,0:T(8,128)S(1)}, bf16[2,384,128]{2,1,0:T(8,128)(2,1)S(1)}, bf16[2,2,128,128]{3,2,1,0:T(8,128)(2,1)S(1)}, bf16[2,4,3,32,256]{4,3,2,1,0:T(8,128)(2,1)S(1)}) custom-call(s32[2,4]{1,0:T(2,128)S(1)} %bitcast.22, s32[1,1]{1,0:T(1,128)S(6)} %copy.11.count_ref.refs_1_, f32[2,3,384,128]{3,2,1,0:T(8,128)S(1)} %get-tuple-element.28.refs_2_, ...), custom_call_target="tpu_custom_call" | custom-call | flops 8000000000 | bytes 24000000 | tf_op jit(solution)/shard_map/patches/pallas_call | solution.py:211
  53.5 35.2 %close.1 = (bf16[2,4,2,32,256]{4,3,2,1,0:T(8,128)(2,1)S(1)}, f32[2,256,256]{2,1,0:T(8,128)S(1)}, bf16[2,4,4,2,8,256]{5,4,3,2,1,0:T(8,128)(2,1)S(1)}) custom-call(f32[2,256,256]{2,1,0:T(8,128)S(1)} %get-tuple-element.30.center_ref, bf16[2,384,128]{2,1,0:T(8,128)(2,1)S(1)} %get-tuple-element.31.rr, bf16[2,2,128,128]{3,2,1,0:T(8,128)(2,1)S(1)} %get-tuple-element.32.rb, ...), custom_call_target="tpu_custom_call" | custom-call | flops 24999999488 | bytes 75000000 | tf_op jit(solution)/shard_map/close/pallas_call | solution.py:702
  88.7 1.3 %finish.1 = (f32[2,256,256]{2,1,0:T(8,128)}, f32[2,256,256]{2,1,0:T(8,128)}, f32[2,256,256]{2,1,0:T(8,128)}) custom-call(bf16[2,4,2,32,256]{4,3,2,1,0:T(8,128)(2,1)S(1)} %get-tuple-element.35.settled, f32[2,256,256]{2,1,0:T(8,128)S(1)} %get-tuple-element.36.kept, bf16[2,4,4,2,8,256]{5,4,3,2,1,0:T(8,128)(2,1)S(1)} %get-tuple-element.37.grown, ...), custom_call_target="tpu_custom_call" | custom-call | flops 1000000000 | bytes 3000000 | tf_op jit(solution)/shard_map/finish/pallas_call | solution.py:730
Async XLA Ops:
  1.3 1.0 %copy-start.1 = (f32[1,2,256,256]{3,2,1,0:T(8,128)S(1)}, f32[1,2,256,256]{3,2,1,0:T(8,128)}, u32[]{:S(2)}) copy-start(f32[1,2,256,256]{3,2,1,0:T(8,128)} %param.8) | copy-start | bytes 1572868
  2.3 0.7 copy-start.5
  3.0 23.3 %copy-start = (bf16[1,1,4,256,256]{4,3,2,1,0:T(8,128)(2,1)S(1)}, bf16[1,1,4,256,256]{4,3,2,1,0:T(8,128)(2,1)}, u32[]{:S(2)}) copy-start(bf16[1,1,4,256,256]{4,3,2,1,0:T(8,128)(2,1)} %param.11) | copy-start | bytes 1572868
  3.0 23.4 %copy-start.4 = (f32[1,2,256,256]{3,2,1,0:T(8,128)S(1)}, f32[1,2,256,256]{3,2,1,0:T(8,128)}, u32[]{:S(2)}) copy-start(f32[1,2,256,256]{3,2,1,0:T(8,128)} %param.10) | copy-start | bytes 1572868
  3.0 23.4 %copy-start.6 = (s32[1,1,4,2]{2,3,1,0:T(2,128)S(1)}, s32[1,1,4,2]{2,3,1,0:T(2,128)}, u32[]{:S(2)}) copy-start(s32[1,1,4,2]{2,3,1,0:T(2,128)} %param.12) | copy-start | bytes 100
  3.0 23.4 %copy-start.7 = (bf16[512,512]{1,0:T(8,128)(2,1)S(1)}, bf16[512,512]{1,0:T(8,128)(2,1)}, u32[]{:S(2)}) copy-start(bf16[512,512]{1,0:T(8,128)(2,1)} %constant.5.clone.refs_7_.refs_6_) | copy-start | bytes 1572868
  3.0 23.4 %copy-start.8 = (bf16[512,512]{1,0:T(8,128)(2,1)S(1)}, bf16[512,512]{1,0:T(8,128)(2,1)}, u32[]{:S(2)}) copy-start(bf16[512,512]{1,0:T(8,128)(2,1)} %constant.4.clone.refs_6_.refs_5_) | copy-start | bytes 1572868
  26.4 3.3 %copy-start.2 = (f32[1,2,256,256]{3,2,1,0:T(8,128)S(1)}, f32[1,2,256,256]{3,2,1,0:T(8,128)}, u32[]{:S(2)}) copy-start(f32[1,2,256,256]{3,2,1,0:T(8,128)} %param.8) | copy-start | bytes 1572868
  26.4 3.3 %copy-start.3 = (f32[1,1,2,256,256]{4,3,2,1,0:T(8,128)S(1)}, f32[1,1,2,256,256]{4,3,2,1,0:T(8,128)}, u32[]{:S(2)}) copy-start(f32[1,1,2,256,256]{4,3,2,1,0:T(8,128)} %param.9) | copy-start | bytes 1572868
